TPU v7x, 256 devices: a whole 4x4x8 slice. The times are simulated.
256 devices in a mesh: row: 16 (over z_lo, x), col: 16 (over y, z_hi, core).
Axes of the slice: x: 4, y: 4, z: 8 (z_hi: 2, z_lo: 4; z = z_hi * 4 + z_lo), core: 2. Of those that a mesh axis runs over, the one named last changes fastest.
Arguments:
- offsets: int32 [16, 16, 2], P('row', 'col'), may hold values from 1 to 3
- targets: float32 [3, 3, 512, 2048], P(None, None, 'row', 'col'), may hold values from -60 to 60
- grid_fine: float32 [32, 512, 2048], P(None, 'row', 'col'), may hold values from -6 to 6
- grid_coarse: float32 [32, 128, 512], P(None, 'row', 'col'), may hold values from -6 to 6
- weight_in: float32 [512, 64], replicated, may hold values from -0.75 to 0.75
- weight_mid: float32 [1, 512, 512], replicated, may hold values from -0.25 to 0.25
- weight_out: float32 [3, 512], replicated, may hold values from -0.397747564 to 0.397747564
- fine_first: float32 [32, 512, 2048], P(None, 'row', 'col'), may hold values from -0.012 to 0.012
- fine_second: float32 [32, 512, 2048], P(None, 'row', 'col'), may hold values from 1e-06 to 0.0001
- coarse_first: float32 [32, 128, 512], P(None, 'row', 'col'), may hold values from -0.012 to 0.012
- coarse_second: float32 [32, 128, 512], P(None, 'row', 'col'), may hold values from 1e-06 to 0.0001
- in_first: float32 [512, 64], replicated, may hold values from -0.012 to 0.012
- in_second: float32 [512, 64], replicated, may hold values from 1e-06 to 0.0001
- mid_first: float32 [1, 512, 512], replicated, may hold values from -0.012 to 0.012
- mid_second: float32 [1, 512, 512], replicated, may hold values from 1e-06 to 0.0001
- out_first: float32 [3, 512], replicated, may hold values from -0.012 to 0.012
- out_second: float32 [3, 512], replicated, may hold values from 1e-06 to 0.0001
Outputs:
- fine_step: float32 [32, 512, 2048], P(None, 'row', 'col')
- coarse_step: float32 [32, 128, 512], P(None, 'row', 'col')
- input_step: float32 [512, 64], replicated
- middle_step: float32 [1, 512, 512], replicated
- output_step: float32 [3, 512], replicated
All inputs are finite; a program needn't handle non-finite values.
Results may differ from a plain program's by a relative error of at most 0.0014.
The roundings to bfloat16 on the way count: a program that leaves them out, or rounds other values in their place, can miss the bound.
Values sent between devices are 32-bit elements; how exact they have to be, the bound alone decides.
No kernel may reach another device: no remote copies, remote signals or barrier semaphores. Data moves between devices by JAX's collectives and lax.ppermute only.
A program may use at most 64 MiB of HBM per device.

v0:
```python
import jax
import jax.numpy as jnp
from jax import lax
from jax.sharding import PartitionSpec as P

SUB = 4
RATIO = 4
ADAM_STEP = 10


BETA_ONE = 0.9
BETA_TWO = 0.99
ADAM_EPSILON = 1e-08
CLIP_RMS = 0.01
LOSS_VALUE = 0.25
MEAN_EPSILON = 1e-06


def shifted(block, axis, distance):
    devices = range(lax.axis_size(axis))
    route = [(i - distance, i) for i in devices if i - distance in devices]
    return lax.ppermute(block, axis, route)


def interp_table(samples, level_ratio, offset):
    positions = jnp.arange(samples, dtype=jnp.int32)
    base_index = positions // level_ratio
    fraction = (
        (positions % level_ratio).astype(jnp.float32) + offset.astype(jnp.float32) / SUB
    ) / level_ratio
    column = jnp.arange(samples // level_ratio + 1, dtype=jnp.int32)
    lower_hit = (column[None, :] == base_index[:, None]).astype(jnp.float32)
    upper_hit = (column[None, :] == base_index[:, None] + 1).astype(jnp.float32)
    return lower_hit * (1.0 - fraction)[:, None] + upper_hit * fraction[:, None]


def level_tables(row_count, col_count, shift_y, shift_x):
    return (
        interp_table(row_count, 1, shift_y),
        interp_table(col_count, 1, shift_x),
        interp_table(row_count, RATIO, shift_y),
        interp_table(col_count, RATIO, shift_x),
    )


def sample_level(extended, row_table, col_table):
    across = jnp.einsum("kjl,ml->kjm", extended, col_table, precision=lax.Precision.HIGHEST)
    return jnp.einsum("ij,kjm->kim", row_table, across, precision=lax.Precision.HIGHEST)


def spread_level(cotangent, row_table, col_table):
    backward = jnp.einsum("ij,kim->kjm", row_table, cotangent, precision=lax.Precision.HIGHEST)
    return jnp.einsum("kjm,ml->kjl", backward, col_table, precision=lax.Precision.HIGHEST)


def sample_features(fine_ext, coarse_ext, tables):
    fine_feat = sample_level(fine_ext, tables[0], tables[1])
    coarse_feat = sample_level(coarse_ext, tables[2], tables[3])
    channels, row_count, col_count = fine_feat.shape
    return jnp.concatenate(
        [
            fine_feat.reshape(channels, row_count * col_count),
            coarse_feat.reshape(channels, row_count * col_count),
        ],
        axis=0,
    ).astype(jnp.bfloat16)


def spread_features(feature_grad, tables):
    channels = feature_grad.shape[0] // 2
    row_count = tables[0].shape[0]
    col_count = tables[1].shape[0]
    fine_cot = feature_grad[:channels].reshape(channels, row_count, col_count)
    coarse_cot = feature_grad[channels:].reshape(channels, row_count, col_count)
    return (
        spread_level(fine_cot, tables[0], tables[1]),
        spread_level(coarse_cot, tables[2], tables[3]),
    )


def matmul(former, latter):
    return jnp.dot(former, latter, preferred_element_type=jnp.float32)


def contract_rows(former, latter):
    return lax.dot_general(
        former, latter, (((0,), (0,)), ((), ())), preferred_element_type=jnp.float32
    )


def contract_cols(former, latter):
    return lax.dot_general(
        former, latter, (((1,), (1,)), ((), ())), preferred_element_type=jnp.float32
    )


def silu_slope(pre_act):
    sigmoid = jax.nn.sigmoid(pre_act)
    return sigmoid * (1.0 + pre_act * (1.0 - sigmoid))


def decoder_forward(features, low_in, low_mid, low_out):
    pre_acts = [matmul(low_in, features)]
    activations = [jax.nn.silu(pre_acts[0]).astype(jnp.bfloat16)]
    pre_acts.append(matmul(low_mid[0], activations[-1]))
    activations.append(jax.nn.silu(pre_acts[-1]).astype(jnp.bfloat16))
    return (matmul(low_out, activations[-1]), pre_acts, activations)


def decoder_backward(features, pre_acts, activations, cotangent, low_in, low_mid, low_out):
    out_cotangent = cotangent.astype(jnp.bfloat16)
    grad_out = contract_cols(out_cotangent, activations[-1])
    upward = contract_rows(low_out, out_cotangent)
    grads_mid = []
    delta_low = (upward * silu_slope(pre_acts[1])).astype(jnp.bfloat16)
    grads_mid.insert(0, contract_cols(delta_low, activations[0]))
    upward = contract_rows(low_mid[0], delta_low)
    delta_low = (upward * silu_slope(pre_acts[0])).astype(jnp.bfloat16)
    grad_in = contract_cols(delta_low, features)
    feature_grad = contract_rows(low_in, delta_low)
    return (grad_in, jnp.stack(grads_mid), grad_out, feature_grad)


def pixel_cotangent(value_error, row_error, row_prior, col_error, col_prior):
    return (
        2.0 * LOSS_VALUE * value_error
        + 2.0 * (row_prior - row_error)
        + 2.0 * (col_prior - col_error)
    )


def clip_factor(total, entries):
    return jnp.minimum(1.0, CLIP_RMS / jnp.sqrt(total / entries + MEAN_EPSILON))


def adam_step(gradient, moment_one, moment_two, clip_scale):
    clipped = gradient * clip_scale
    new_one = BETA_ONE * moment_one + (1.0 - BETA_ONE) * clipped
    new_two = BETA_TWO * moment_two + (1.0 - BETA_TWO) * clipped * clipped
    return (
        new_one
        / (1.0 - BETA_ONE**ADAM_STEP)
        / (jnp.sqrt(new_two / (1.0 - BETA_TWO**ADAM_STEP)) + ADAM_EPSILON)
    )


def grid_total_sum(grid_local):
    return lax.psum(grid_local, ("row", "col"))


def shards(
    offsets,
    targets,
    grid_fine,
    grid_coarse,
    weight_in,
    weight_mid,
    weight_out,
    fine_first,
    fine_second,
    coarse_first,
    coarse_second,
    in_first,
    in_second,
    mid_first,
    mid_second,
    out_first,
    out_second,
):
    channels, sample_rows, sample_cols = grid_fine.shape
    coarse_rows = grid_coarse.shape[1]
    coarse_cols = grid_coarse.shape[2]
    low_in = weight_in.astype(jnp.bfloat16)
    low_mid = weight_mid.astype(jnp.bfloat16)
    low_out = weight_out.astype(jnp.bfloat16)
    top_rows = jnp.concatenate([grid_fine[:, :1, :], grid_coarse[:, :1, :]], axis=2)
    top_rows = shifted(top_rows, "row", -1)
    fine_tall = jnp.concatenate([grid_fine, top_rows[:, :, :sample_cols]], axis=1)
    coarse_tall = jnp.concatenate([grid_coarse, top_rows[:, :, sample_cols:]], axis=1)
    edge_cols = jnp.concatenate([fine_tall[:, :, :1], coarse_tall[:, :, :1]], axis=1)
    edge_cols = shifted(edge_cols, "col", -1)
    fine_ext = jnp.concatenate([fine_tall, edge_cols[:, : sample_rows + 1, :]], axis=2)
    coarse_ext = jnp.concatenate([coarse_tall, edge_cols[:, sample_rows + 1 :, :]], axis=2)
    tables = level_tables(sample_rows, sample_cols, offsets[0, 0, 0], offsets[0, 0, 1])
    features = sample_features(fine_ext, coarse_ext, tables)
    predicted, pre_acts, activations = decoder_forward(features, low_in, low_mid, low_out)
    outputs = predicted.shape[0]
    predicted = predicted.reshape(outputs, sample_rows, sample_cols)
    below = shifted(predicted[:, :1, :], "row", -1)
    beside = shifted(predicted[:, :, :1], "col", -1)
    row_global = lax.axis_index("row") * sample_rows + jnp.arange(sample_rows, dtype=jnp.int32)
    col_global = lax.axis_index("col") * sample_cols + jnp.arange(sample_cols, dtype=jnp.int32)
    row_valid = (row_global < lax.axis_size("row") * sample_rows - 1)[None, :, None]
    col_valid = (col_global < lax.axis_size("col") * sample_cols - 1)[None, None, :]
    row_next = jnp.concatenate([predicted[:, 1:, :], below], axis=1)
    col_next = jnp.concatenate([predicted[:, :, 1:], beside], axis=2)
    value_error = predicted - targets[0]
    row_error = jnp.where(row_valid, row_next - predicted - targets[1], 0.0)
    col_error = jnp.where(col_valid, col_next - predicted - targets[2], 0.0)
    above = shifted(row_error[:, -1:, :], "row", 1)
    before = shifted(col_error[:, :, -1:], "col", 1)
    row_prior = jnp.concatenate([above, row_error[:, :-1, :]], axis=1)
    col_prior = jnp.concatenate([before, col_error[:, :, :-1]], axis=2)
    cotangent = pixel_cotangent(value_error, row_error, row_prior, col_error, col_prior)
    grad_in, grad_mid, grad_out, feature_grad = decoder_backward(
        features,
        pre_acts,
        activations,
        cotangent.reshape(outputs, sample_rows * sample_cols),
        low_in,
        low_mid,
        low_out,
    )
    fine_back, coarse_back = spread_features(feature_grad, tables)
    side_cols = jnp.concatenate(
        [fine_back[:, :, sample_cols:], coarse_back[:, :, coarse_cols:]], axis=1
    )
    side_cols = shifted(side_cols, "col", 1)
    fine_tall_grad = jnp.concatenate(
        [fine_back[:, :, :1] + side_cols[:, : sample_rows + 1, :], fine_back[:, :, 1:sample_cols]],
        axis=2,
    )
    coarse_tall_grad = jnp.concatenate(
        [
            coarse_back[:, :, :1] + side_cols[:, sample_rows + 1 :, :],
            coarse_back[:, :, 1:coarse_cols],
        ],
        axis=2,
    )
    bottom_rows = jnp.concatenate(
        [fine_tall_grad[:, sample_rows:, :], coarse_tall_grad[:, coarse_rows:, :]], axis=2
    )
    bottom_rows = shifted(bottom_rows, "row", 1)
    fine_grad = jnp.concatenate(
        [
            fine_tall_grad[:, :1, :] + bottom_rows[:, :, :sample_cols],
            fine_tall_grad[:, 1:sample_rows, :],
        ],
        axis=1,
    )
    coarse_grad = jnp.concatenate(
        [
            coarse_tall_grad[:, :1, :] + bottom_rows[:, :, sample_cols:],
            coarse_tall_grad[:, 1:coarse_rows, :],
        ],
        axis=1,
    )
    grid_local = jnp.sum(fine_grad * fine_grad) + jnp.sum(coarse_grad * coarse_grad)
    devices = lax.axis_size("row") * lax.axis_size("col")
    grid_entries = (fine_grad.size + coarse_grad.size) * devices
    decoder_entries = weight_in.size + weight_mid.size + weight_out.size
    grad_in, grad_mid, grad_out = lax.psum((grad_in, grad_mid, grad_out), ("row", "col"))
    grid_total = grid_total_sum(grid_local)
    decoder_total = (
        jnp.sum(grad_in * grad_in) + jnp.sum(grad_mid * grad_mid) + jnp.sum(grad_out * grad_out)
    )
    decoder_scale = clip_factor(decoder_total, decoder_entries)
    middle_step = adam_step(grad_mid, mid_first, mid_second, decoder_scale)
    grid_scale = clip_factor(grid_total, grid_entries)
    fine_step = adam_step(fine_grad, fine_first, fine_second, grid_scale)
    coarse_step = adam_step(coarse_grad, coarse_first, coarse_second, grid_scale)
    input_step = adam_step(grad_in, in_first, in_second, decoder_scale)
    output_step = adam_step(grad_out, out_first, out_second, decoder_scale)
    return (fine_step, coarse_step, input_step, middle_step, output_step)


def solution(mesh):
    placed = (
        P("row", "col", None),
        P(None, None, "row", "col"),
        P(None, "row", "col"),
        P(None, "row", "col"),
        P(),
        P(),
        P(),
        P(None, "row", "col"),
        P(None, "row", "col"),
        P(None, "row", "col"),
        P(None, "row", "col"),
        P(),
        P(),
        P(),
        P(),
        P(),
        P(),
    )
    return jax.shard_map(
        shards,
        mesh=mesh,
        in_specs=placed,
        out_specs=(P(None, "row", "col"), P(None, "row", "col"), P(), P(), P()),
        check_vma=False,
    )
```

profile of v0, /device:TPU:1, one launch (start us, length us, event | category | flops | bytes accessed | tf_op | source)
XLA Modules:
  0.0 379.6 jit_solution(6666377769657797324)
XLA Ops:
  9.2 1.3 collective-permute-start
  10.5 1.3 fusion.148
  16.3 5.7 %collective-permute-start.1 = (f32[32,42,1]{1,0,2:T(8,128)S(1)}, f32[32,42,1]{1,0,2:T(8,128)S(1)}, u32[]{:S(2)}, u32[]{:S(2)}) collective-permute-start(f32[32,42,1]{1,0,2:T(8,128)S(1)} %pad_maximum_fusion.7), channel_id=1, source_target_pairs={{1,0},{2,1},{3,2},{4,3},{5,4},{6,5},{7,6},{8,7},{9,8},{10,9},{11,1... | collective-permute-start | bytes 16136 | tf_op jit(solution)/shard_map/ppermute | solution.py:22
  22.0 6.4 %collective-permute-done.1 = f32[32,42,1]{1,0,2:T(8,128)S(1)} collective-permute-done((f32[32,42,1]{1,0,2:T(8,128)S(1)}, f32[32,42,1]{1,0,2:T(8,128)S(1)}, u32[]{:S(2)}, u32[]{:S(2)}) %collective-permute-start.1) | collective-permute-done | bytes 5408 | tf_op jit(solution)/shard_map/ppermute | solution.py:22
  29.2 2.2 fusion.14
  33.2 1.3 fusion.82
  34.5 4.4 %fusion.5 = (bf16[512,4096]{0,1:T(8,128)(2,1)S(1)}, f32[4096,512]{1,0:T(8,128)S(1)}) fusion(f32[1,512,512]{2,1,0:T(8,128)S(1)} %copy-done.11, f32[4096,512]{1,0:T(8,128)S(1)} %fusion.82), kind=kOutput, calls=%fused_computation.10 | convolution fusion | flops 2168717312 | bytes 22020096 | tf_op jit(solution)/shard_map/dot_general | solution.py:82
  39.0 1.2 fusion.125
  40.2 1.3 collective-permute-start.2
  41.5 1.9 collective-permute-start.4
  43.5 7.3 %collective-permute-done.4 = f32[3,32,1]{2,1,0:T(8,128)S(1)} collective-permute-done((f32[3,32,1]{2,1,0:T(8,128)S(1)}, f32[3,32,1]{2,1,0:T(8,128)S(1)}, u32[]{:S(2)}, u32[]{:S(2)}) %collective-permute-start.4) | collective-permute-done | bytes 416 | tf_op jit(solution)/shard_map/ppermute | solution.py:22
  51.0 1.9 collective-permute-start.5
  53.0 4.2 %collective-permute-start.3 = (f32[3,1,128]{2,1,0:T(1,128)S(1)}, f32[3,1,128]{2,1,0:T(1,128)S(1)}, u32[]{:S(2)}, u32[]{:S(2)}) collective-permute-start(f32[3,1,128]{2,1,0:T(1,128)S(1)} %slice.163), channel_id=1, source_target_pairs={{0,16},{16,32},{32,48},{48,64},{64,80},{80,96},{96,112},{112,128},... | collective-permute-start | bytes 4616 | tf_op jit(solution)/shard_map/ppermute | solution.py:22
  57.9 3.5 fusion.1
  61.4 3.4 convolution_bitcast_fusion.1
  64.9 3.6 fusion
  68.5 2.0 copy-done.1
  70.4 1.4 convolution_bitcast_fusion
  74.6 1.2 fusion.56
  76.3 9.7 %collective-permute-start.6 = (f32[32,42,1]{1,0,2:T(8,128)S(1)}, f32[32,42,1]{1,0,2:T(8,128)S(1)}, u32[]{:S(2)}, u32[]{:S(2)}) collective-permute-start(f32[32,42,1]{1,0,2:T(8,128)S(1)} %pad_maximum_fusion.8), channel_id=1, source_target_pairs={{0,1},{1,2},{2,3},{3,4},{4,5},{5,6},{6,7},{7,8},{8,9},{9,10},{10,1... | collective-permute-start | bytes 16136 | tf_op jit(solution)/shard_map/ppermute | solution.py:22
  86.0 3.7 fusion.150
  90.1 1.2 copy.74
  92.6 4.2 %collective-permute-start.7 = (f32[32,1,160]{2,1,0:T(1,128)S(1)}, f32[32,1,160]{2,1,0:T(1,128)S(1)}, u32[]{:S(2)}, u32[]{:S(2)}) collective-permute-start(f32[32,1,160]{2,1,0:T(1,128)S(1)} %fusion.80), channel_id=1, source_target_pairs={{0,16},{16,32},{32,48},{48,64},{64,80},{80,96},{96,112},{112,128},... | collective-permute-start | bytes 61448 | tf_op jit(solution)/shard_map/ppermute | solution.py:22
  96.9 2.8 fusion.149
  102.8 80.8 %all-reduce = (f32[]{:T(128)}, f32[3,512]{1,0:T(4,128)S(1)}) all-reduce(f32[]{:T(128)S(6)} %add.300, f32[3,512]{1,0:T(4,128)S(1)} %fusion.149), channel_id=1, replica_groups=mesh['row'=16,'col'=16] {'row','col'}, use_global_device_ids=true, to_apply=%region_2.3 | all-reduce | flops 1537 | bytes 12296 | tf_op jit(solution)/shard_map/psum | solution.py:148
  184.9 1.7 fusion.49
  186.6 2.5 fusion.29
  189.0 172.6 %all-reduce.4.cloned.1.call-done = (f32[512,64]{0,1:T(8,128)}, f32[1,512,512]{2,1,0:T(8,128)}) async-done(((f32[512,64]{0,1:T(8,128)}, f32[1,512,512]{2,1,0:T(8,128)}), (f32[512,64]{0,1:T(8,128)}, f32[1,512,512]{2,1,0:T(8,128)})) %all-reduce.4.cloned.1.call-update) | async-done | bytes 1179664 | tf_op jit(solution)/shard_map/psum | solution.py:252
  361.6 2.1 multiply_reduce_fusion
  363.7 1.5 multiply_reduce_fusion.2
  367.9 3.2 fusion.24
  371.1 1.7 fusion.54
  (97 shorter events, 16.6 us)
Async XLA Ops:
  7.2 26.0 %copy-start.3 = (f32[512,64]{0,1:T(8,128)S(1)}, f32[512,64]{0,1:T(8,128)}, u32[]{:S(2)}) copy-start(f32[512,64]{0,1:T(8,128)} %param.21) | copy-start | bytes 393220
  7.2 354.5 %all-reduce.4.cloned.1.call-start = ((), (), s32[]{:S(2)}) async-start(), calls=%async_computation | async-start | bytes 2359296 | tf_op jit(solution)/shard_map/psum | solution.py:252
  9.2 5.2 %collective-permute-start = (f32[32,1,160]{2,1,0:T(1,128)S(1)}, f32[32,1,160]{2,1,0:T(1,128)S(1)}, u32[]{:S(2)}, u32[]{:S(2)}) collective-permute-start(f32[32,1,160]{2,1,0:T(1,128)S(1)} %copy.60), channel_id=1, source_target_pairs={{16,0},{32,16},{48,32},{64,48},{80,64},{96,80},{112,96},{128,112},... | collective-permute-start | bytes 61448 | tf_op jit(solution)/shard_map/ppermute | solution.py:22
  16.3 12.2 %collective-permute-start.1 = (f32[32,42,1]{1,0,2:T(8,128)S(1)}, f32[32,42,1]{1,0,2:T(8,128)S(1)}, u32[]{:S(2)}, u32[]{:S(2)}) collective-permute-start(f32[32,42,1]{1,0,2:T(8,128)S(1)} %pad_maximum_fusion.7), channel_id=1, source_target_pairs={{1,0},{2,1},{3,2},{4,3},{5,4},{6,5},{7,6},{8,7},{9,8},{10,9},{11,1... | collective-permute-start | bytes 16136 | tf_op jit(solution)/shard_map/ppermute | solution.py:22
  31.4 3.1 copy-start.11
  34.5 4.4 %copy-start.8 = (f32[3,512]{1,0:T(4,128)S(1)}, f32[3,512]{1,0:T(4,128)}, u32[]{:S(2)}) copy-start(f32[3,512]{1,0:T(4,128)} %param.23) | copy-start | bytes 18436
  34.5 16.3 %copy-start.4 = (f32[3,3,32,128]{3,2,1,0:T(8,128)S(1)}, f32[3,3,32,128]{3,2,1,0:T(8,128)}, u32[]{:S(2)}) copy-start(f32[3,3,32,128]{3,2,1,0:T(8,128)} %param.18) | copy-start | bytes 442372
  38.9 22.5 %copy-start = (bf16[512,4096]{0,1:T(8,128)(2,1)}, bf16[512,4096]{0,1:T(8,128)(2,1)S(1)}, u32[]{:S(2)}) copy-start(bf16[512,4096]{0,1:T(8,128)(2,1)S(1)} %get-tuple-element.26) | copy-start | bytes 12582916
  40.2 10.6 %collective-permute-start.2 = (f32[3,1,128]{2,1,0:T(1,128)S(1)}, f32[3,1,128]{2,1,0:T(1,128)S(1)}, u32[]{:S(2)}, u32[]{:S(2)}) collective-permute-start(f32[3,1,128]{2,1,0:T(1,128)S(1)} %slice.162), channel_id=1, source_target_pairs={{16,0},{32,16},{48,32},{64,48},{80,64},{96,80},{112,96},{128,112},... | collective-permute-start | bytes 4616 | tf_op jit(solution)/shard_map/ppermute | solution.py:22
  41.5 9.3 %collective-permute-start.4 = (f32[3,32,1]{2,1,0:T(8,128)S(1)}, f32[3,32,1]{2,1,0:T(8,128)S(1)}, u32[]{:S(2)}, u32[]{:S(2)}) collective-permute-start(f32[3,32,1]{2,1,0:T(8,128)S(1)} %bitcast.213), channel_id=1, source_target_pairs={{1,0},{2,1},{3,2},{4,3},{5,4},{6,5},{7,6},{8,7},{9,8},{10,9},{11,1... | collective-permute-start | bytes 1160 | tf_op jit(solution)/shard_map/ppermute | solution.py:22
  51.0 6.2 %collective-permute-start.5 = (f32[3,32,1]{2,1,0:T(8,128)S(1)}, f32[3,32,1]{2,1,0:T(8,128)S(1)}, u32[]{:S(2)}, u32[]{:S(2)}) collective-permute-start(f32[3,32,1]{2,1,0:T(8,128)S(1)} %slice.167), channel_id=1, source_target_pairs={{0,1},{1,2},{2,3},{3,4},{4,5},{5,6},{6,7},{7,8},{8,9},{9,10},{10,1... | collective-permute-start | bytes 1160 | tf_op jit(solution)/shard_map/ppermute | solution.py:22
  53.0 4.7 %collective-permute-start.3 = (f32[3,1,128]{2,1,0:T(1,128)S(1)}, f32[3,1,128]{2,1,0:T(1,128)S(1)}, u32[]{:S(2)}, u32[]{:S(2)}) collective-permute-start(f32[3,1,128]{2,1,0:T(1,128)S(1)} %slice.163), channel_id=1, source_target_pairs={{0,16},{16,32},{32,48},{48,64},{64,80},{80,96},{96,112},{112,128},... | collective-permute-start | bytes 4616 | tf_op jit(solution)/shard_map/ppermute | solution.py:22
  68.5 2.0 copy-start.1
  76.3 15.4 %collective-permute-start.6 = (f32[32,42,1]{1,0,2:T(8,128)S(1)}, f32[32,42,1]{1,0,2:T(8,128)S(1)}, u32[]{:S(2)}, u32[]{:S(2)}) collective-permute-start(f32[32,42,1]{1,0,2:T(8,128)S(1)} %pad_maximum_fusion.8), channel_id=1, source_target_pairs={{0,1},{1,2},{2,3},{3,4},{4,5},{5,6},{6,7},{7,8},{8,9},{9,10},{10,1... | collective-permute-start | bytes 16136 | tf_op jit(solution)/shard_map/ppermute | solution.py:22
  89.7 95.2 %copy-start.5 = (f32[32,8,32]{2,1,0:T(8,128)S(1)}, f32[32,8,32]{2,1,0:T(8,128)}, u32[]{:S(2)}) copy-start(f32[32,8,32]{2,1,0:T(8,128)} %param.27) | copy-start | bytes 98308
  91.7 275.5 %copy-start.9 = (f32[3,512]{1,0:T(4,128)S(1)}, f32[3,512]{1,0:T(4,128)}, u32[]{:S(2)}) copy-start(f32[3,512]{1,0:T(4,128)} %param.33) | copy-start | bytes 18436
  91.7 275.5 %copy-start.10 = (f32[3,512]{1,0:T(4,128)S(1)}, f32[3,512]{1,0:T(4,128)}, u32[]{:S(2)}) copy-start(f32[3,512]{1,0:T(4,128)} %param.32) | copy-start | bytes 18436
  91.7 276.2 %copy-start.2 = (f32[1,512,512]{2,1,0:T(8,128)S(1)}, f32[1,512,512]{2,1,0:T(8,128)}, u32[]{:S(2)}) copy-start(f32[1,512,512]{2,1,0:T(8,128)} %param.31) | copy-start | bytes 3145732
  92.6 278.5 %copy-start.6 = (f32[512,64]{0,1:T(8,128)S(1)}, f32[512,64]{0,1:T(8,128)}, u32[]{:S(2)}) copy-start(f32[512,64]{0,1:T(8,128)} %param.29) | copy-start | bytes 393220
  92.6 278.5 %copy-start.7 = (f32[512,64]{0,1:T(8,128)S(1)}, f32[512,64]{0,1:T(8,128)}, u32[]{:S(2)}) copy-start(f32[512,64]{0,1:T(8,128)} %param.28) | copy-start | bytes 393220
  92.6 7.1 %collective-permute-start.7 = (f32[32,1,160]{2,1,0:T(1,128)S(1)}, f32[32,1,160]{2,1,0:T(1,128)S(1)}, u32[]{:S(2)}, u32[]{:S(2)}) collective-permute-start(f32[32,1,160]{2,1,0:T(1,128)S(1)} %fusion.80), channel_id=1, source_target_pairs={{0,16},{16,32},{32,48},{48,64},{64,80},{80,96},{96,112},{112,128},... | collective-permute-start | bytes 61448 | tf_op jit(solution)/shard_map/ppermute | solution.py:22
Sparse Core Ops, SparseCore 0:
  102.9 258.7 all-reduce.3
where the time goes:
time: 382 us; the launch traced here: 380 us
  waiting for transfers between devices  187 us (49%)
  blocking collectives  80.8 us (21%)
  matrix products  31.7 us (8%)
  starting transfers between devices  30.3 us (8%)
  between operations  19.8 us (5%)
  other arithmetic  17.6 us (5%)
  local copies, waits for them, and re-layouts  12.2 us (3%)
    psum x1, waiting for transfers between devices, shards(): lax.psum((grad_in, grad_mid, grad_out), ('row', 'col'))  173 us
    psum x1, blocking collectives, grid_total_sum(): return lax.psum(grid_local, ('row', 'col'))  80.8 us
    ppermute x8, starting transfers between devices, shifted(): return lax.ppermute(block, axis, route)  30.3 us
    ppermute x8, waiting for transfers between devices, shifted(): return lax.ppermute(block, axis, route)  14.6 us
    dot_general x3, matrix products, contract_cols(): lax.dot_general(former, latter, (((1,), (1,)), ((), ())), preferred_eleme...  9.94 us
    div x5, other arithmetic, adam_step(): new_one / (1.0 - BETA_ONE ** ADAM_STEP)  9.61 us
    dot_general x3, matrix products, contract_rows(): lax.dot_general(former, latter, (((0,), (0,)), ((), ())), preferred_eleme...  8.46 us
  transfers between devices with their start and end apart: 9, of which 5 were waited for; matrix products, arithmetic and copies ran while one was open for 4% of the time, Pallas kernels for 0%

commit v1 on v0

--- a/solution.py
+++ b/solution.py
@@ -1,7 +1,13 @@
 import jax
 import jax.numpy as jnp
 from jax import lax
+from jax.experimental import pallas as pl
+from jax.experimental.pallas import tpu as pltpu
+from jax.sharding import Mesh
 from jax.sharding import PartitionSpec as P
+
+ROW = ("zl", "x")
+COL = ("y", "zh", "c")
 
 SUB = 4
 RATIO = 4
@@ -16,8 +22,15 @@
 MEAN_EPSILON = 1e-06
 
 
+def axes_size(axes):
+    total = 1
+    for axis in axes:
+        total *= lax.axis_size(axis)
+    return total
+
+
 def shifted(block, axis, distance):
-    devices = range(lax.axis_size(axis))
+    devices = range(axes_size(axis))
     route = [(i - distance, i) for i in devices if i - distance in devices]
     return lax.ppermute(block, axis, route)
 
@@ -116,9 +129,9 @@
     grads_mid.insert(0, contract_cols(delta_low, activations[0]))
     upward = contract_rows(low_mid[0], delta_low)
     delta_low = (upward * silu_slope(pre_acts[0])).astype(jnp.bfloat16)
-    grad_in = contract_cols(delta_low, features)
+    grad_in = contract_cols(features, delta_low)
     feature_grad = contract_rows(low_in, delta_low)
-    return (grad_in, jnp.stack(grads_mid), grad_out, feature_grad)
+    return (grad_in, grads_mid[0], grad_out, feature_grad)
 
 
 def pixel_cotangent(value_error, row_error, row_prior, col_error, col_prior):
@@ -144,8 +157,142 @@
     )
 
 
-def grid_total_sum(grid_local):
-    return lax.psum(grid_local, ("row", "col"))
+def swapped(block, axis, mask):
+    size = lax.axis_size(axis)
+    return lax.ppermute(block, axis, [(i, i ^ mask) for i in range(size)])
+
+
+def pair_sum(values):
+    values = list(values)
+    while len(values) > 1:
+        values = [values[i] + values[i + 1] for i in range(0, len(values), 2)]
+    return values[0]
+
+
+def exchange_sum(block, axis):
+    return pair_sum([block] + [swapped(block, axis, d) for d in range(1, lax.axis_size(axis))])
+
+
+def exchange_gather(block, axis):
+    return [block] + [swapped(block, axis, d) for d in range(1, lax.axis_size(axis))]
+
+
+def scatter_sum(blocks, axis):
+    return pair_sum([blocks[0]] + [swapped(blocks[d], axis, d) for d in range(1, len(blocks))])
+
+
+def vmem():
+    return pl.BlockSpec(memory_space=pltpu.VMEM)
+
+
+def smem():
+    return pl.BlockSpec(memory_space=pltpu.SMEM)
+
+
+def split_kernel(place_ref, mid_ref, in_ref, out_ref, keep_ref, send_ref):
+    core = place_ref[0]
+    tile = place_ref[1]
+    for d in range(16):
+        chunk = tile ^ d
+        band = chunk >> 1
+        side = chunk & 1
+        for half, target in ((core, keep_ref), (1 - core, send_ref)):
+            cols = pl.ds(pl.multiple_of((half * 2 + side) * 128, 128), 128)
+            target[d, 0:64, :] = mid_ref[pl.ds(pl.multiple_of(band * 64, 64), 64), cols]
+            target[d, 64:72, :] = in_ref[pl.ds(pl.multiple_of(band * 8, 8), 8), cols]
+            target[d, 72:80, :] = jnp.where(band == 0, out_ref[:, cols], 0.0)
+
+
+def split_grads(place, grad_mid, grad_in, grad_out):
+    part = jax.ShapeDtypeStruct((16, 80, 128), jnp.float32)
+    return pl.pallas_call(
+        split_kernel,
+        out_shape=(part, part),
+        in_specs=[smem(), vmem(), vmem(), vmem()],
+        out_specs=(vmem(), vmem()),
+        name="split_grads",
+    )(place, grad_mid, grad_in, grad_out)
+
+
+def decoder_kernel(
+    place_ref,
+    own_ref,
+    other_ref,
+    mid_one_ref,
+    mid_two_ref,
+    in_one_ref,
+    in_two_ref,
+    out_one_ref,
+    out_two_ref,
+    mid_ref,
+    in_ref,
+    out_ref,
+    scale_ref,
+    in_grad,
+    out_grad,
+    *,
+    decoder_entries,
+    grid_entries,
+):
+    core = place_ref[0]
+    tile = place_ref[1]
+    own_sum = pair_sum([own_ref[d, 80:88, :] for d in range(16)])
+    other_sum = pair_sum([other_ref[d, 80:88, :] for d in range(16)])
+    totals = own_sum + other_sum
+    grid_scale = clip_factor(totals[0:1, :], grid_entries)
+    scale = clip_factor(totals[1:2, :], decoder_entries)
+    scale_ref[...] = grid_scale
+    for band in range(8):
+        for block in range(4):
+            half = block // 2
+            chunk = band * 2 + block % 2
+            d = tile ^ chunk
+            data = jnp.where(half == core, own_ref[d, 0:80, :], other_ref[d, 0:80, :])
+            cols = slice(block * 128, block * 128 + 128)
+            rows = slice(band * 64, band * 64 + 64)
+            mid_ref[rows, cols] = adam_step(
+                data[0:64], mid_one_ref[rows, cols], mid_two_ref[rows, cols], scale
+            )
+            in_grad[band * 8 : band * 8 + 8, cols] = data[64:72]
+            if band == 0:
+                out_grad[:, cols] = data[72:80]
+    for block in range(4):
+        cols = slice(block * 128, block * 128 + 128)
+        turned = in_grad[:, cols].T
+        in_ref[cols, :] = adam_step(turned, in_one_ref[cols, :], in_two_ref[cols, :], scale[:, 0:64])
+        out_ref[:, cols] = adam_step(
+            out_grad[0:3, cols], out_one_ref[:, cols], out_two_ref[:, cols], scale
+        )
+
+
+def decoder_steps(place, own, other, moments, decoder_entries, grid_entries):
+    shapes = (moments[0].shape, moments[2].shape, moments[4].shape, (1, 128))
+    return pl.pallas_call(
+        lambda *refs: decoder_kernel(
+            *refs, decoder_entries=decoder_entries, grid_entries=grid_entries
+        ),
+        out_shape=tuple(jax.ShapeDtypeStruct(s, jnp.float32) for s in shapes),
+        in_specs=[smem()] + [vmem()] * 8,
+        out_specs=(vmem(),) * 4,
+        scratch_shapes=[pltpu.VMEM((64, 512), jnp.float32), pltpu.VMEM((8, 512), jnp.float32)],
+        name="decoder_steps",
+    )(place, own, other, *moments)
+
+
+def reduce_grads(place, grad_mid, grad_in, grad_out, grid_local):
+    keep, send = split_grads(place, grad_mid, grad_in, grad_out)
+    part = keep + swapped(send, "c", 1)
+    part = scatter_sum([part[d * 4 : d * 4 + 4] for d in range(4)], "x")
+    part = scatter_sum([part[d] for d in range(4)], "y")
+    tail = jnp.broadcast_to(grid_local, (8, 128))
+    part = exchange_sum(jnp.concatenate([part, tail]), "zl")
+    part = exchange_sum(part, "zh")
+    squares = jnp.sum(part[:80] * part[:80])
+    tail = jnp.where(jnp.arange(8)[:, None] == 1, squares, part[80:])
+    part = jnp.concatenate([part[:80], tail])
+    own = jnp.stack(exchange_gather(part, "y"))
+    own = jnp.concatenate(exchange_gather(own, "x"))
+    return own, swapped(own, "c", 1)
 
 
 def shards(
@@ -174,11 +321,11 @@
     low_mid = weight_mid.astype(jnp.bfloat16)
     low_out = weight_out.astype(jnp.bfloat16)
     top_rows = jnp.concatenate([grid_fine[:, :1, :], grid_coarse[:, :1, :]], axis=2)
-    top_rows = shifted(top_rows, "row", -1)
+    top_rows = shifted(top_rows, ROW, -1)
     fine_tall = jnp.concatenate([grid_fine, top_rows[:, :, :sample_cols]], axis=1)
     coarse_tall = jnp.concatenate([grid_coarse, top_rows[:, :, sample_cols:]], axis=1)
     edge_cols = jnp.concatenate([fine_tall[:, :, :1], coarse_tall[:, :, :1]], axis=1)
-    edge_cols = shifted(edge_cols, "col", -1)
+    edge_cols = shifted(edge_cols, COL, -1)
     fine_ext = jnp.concatenate([fine_tall, edge_cols[:, : sample_rows + 1, :]], axis=2)
     coarse_ext = jnp.concatenate([coarse_tall, edge_cols[:, sample_rows + 1 :, :]], axis=2)
     tables = level_tables(sample_rows, sample_cols, offsets[0, 0, 0], offsets[0, 0, 1])
@@ -186,19 +333,19 @@
     predicted, pre_acts, activations = decoder_forward(features, low_in, low_mid, low_out)
     outputs = predicted.shape[0]
     predicted = predicted.reshape(outputs, sample_rows, sample_cols)
-    below = shifted(predicted[:, :1, :], "row", -1)
-    beside = shifted(predicted[:, :, :1], "col", -1)
-    row_global = lax.axis_index("row") * sample_rows + jnp.arange(sample_rows, dtype=jnp.int32)
-    col_global = lax.axis_index("col") * sample_cols + jnp.arange(sample_cols, dtype=jnp.int32)
-    row_valid = (row_global < lax.axis_size("row") * sample_rows - 1)[None, :, None]
-    col_valid = (col_global < lax.axis_size("col") * sample_cols - 1)[None, None, :]
+    below = shifted(predicted[:, :1, :], ROW, -1)
+    beside = shifted(predicted[:, :, :1], COL, -1)
+    row_global = lax.axis_index(ROW) * sample_rows + jnp.arange(sample_rows, dtype=jnp.int32)
+    col_global = lax.axis_index(COL) * sample_cols + jnp.arange(sample_cols, dtype=jnp.int32)
+    row_valid = (row_global < axes_size(ROW) * sample_rows - 1)[None, :, None]
+    col_valid = (col_global < axes_size(COL) * sample_cols - 1)[None, None, :]
     row_next = jnp.concatenate([predicted[:, 1:, :], below], axis=1)
     col_next = jnp.concatenate([predicted[:, :, 1:], beside], axis=2)
     value_error = predicted - targets[0]
     row_error = jnp.where(row_valid, row_next - predicted - targets[1], 0.0)
     col_error = jnp.where(col_valid, col_next - predicted - targets[2], 0.0)
-    above = shifted(row_error[:, -1:, :], "row", 1)
-    before = shifted(col_error[:, :, -1:], "col", 1)
+    above = shifted(row_error[:, -1:, :], ROW, 1)
+    before = shifted(col_error[:, :, -1:], COL, 1)
     row_prior = jnp.concatenate([above, row_error[:, :-1, :]], axis=1)
     col_prior = jnp.concatenate([before, col_error[:, :, :-1]], axis=2)
     cotangent = pixel_cotangent(value_error, row_error, row_prior, col_error, col_prior)
@@ -215,7 +362,7 @@
     side_cols = jnp.concatenate(
         [fine_back[:, :, sample_cols:], coarse_back[:, :, coarse_cols:]], axis=1
     )
-    side_cols = shifted(side_cols, "col", 1)
+    side_cols = shifted(side_cols, COL, 1)
     fine_tall_grad = jnp.concatenate(
         [fine_back[:, :, :1] + side_cols[:, : sample_rows + 1, :], fine_back[:, :, 1:sample_cols]],
         axis=2,
@@ -230,7 +377,7 @@
     bottom_rows = jnp.concatenate(
         [fine_tall_grad[:, sample_rows:, :], coarse_tall_grad[:, coarse_rows:, :]], axis=2
     )
-    bottom_rows = shifted(bottom_rows, "row", 1)
+    bottom_rows = shifted(bottom_rows, ROW, 1)
     fine_grad = jnp.concatenate(
         [
             fine_tall_grad[:, :1, :] + bottom_rows[:, :, :sample_cols],
@@ -246,37 +393,46 @@
         axis=1,
     )
     grid_local = jnp.sum(fine_grad * fine_grad) + jnp.sum(coarse_grad * coarse_grad)
-    devices = lax.axis_size("row") * lax.axis_size("col")
+    devices = axes_size(ROW) * axes_size(COL)
     grid_entries = (fine_grad.size + coarse_grad.size) * devices
     decoder_entries = weight_in.size + weight_mid.size + weight_out.size
-    grad_in, grad_mid, grad_out = lax.psum((grad_in, grad_mid, grad_out), ("row", "col"))
-    grid_total = grid_total_sum(grid_local)
-    decoder_total = (
-        jnp.sum(grad_in * grad_in) + jnp.sum(grad_mid * grad_mid) + jnp.sum(grad_out * grad_out)
-    )
-    decoder_scale = clip_factor(decoder_total, decoder_entries)
-    middle_step = adam_step(grad_mid, mid_first, mid_second, decoder_scale)
-    grid_scale = clip_factor(grid_total, grid_entries)
+    place = jnp.stack([lax.axis_index("c"), lax.axis_index("x") * 4 + lax.axis_index("y")])
+    own, other = reduce_grads(
+        place,
+        grad_mid,
+        grad_in,
+        jnp.concatenate([grad_out, jnp.zeros((5, grad_out.shape[1]), jnp.float32)]),
+        grid_local,
+    )
+    middle_step, input_step, output_step, scale = decoder_steps(
+        place,
+        own,
+        other,
+        (mid_first[0], mid_second[0], in_first, in_second, out_first, out_second),
+        decoder_entries,
+        grid_entries,
+    )
+    grid_scale = scale[0, 0]
     fine_step = adam_step(fine_grad, fine_first, fine_second, grid_scale)
     coarse_step = adam_step(coarse_grad, coarse_first, coarse_second, grid_scale)
-    input_step = adam_step(grad_in, in_first, in_second, decoder_scale)
-    output_step = adam_step(grad_out, out_first, out_second, decoder_scale)
-    return (fine_step, coarse_step, input_step, middle_step, output_step)
+    return (fine_step, coarse_step, input_step, middle_step[None], output_step)
 
 
 def solution(mesh):
+    sizes = {"zl": 4, "x": 4, "y": 4, "zh": 2, "c": 2}
+    mesh = Mesh(mesh.devices.reshape(tuple(sizes.values())), tuple(sizes))
     placed = (
-        P("row", "col", None),
-        P(None, None, "row", "col"),
-        P(None, "row", "col"),
-        P(None, "row", "col"),
-        P(),
-        P(),
-        P(),
-        P(None, "row", "col"),
-        P(None, "row", "col"),
-        P(None, "row", "col"),
-        P(None, "row", "col"),
+        P(ROW, COL, None),
+        P(None, None, ROW, COL),
+        P(None, ROW, COL),
+        P(None, ROW, COL),
+        P(),
+        P(),
+        P(),
+        P(None, ROW, COL),
+        P(None, ROW, COL),
+        P(None, ROW, COL),
+        P(None, ROW, COL),
         P(),
         P(),
         P(),
@@ -288,6 +444,6 @@
         shards,
         mesh=mesh,
         in_specs=placed,
-        out_specs=(P(None, "row", "col"), P(None, "row", "col"), P(), P(), P()),
+        out_specs=(P(None, ROW, COL), P(None, ROW, COL), P(), P(), P()),
         check_vma=False,
     )

time: 382 us -> 184 us (0.48)
  waiting for transfers between devices: 187 us -> 43.6 us
  blocking collectives: 80.8 us -> 0 us
  starting transfers between devices: 30.3 us -> 65 us
  between operations: 19.8 us -> 3.93 us
  Pallas kernels: 0 us -> 6.77 us
  other arithmetic: 17.6 us -> 12.2 us
  local copies, waits for them, and re-layouts: 12.2 us -> 16.7 us
    psum x1 -> x0, waiting for transfers between devices: 173 us -> none  [shards(): lax.psum((grad_in, grad_mid, grad_out), ('row', 'col'))]
    psum x1 -> x0, blocking collectives: 80.8 us -> none  [grid_total_sum(): return lax.psum(grid_local, ('row', 'col'))]
    ppermute x0 -> x18, starting transfers between devices: none -> 34.7 us  [swapped(): return lax.ppermute(block, axis, [(i, i ^ mask) for i in range(size)])]
    ppermute x0 -> x18, waiting for transfers between devices: none -> 28.2 us  [swapped(): return lax.ppermute(block, axis, [(i, i ^ mask) for i in range(size)])]
    pallas_call x0 -> x2, Pallas kernels: none -> 6.77 us  [the longest x1 4.16 us: decoder_steps(): pl.pallas_call(lambda *refs: decoder_kernel(*refs, decoder_entries=decode...]
    unnamed x32 -> x46, local copies, waits for them, and re-layouts: 4.27 us -> 9.58 us
    div x5 -> x2, other arithmetic: 9.61 us -> 5.2 us  [adam_step(): new_one / (1.0 - BETA_ONE ** ADAM_STEP)]
    reduce_sum x3 -> x0, other arithmetic: 4.3 us -> none  [the longest x1 2.1 us: shards(): jnp.sum(grad_mid * grad_mid)]
  transfers between devices with their start and end apart: 9 -> 26, of which waited for: 5 -> 16; matrix products, arithmetic and copies ran while one was open for 4% -> 7% of each run, Pallas kernels for 0% -> 1%
where the time goes in v1:
time: 184 us; the launch traced here: 183 us
  starting transfers between devices  65 us (35%)
  waiting for transfers between devices  43.6 us (24%)
  matrix products  35.2 us (19%)
  local copies, waits for them, and re-layouts  16.7 us (9%)
  other arithmetic  12.2 us (7%)
  Pallas kernels  6.77 us (4%)
  between operations  3.93 us (2%)
    ppermute x18, starting transfers between devices, swapped(): return lax.ppermute(block, axis, [(i, i ^ mask) for i in range(size)])  34.7 us
    ppermute x8, starting transfers between devices, shifted(): return lax.ppermute(block, axis, route)  30.2 us
    ppermute x18, waiting for transfers between devices, swapped(): return lax.ppermute(block, axis, [(i, i ^ mask) for i in range(size)])  28.2 us
    ppermute x8, waiting for transfers between devices, shifted(): return lax.ppermute(block, axis, route)  15.4 us
    dot_general x3, matrix products, contract_rows(): lax.dot_general(former, latter, (((0,), (0,)), ((), ())), preferred_eleme...  10.7 us
    dot_general x3, matrix products, matmul(): return jnp.dot(former, latter, preferred_element_type=jnp.float32)  10.4 us
    unnamed x46, local copies, waits for them, and re-layouts  9.58 us
    dot_general x3, matrix products, contract_cols(): lax.dot_general(former, latter, (((1,), (1,)), ((), ())), preferred_eleme...  7.65 us
  transfers between devices with their start and end apart: 26, of which 16 were waited for; matrix products, arithmetic and copies ran while one was open for 7% of the time, Pallas kernels for 1%

profile of v1, /device:TPU:1, one launch (start us, length us, event | category | flops | bytes accessed | tf_op | source)
XLA Modules:
  0.0 183.4 jit_solution(6614667756605946846)
XLA Ops:
  9.6 5.7 %collective-permute-start.1 = (f32[32,42,1]{1,0,2:T(8,128)S(1)}, f32[32,42,1]{1,0,2:T(8,128)S(1)}, u32[]{:S(2)}, u32[]{:S(2)}) collective-permute-start(f32[32,42,1]{1,0,2:T(8,128)S(1)} %pad_maximum_fusion.9), channel_id=1, source_target_pairs={{1,0},{2,1},{3,2},{4,3},{5,4},{6,5},{7,6},{8,7},{9,8},{10,9},{11,1... | collective-permute-start | bytes 16136 | tf_op jit(solution)/shard_map/ppermute | solution.py:35
  15.4 6.5 %collective-permute-done.1 = f32[32,42,1]{1,0,2:T(8,128)S(1)} collective-permute-done((f32[32,42,1]{1,0,2:T(8,128)S(1)}, f32[32,42,1]{1,0,2:T(8,128)S(1)}, u32[]{:S(2)}, u32[]{:S(2)}) %collective-permute-start.1) | collective-permute-done | bytes 5408 | tf_op jit(solution)/shard_map/ppermute | solution.py:35
  22.2 2.2 %fusion.14 = f32[32,33,128]{2,1,0:T(8,128)S(1)} fusion(f32[32,33,1]{2,1,0:T(8,128)S(1)} %copy.74, f32[32,1,128]{2,1,0:T(1,128)S(1)} %slice.203, f32[32,32,128]{2,1,0:T(8,128)} %param.19, f32[]{:T(128)} %bitcast.1, s32[128]{0:T(128)S(1)} %iota_add_fusion.1, f32[]{:T(128)S(6)} %sub.86), kind=kOutput, calls=%fused_computation.23 | convolution fusion | flops 209595072 | bytes 1086088 | tf_op jit(solution)/shard_map/kjl,ml->kjm/dot_general | solution.py:60
  26.6 4.6 %fusion.11 = (bf16[512,4096]{0,1:T(8,128)(2,1)S(1)}, f32[4096,512]{1,0:T(8,128)}) fusion(bf16[64,4096]{1,0:T(8,128)(2,1)S(1)} %bitcast_dynamic-update-slice_fusion, f32[512,64]{0,1:T(8,128)S(1)} %copy-done.8), kind=kOutput, calls=%fused_computation.19 | convolution fusion | flops 278953984 | bytes 13238272 | tf_op jit(solution)/shard_map/dot_general | solution.py:95
  31.2 4.6 %fusion.5 = (bf16[512,4096]{0,1:T(8,128)(2,1)S(1)}, f32[4096,512]{1,0:T(8,128)}) fusion(bf16[512,4096]{0,1:T(8,128)(2,1)S(1)} %get-tuple-element.64, f32[1,512,512]{2,1,0:T(8,128)S(1)} %copy-done.12), kind=kOutput, calls=%fused_computation.10 | convolution fusion | flops 2158231552 | bytes 17825792 | tf_op jit(solution)/shard_map/dot_general | solution.py:95
  35.8 2.0 %copy-done = bf16[512,4096]{0,1:T(8,128)(2,1)} copy-done((bf16[512,4096]{0,1:T(8,128)(2,1)}, bf16[512,4096]{0,1:T(8,128)(2,1)S(1)}, u32[]{:S(2)}) %copy-start) | copy-done | bytes 4194328
  40.3 1.9 %collective-permute-start.4 = (f32[3,32,1]{2,1,0:T(8,128)S(1)}, f32[3,32,1]{2,1,0:T(8,128)S(1)}, u32[]{:S(2)}, u32[]{:S(2)}) collective-permute-start(f32[3,32,1]{2,1,0:T(8,128)S(1)} %bitcast.239), channel_id=1, source_target_pairs={{1,0},{2,1},{3,2},{4,3},{5,4},{6,5},{7,6},{8,7},{9,8},{10,9},{11,1... | collective-permute-start | bytes 1160 | tf_op jit(solution)/shard_map/ppermute | solution.py:35
  42.4 7.2 %collective-permute-done.4 = f32[3,32,1]{2,1,0:T(8,128)S(1)} collective-permute-done((f32[3,32,1]{2,1,0:T(8,128)S(1)}, f32[3,32,1]{2,1,0:T(8,128)S(1)}, u32[]{:S(2)}, u32[]{:S(2)}) %collective-permute-start.4) | collective-permute-done | bytes 416 | tf_op jit(solution)/shard_map/ppermute | solution.py:35
  49.8 2.2 %collective-permute-start.5 = (f32[3,32,1]{2,1,0:T(8,128)S(1)}, f32[3,32,1]{2,1,0:T(8,128)S(1)}, u32[]{:S(2)}, u32[]{:S(2)}) collective-permute-start(f32[3,32,1]{2,1,0:T(8,128)S(1)} %slice.213), channel_id=1, source_target_pairs={{0,1},{1,2},{2,3},{3,4},{4,5},{5,6},{6,7},{7,8},{8,9},{9,10},{10,1... | collective-permute-start | bytes 1160 | tf_op jit(solution)/shard_map/ppermute | solution.py:35
  52.7 4.2 %collective-permute-start.3 = (f32[3,1,128]{2,1,0:T(1,128)S(1)}, f32[3,1,128]{2,1,0:T(1,128)S(1)}, u32[]{:S(2)}, u32[]{:S(2)}) collective-permute-start(f32[3,1,128]{2,1,0:T(1,128)S(1)} %slice.209), channel_id=1, source_target_pairs={{0,16},{16,32},{32,48},{48,64},{64,80},{80,96},{96,112},{112,128},... | collective-permute-start | bytes 4616 | tf_op jit(solution)/shard_map/ppermute | solution.py:35
  57.7 5.8 %fusion.1 = bf16[512,4096]{0,1:T(8,128)(2,1)S(1)} fusion(f32[4096,512]{1,0:T(8,128)} %get-tuple-element.67, bf16[3,4096]{1,0:T(4,128)(2,1)S(1)} %fusion.54, f32[3,512]{1,0:T(4,128)S(1)} %copy-done.11), kind=kOutput, calls=%fused_computation.3 | convolution fusion | flops 31458816 | bytes 12613632 | tf_op jit(solution)/shard_map/dot_general | solution.py:99
  63.5 3.3 %fusion.138.mid_ref = f32[512,512]{1,0:T(8,128)} fusion(bf16[512,4096]{0,1:T(8,128)(2,1)S(1)} %fusion.1, bf16[512,4096]{0,1:T(8,128)(2,1)S(1)} %copy-done.2), kind=kOutput, calls=%fused_computation.237 | convolution fusion | flops 2147483648 | bytes 9437184 | tf_op jit(solution)/shard_map/dot_general | solution.py:105
  66.8 3.6 %fusion = bf16[512,4096]{0,1:T(8,128)(2,1)S(1)} fusion(f32[4096,512]{1,0:T(8,128)S(1)} %bitcast.255, bf16[512,4096]{0,1:T(8,128)(2,1)S(1)} %fusion.1, f32[1,512,512]{2,1,0:T(8,128)S(1)} %copy-done.12), kind=kOutput, calls=%fused_computation.1 | convolution fusion | flops 2166620160 | bytes 17825792 | tf_op jit(solution)/shard_map/dot_general | solution.py:99
  77.2 9.7 %collective-permute-start.6 = (f32[32,42,1]{1,0,2:T(8,128)S(1)}, f32[32,42,1]{1,0,2:T(8,128)S(1)}, u32[]{:S(2)}, u32[]{:S(2)}) collective-permute-start(f32[32,42,1]{1,0,2:T(8,128)S(1)} %pad_maximum_fusion.10), channel_id=1, source_target_pairs={{0,1},{1,2},{2,3},{3,4},{4,5},{5,6},{6,7},{7,8},{8,9},{9,10},{10,1... | collective-permute-start | bytes 16136 | tf_op jit(solution)/shard_map/ppermute | solution.py:35
  86.9 2.8 %fusion.140 = f32[3,512]{1,0:T(4,128)S(1)} fusion(bf16[3,4096]{1,0:T(4,128)(2,1)S(1)} %fusion.54, bf16[512,4096]{0,1:T(8,128)(2,1)} %copy-done), kind=kOutput, calls=%fused_computation.239 | convolution fusion | flops 12582912 | bytes 4225024 | tf_op jit(solution)/shard_map/dot_general | solution.py:105
  90.7 2.6 %split_grads.1 = (f32[16,80,128]{2,1,0:T(8,128)}, f32[16,80,128]{2,1,0:T(8,128)}) custom-call(s32[2]{0:T(128)} %pad_add_fusion.place_ref.refs_0_, f32[512,512]{1,0:T(8,128)} %fusion.138.mid_ref, f32[64,512]{1,0:T(8,128)} %fusion.139.in_ref, f32[8,512]{1,0:T(8,128)} %concatenate.93.out_ref), custom_call_target="tpu_custom_call" | custom-call | tf_op jit(solution)/shard_map/split_grads/pallas_call | solution.py:208
  95.0 3.9 %collective-permute-start.7 = (f32[32,1,160]{2,1,0:T(1,128)S(1)}, f32[32,1,160]{2,1,0:T(1,128)S(1)}, u32[]{:S(2)}, u32[]{:S(2)}) collective-permute-start(f32[32,1,160]{2,1,0:T(1,128)S(1)} %fusion.73), channel_id=1, source_target_pairs={{0,16},{16,32},{32,48},{48,64},{64,80},{80,96},{96,112},{112,128},... | collective-permute-start | bytes 61448 | tf_op jit(solution)/shard_map/ppermute | solution.py:35
  101.3 2.0 %collective-permute-start.9 = (f32[4,80,128]{2,1,0:T(8,128)S(1)}, f32[4,80,128]{2,1,0:T(8,128)S(1)}, u32[]{:S(2)}, u32[]{:S(2)}) collective-permute-start(f32[4,80,128]{2,1,0:T(8,128)S(1)} %get-tuple-element.45), channel_id=1, source_target_pairs={{0,16},{16,0},{32,48},{48,32},{1,17},{17,1},{33,49},{49,33},{2,18}... | collective-permute-start | bytes 491528 | tf_op jit(solution)/shard_map/ppermute | solution.py:162
  103.3 7.3 %collective-permute-start.10 = (f32[4,80,128]{2,1,0:T(8,128)S(1)}, f32[4,80,128]{2,1,0:T(8,128)S(1)}, u32[]{:S(2)}, u32[]{:S(2)}) collective-permute-start(f32[4,80,128]{2,1,0:T(8,128)S(1)} %get-tuple-element.44), channel_id=1, source_target_pairs={{0,32},{16,48},{32,0},{48,16},{1,33},{17,49},{33,1},{49,17},{2,34}... | collective-permute-start | bytes 491528 | tf_op jit(solution)/shard_map/ppermute | solution.py:162
  110.8 6.0 %collective-permute-done.10 = f32[4,80,128]{2,1,0:T(8,128)S(1)} collective-permute-done((f32[4,80,128]{2,1,0:T(8,128)S(1)}, f32[4,80,128]{2,1,0:T(8,128)S(1)}, u32[]{:S(2)}, u32[]{:S(2)}) %collective-permute-start.10) | collective-permute-done | bytes 163872 | tf_op jit(solution)/shard_map/ppermute | solution.py:162
  116.7 3.1 %collective-permute-done.11 = f32[4,80,128]{2,1,0:T(8,128)S(1)} collective-permute-done((f32[4,80,128]{2,1,0:T(8,128)S(1)}, f32[4,80,128]{2,1,0:T(8,128)S(1)}, u32[]{:S(2)}, u32[]{:S(2)}) %collective-permute-start.11) | collective-permute-done | bytes 163872 | tf_op jit(solution)/shard_map/ppermute | solution.py:162
  127.1 2.8 %collective-permute-start.16 = (f32[88,128]{1,0:T(8,128)S(1)}, f32[88,128]{1,0:T(8,128)S(1)}, u32[]{:S(2)}, u32[]{:S(2)}) collective-permute-start(f32[88,128]{1,0:T(8,128)S(1)} %concatenate.95), channel_id=1, source_target_pairs={{0,128},{64,192},{128,0},{192,64},{1,129},{65,193},{129,1},{193,65... | collective-permute-start | bytes 135176 | tf_op jit(solution)/shard_map/ppermute | solution.py:162
  131.7 3.1 %collective-permute-done.17 = f32[88,128]{1,0:T(8,128)S(1)} collective-permute-done((f32[88,128]{1,0:T(8,128)S(1)}, f32[88,128]{1,0:T(8,128)S(1)}, u32[]{:S(2)}, u32[]{:S(2)}) %collective-permute-start.17) | collective-permute-done | bytes 45088 | tf_op jit(solution)/shard_map/ppermute | solution.py:162
  135.6 6.8 %collective-permute-done.18 = f32[88,128]{1,0:T(8,128)S(1)} collective-permute-done((f32[88,128]{1,0:T(8,128)S(1)}, f32[88,128]{1,0:T(8,128)S(1)}, u32[]{:S(2)}, u32[]{:S(2)}) %collective-permute-start.18) | collective-permute-done | bytes 45088 | tf_op jit(solution)/shard_map/ppermute | solution.py:162
  143.8 2.3 %collective-permute-start.20 = (f32[88,128]{1,0:T(8,128)S(1)}, f32[88,128]{1,0:T(8,128)S(1)}, u32[]{:S(2)}, u32[]{:S(2)}) collective-permute-start(f32[88,128]{1,0:T(8,128)S(1)} %get-tuple-element.59), channel_id=1, source_target_pairs={{0,8},{4,12},{8,0},{12,4},{1,9},{5,13},{9,1},{13,5},{2,10},{6,14},... | collective-permute-start | bytes 135176 | tf_op jit(solution)/shard_map/ppermute | solution.py:162
  148.3 1.9 %collective-permute-done.21 = f32[88,128]{1,0:T(8,128)S(1)} collective-permute-done((f32[88,128]{1,0:T(8,128)S(1)}, f32[88,128]{1,0:T(8,128)S(1)}, u32[]{:S(2)}, u32[]{:S(2)}) %collective-permute-start.21) | collective-permute-done | bytes 45088 | tf_op jit(solution)/shard_map/ppermute | solution.py:162
  150.3 2.8 %collective-permute-start.23 = (f32[4,88,128]{2,1,0:T(8,128)S(1)}, f32[4,88,128]{2,1,0:T(8,128)S(1)}, u32[]{:S(2)}, u32[]{:S(2)}) collective-permute-start(f32[4,88,128]{2,1,0:T(8,128)S(1)} %pad_maximum_fusion.1), channel_id=1, source_target_pairs={{0,32},{16,48},{32,0},{48,16},{1,33},{17,49},{33,1},{49,17},{2,34}... | collective-permute-start | bytes 540680 | tf_op jit(solution)/shard_map/ppermute | solution.py:162
  154.7 3.4 %collective-permute-done.23 = f32[4,88,128]{2,1,0:T(8,128)S(1)} collective-permute-done((f32[4,88,128]{2,1,0:T(8,128)S(1)}, f32[4,88,128]{2,1,0:T(8,128)S(1)}, u32[]{:S(2)}, u32[]{:S(2)}) %collective-permute-start.23) | collective-permute-done | bytes 180256 | tf_op jit(solution)/shard_map/ppermute | solution.py:162
  159.9 8.9 %collective-permute-start.25 = (f32[16,88,128]{2,1,0:T(8,128)S(1)}, f32[16,88,128]{2,1,0:T(8,128)S(1)}, u32[]{:S(2)}, u32[]{:S(2)}) collective-permute-start(f32[16,88,128]{2,1,0:T(8,128)S(1)} %constant_dynamic-update-slice_fusion.refs_1_), channel_id=1, source_target_pairs={{0,1},{1,0},{2,3},{3,2},{4,5},{5,4},{6,7},{7,6},{8,9},{9,8},{10,11... | collective-permute-start | bytes 2162696 | tf_op jit(solution)/shard_map/ppermute | solution.py:162
  172.3 4.2 %decoder_steps.1 = (f32[512,512]{1,0:T(8,128)}, f32[512,64]{1,0:T(8,128)}, f32[3,512]{1,0:T(4,128)}, f32[1,128]{1,0:T(1,128)}) custom-call(s32[2]{0:T(128)} %pad_add_fusion.place_ref.refs_0_, f32[16,88,128]{2,1,0:T(8,128)} %copy-done.3, f32[16,88,128]{2,1,0:T(8,128)} %copy-done.4, f32[512,512]{1,0:T(8,128)} %bitcast.236, f32[512,512]{1,0:T(8,128)} %bitcast.237, ...), custom_call_target="tpu_custom_call" | custom-call | tf_op jit(solution)/shard_map/decoder_steps/pallas_call | solution.py:270
  178.2 2.9 %fusion.24 = f32[32,32,128]{2,1,0:T(8,128)} fusion(f32[32,32,128]{2,1,0:T(8,128)S(1)} %copy-done.6, f32[32,32,128]{2,1,0:T(8,128)} %param.24, f32[]{:T(128)} %bitcast.251, f32[32,33,127]{2,1,0:T(8,128)S(1)} %slice.221, f32[32,33,1]{2,1,0:T(8,128)S(1)} %copy.81, f32[32,1,128]{2,1,0:T(1,128)S(1)} %slice_add_fusion.2), kind=kLoop, calls=%fused_computation.39 | loop fusion | flops 2228224 | bytes 2129924 | tf_op jit(solution)/shard_map/div | solution.py:154
  181.1 2.3 %fusion.45 = f32[32,8,32]{2,1,0:T(8,128)} fusion(f32[32,8,32]{2,1,0:T(8,128)S(1)} %copy-done.10, f32[32,8,32]{2,1,0:T(8,128)S(1)} %get-tuple-element.38, f32[32,8,32]{2,1,0:T(8,128)} %param.26, f32[]{:T(128)} %bitcast.252), kind=kLoop, calls=%fused_computation.71 | loop fusion | flops 98304 | bytes 131076 | tf_op jit(solution)/shard_map/div | solution.py:154
  (157 shorter events, 46.8 us)
Async XLA Ops:
  2.6 5.2 %collective-permute-start = (f32[32,1,160]{2,1,0:T(1,128)S(1)}, f32[32,1,160]{2,1,0:T(1,128)S(1)}, u32[]{:S(2)}, u32[]{:S(2)}) collective-permute-start(f32[32,1,160]{2,1,0:T(1,128)S(1)} %copy.69), channel_id=1, source_target_pairs={{16,0},{32,16},{48,32},{64,48},{80,64},{96,80},{112,96},{128,112},... | collective-permute-start | bytes 61448 | tf_op jit(solution)/shard_map/ppermute | solution.py:35
  6.5 20.0 %copy-start.8 = (f32[512,64]{0,1:T(8,128)S(1)}, f32[512,64]{0,1:T(8,128)}, u32[]{:S(2)}) copy-start(f32[512,64]{0,1:T(8,128)} %param.21) | copy-start | bytes 393220
  9.6 12.2 %collective-permute-start.1 = (f32[32,42,1]{1,0,2:T(8,128)S(1)}, f32[32,42,1]{1,0,2:T(8,128)S(1)}, u32[]{:S(2)}, u32[]{:S(2)}) collective-permute-start(f32[32,42,1]{1,0,2:T(8,128)S(1)} %pad_maximum_fusion.9), channel_id=1, source_target_pairs={{1,0},{2,1},{3,2},{4,3},{5,4},{6,5},{7,6},{8,7},{9,8},{10,9},{11,1... | collective-permute-start | bytes 16136 | tf_op jit(solution)/shard_map/ppermute | solution.py:35
  35.8 13.8 %copy-start.7 = (f32[3,3,32,128]{3,2,1,0:T(8,128)S(1)}, f32[3,3,32,128]{3,2,1,0:T(8,128)}, u32[]{:S(2)}) copy-start(f32[3,3,32,128]{3,2,1,0:T(8,128)} %param.18) | copy-start | bytes 442372
  39.0 10.6 %collective-permute-start.2 = (f32[3,1,128]{2,1,0:T(1,128)S(1)}, f32[3,1,128]{2,1,0:T(1,128)S(1)}, u32[]{:S(2)}, u32[]{:S(2)}) collective-permute-start(f32[3,1,128]{2,1,0:T(1,128)S(1)} %slice.208), channel_id=1, source_target_pairs={{16,0},{32,16},{48,32},{64,48},{80,64},{96,80},{112,96},{128,112},... | collective-permute-start | bytes 4616 | tf_op jit(solution)/shard_map/ppermute | solution.py:35
  40.3 9.3 %collective-permute-start.4 = (f32[3,32,1]{2,1,0:T(8,128)S(1)}, f32[3,32,1]{2,1,0:T(8,128)S(1)}, u32[]{:S(2)}, u32[]{:S(2)}) collective-permute-start(f32[3,32,1]{2,1,0:T(8,128)S(1)} %bitcast.239), channel_id=1, source_target_pairs={{1,0},{2,1},{3,2},{4,3},{5,4},{6,5},{7,6},{8,7},{9,8},{10,9},{11,1... | collective-permute-start | bytes 1160 | tf_op jit(solution)/shard_map/ppermute | solution.py:35
  49.6 17.2 %slice-start = ((s8[8388608]{0:T(1024)(128)(4,1)}), s8[4194304]{0:T(1024)(128)(4,1)S(1)}, s32[]{:S(2)}) async-start(s8[8388608]{0:T(1024)(128)(4,1)} %bitcast.254), calls=%async_computation | async-start | bytes 8388608
  49.8 7.1 %collective-permute-start.5 = (f32[3,32,1]{2,1,0:T(8,128)S(1)}, f32[3,32,1]{2,1,0:T(8,128)S(1)}, u32[]{:S(2)}, u32[]{:S(2)}) collective-permute-start(f32[3,32,1]{2,1,0:T(8,128)S(1)} %slice.213), channel_id=1, source_target_pairs={{0,1},{1,2},{2,3},{3,4},{4,5},{5,6},{6,7},{7,8},{8,9},{9,10},{10,1... | collective-permute-start | bytes 1160 | tf_op jit(solution)/shard_map/ppermute | solution.py:35
  52.7 4.7 %collective-permute-start.3 = (f32[3,1,128]{2,1,0:T(1,128)S(1)}, f32[3,1,128]{2,1,0:T(1,128)S(1)}, u32[]{:S(2)}, u32[]{:S(2)}) collective-permute-start(f32[3,1,128]{2,1,0:T(1,128)S(1)} %slice.209), channel_id=1, source_target_pairs={{0,16},{16,32},{32,48},{48,64},{64,80},{80,96},{96,112},{112,128},... | collective-permute-start | bytes 4616 | tf_op jit(solution)/shard_map/ppermute | solution.py:35
  77.2 16.9 %collective-permute-start.6 = (f32[32,42,1]{1,0,2:T(8,128)S(1)}, f32[32,42,1]{1,0,2:T(8,128)S(1)}, u32[]{:S(2)}, u32[]{:S(2)}) collective-permute-start(f32[32,42,1]{1,0,2:T(8,128)S(1)} %pad_maximum_fusion.10), channel_id=1, source_target_pairs={{0,1},{1,2},{2,3},{3,4},{4,5},{5,6},{6,7},{7,8},{8,9},{9,10},{10,1... | collective-permute-start | bytes 16136 | tf_op jit(solution)/shard_map/ppermute | solution.py:35
  93.3 6.7 %collective-permute-start.8 = (f32[16,80,128]{2,1,0:T(8,128)}, f32[16,80,128]{2,1,0:T(8,128)}, u32[]{:S(2)}, u32[]{:S(2)}) collective-permute-start(f32[16,80,128]{2,1,0:T(8,128)} %get-tuple-element.12), channel_id=1, source_target_pairs={{0,1},{1,0},{2,3},{3,2},{4,5},{5,4},{6,7},{7,6},{8,9},{9,8},{10,11... | collective-permute-start | bytes 1966088 | tf_op jit(solution)/shard_map/ppermute | solution.py:162
  95.0 4.9 %collective-permute-start.7 = (f32[32,1,160]{2,1,0:T(1,128)S(1)}, f32[32,1,160]{2,1,0:T(1,128)S(1)}, u32[]{:S(2)}, u32[]{:S(2)}) collective-permute-start(f32[32,1,160]{2,1,0:T(1,128)S(1)} %fusion.73), channel_id=1, source_target_pairs={{0,16},{16,32},{32,48},{48,64},{64,80},{80,96},{96,112},{112,128},... | collective-permute-start | bytes 61448 | tf_op jit(solution)/shard_map/ppermute | solution.py:35
  100.0 68.8 %copy-start.9 = (f32[512,64]{0,1:T(8,128)S(1)}, f32[512,64]{0,1:T(8,128)}, u32[]{:S(2)}) copy-start(f32[512,64]{0,1:T(8,128)} %param.28) | copy-start | bytes 393220
  101.3 9.5 %collective-permute-start.9 = (f32[4,80,128]{2,1,0:T(8,128)S(1)}, f32[4,80,128]{2,1,0:T(8,128)S(1)}, u32[]{:S(2)}, u32[]{:S(2)}) collective-permute-start(f32[4,80,128]{2,1,0:T(8,128)S(1)} %get-tuple-element.45), channel_id=1, source_target_pairs={{0,16},{16,0},{32,48},{48,32},{1,17},{17,1},{33,49},{49,33},{2,18}... | collective-permute-start | bytes 491528 | tf_op jit(solution)/shard_map/ppermute | solution.py:162
  103.3 13.4 %collective-permute-start.10 = (f32[4,80,128]{2,1,0:T(8,128)S(1)}, f32[4,80,128]{2,1,0:T(8,128)S(1)}, u32[]{:S(2)}, u32[]{:S(2)}) collective-permute-start(f32[4,80,128]{2,1,0:T(8,128)S(1)} %get-tuple-element.44), channel_id=1, source_target_pairs={{0,32},{16,48},{32,0},{48,16},{1,33},{17,49},{33,1},{49,17},{2,34}... | collective-permute-start | bytes 491528 | tf_op jit(solution)/shard_map/ppermute | solution.py:162
  110.7 9.2 %collective-permute-start.11 = (f32[4,80,128]{2,1,0:T(8,128)S(1)}, f32[4,80,128]{2,1,0:T(8,128)S(1)}, u32[]{:S(2)}, u32[]{:S(2)}) collective-permute-start(f32[4,80,128]{2,1,0:T(8,128)S(1)} %get-tuple-element.43), channel_id=1, source_target_pairs={{0,48},{16,32},{32,16},{48,0},{1,49},{17,33},{33,17},{49,1},{2,50}... | collective-permute-start | bytes 491528 | tf_op jit(solution)/shard_map/ppermute | solution.py:162
  119.9 6.8 %collective-permute-start.12 = (f32[80,128]{1,0:T(8,128)S(1)}, f32[80,128]{1,0:T(8,128)S(1)}, u32[]{:S(2)}, u32[]{:S(2)}) collective-permute-start(f32[80,128]{1,0:T(8,128)S(1)} %get-tuple-element.50), channel_id=1, source_target_pairs={{0,4},{4,0},{8,12},{12,8},{1,5},{5,1},{9,13},{13,9},{2,6},{6,2},{1... | collective-permute-start | bytes 122888 | tf_op jit(solution)/shard_map/ppermute | solution.py:162
  121.3 5.5 %collective-permute-start.13 = (f32[80,128]{1,0:T(8,128)S(1)}, f32[80,128]{1,0:T(8,128)S(1)}, u32[]{:S(2)}, u32[]{:S(2)}) collective-permute-start(f32[80,128]{1,0:T(8,128)S(1)} %get-tuple-element.49), channel_id=1, source_target_pairs={{0,8},{4,12},{8,0},{12,4},{1,9},{5,13},{9,1},{13,5},{2,10},{6,14},... | collective-permute-start | bytes 122888 | tf_op jit(solution)/shard_map/ppermute | solution.py:162
  123.0 4.1 %collective-permute-start.14 = (f32[80,128]{1,0:T(8,128)S(1)}, f32[80,128]{1,0:T(8,128)S(1)}, u32[]{:S(2)}, u32[]{:S(2)}) collective-permute-start(f32[80,128]{1,0:T(8,128)S(1)} %get-tuple-element.48), channel_id=1, source_target_pairs={{0,12},{4,8},{8,4},{12,0},{1,13},{5,9},{9,5},{13,1},{2,14},{6,10},... | collective-permute-start | bytes 122888 | tf_op jit(solution)/shard_map/ppermute | solution.py:162
  125.3 52.8 %copy-start.6 = (f32[32,32,128]{2,1,0:T(8,128)S(1)}, f32[32,32,128]{2,1,0:T(8,128)}, u32[]{:S(2)}) copy-start(f32[32,32,128]{2,1,0:T(8,128)} %param.25) | copy-start | bytes 1572868
  127.1 4.6 %collective-permute-start.16 = (f32[88,128]{1,0:T(8,128)S(1)}, f32[88,128]{1,0:T(8,128)S(1)}, u32[]{:S(2)}, u32[]{:S(2)}) collective-permute-start(f32[88,128]{1,0:T(8,128)S(1)} %concatenate.95), channel_id=1, source_target_pairs={{0,128},{64,192},{128,0},{192,64},{1,129},{65,193},{129,1},{193,65... | collective-permute-start | bytes 135176 | tf_op jit(solution)/shard_map/ppermute | solution.py:162
  129.9 4.9 %collective-permute-start.17 = (f32[88,128]{1,0:T(8,128)S(1)}, f32[88,128]{1,0:T(8,128)S(1)}, u32[]{:S(2)}, u32[]{:S(2)}) collective-permute-start(f32[88,128]{1,0:T(8,128)S(1)} %concatenate.95), channel_id=1, source_target_pairs={{0,192},{64,128},{128,64},{192,0},{1,193},{65,129},{129,65},{193,1... | collective-permute-start | bytes 135176 | tf_op jit(solution)/shard_map/ppermute | solution.py:162
  131.7 3.8 %collective-permute-start.15 = (f32[88,128]{1,0:T(8,128)S(1)}, f32[88,128]{1,0:T(8,128)S(1)}, u32[]{:S(2)}, u32[]{:S(2)}) collective-permute-start(f32[88,128]{1,0:T(8,128)S(1)} %concatenate.95), channel_id=1, source_target_pairs={{0,64},{64,0},{128,192},{192,128},{1,65},{65,1},{129,193},{193,129... | collective-permute-start | bytes 135176 | tf_op jit(solution)/shard_map/ppermute | solution.py:162
  135.5 6.9 %collective-permute-start.18 = (f32[88,128]{1,0:T(8,128)S(1)}, f32[88,128]{1,0:T(8,128)S(1)}, u32[]{:S(2)}, u32[]{:S(2)}) collective-permute-start(f32[88,128]{1,0:T(8,128)S(1)} %add_add_fusion), channel_id=1, source_target_pairs={{0,2},{2,0},{1,3},{3,1},{4,6},{6,4},{5,7},{7,5},{8,10},{10,8},{9,1... | collective-permute-start | bytes 135176 | tf_op jit(solution)/shard_map/ppermute | solution.py:162
  143.7 3.9 %collective-permute-start.19 = (f32[88,128]{1,0:T(8,128)S(1)}, f32[88,128]{1,0:T(8,128)S(1)}, u32[]{:S(2)}, u32[]{:S(2)}) collective-permute-start(f32[88,128]{1,0:T(8,128)S(1)} %get-tuple-element.59), channel_id=1, source_target_pairs={{0,4},{4,0},{8,12},{12,8},{1,5},{5,1},{9,13},{13,9},{2,6},{6,2},{1... | collective-permute-start | bytes 135176 | tf_op jit(solution)/shard_map/ppermute | solution.py:162
  143.8 4.5 %collective-permute-start.20 = (f32[88,128]{1,0:T(8,128)S(1)}, f32[88,128]{1,0:T(8,128)S(1)}, u32[]{:S(2)}, u32[]{:S(2)}) collective-permute-start(f32[88,128]{1,0:T(8,128)S(1)} %get-tuple-element.59), channel_id=1, source_target_pairs={{0,8},{4,12},{8,0},{12,4},{1,9},{5,13},{9,1},{13,5},{2,10},{6,14},... | collective-permute-start | bytes 135176 | tf_op jit(solution)/shard_map/ppermute | solution.py:162
  146.1 4.1 %collective-permute-start.21 = (f32[88,128]{1,0:T(8,128)S(1)}, f32[88,128]{1,0:T(8,128)S(1)}, u32[]{:S(2)}, u32[]{:S(2)}) collective-permute-start(f32[88,128]{1,0:T(8,128)S(1)} %get-tuple-element.59), channel_id=1, source_target_pairs={{0,12},{4,8},{8,4},{12,0},{1,13},{5,9},{9,5},{13,1},{2,14},{6,10},... | collective-permute-start | bytes 135176 | tf_op jit(solution)/shard_map/ppermute | solution.py:162
  150.2 4.4 %collective-permute-start.22 = (f32[4,88,128]{2,1,0:T(8,128)S(1)}, f32[4,88,128]{2,1,0:T(8,128)S(1)}, u32[]{:S(2)}, u32[]{:S(2)}) collective-permute-start(f32[4,88,128]{2,1,0:T(8,128)S(1)} %pad_maximum_fusion.1), channel_id=1, source_target_pairs={{0,16},{16,0},{32,48},{48,32},{1,17},{17,1},{33,49},{49,33},{2,18}... | collective-permute-start | bytes 540680 | tf_op jit(solution)/shard_map/ppermute | solution.py:162
  150.3 7.7 %collective-permute-start.23 = (f32[4,88,128]{2,1,0:T(8,128)S(1)}, f32[4,88,128]{2,1,0:T(8,128)S(1)}, u32[]{:S(2)}, u32[]{:S(2)}) collective-permute-start(f32[4,88,128]{2,1,0:T(8,128)S(1)} %pad_maximum_fusion.1), channel_id=1, source_target_pairs={{0,32},{16,48},{32,0},{48,16},{1,33},{17,49},{33,1},{49,17},{2,34}... | collective-permute-start | bytes 540680 | tf_op jit(solution)/shard_map/ppermute | solution.py:162
  153.1 6.7 %collective-permute-start.24 = (f32[4,88,128]{2,1,0:T(8,128)S(1)}, f32[4,88,128]{2,1,0:T(8,128)S(1)}, u32[]{:S(2)}, u32[]{:S(2)}) collective-permute-start(f32[4,88,128]{2,1,0:T(8,128)S(1)} %pad_maximum_fusion.1), channel_id=1, source_target_pairs={{0,48},{16,32},{32,16},{48,0},{1,49},{17,33},{33,17},{49,1},{2,50}... | collective-permute-start | bytes 540680 | tf_op jit(solution)/shard_map/ppermute | solution.py:162
  159.9 11.5 %copy-start.3 = (f32[16,88,128]{2,1,0:T(8,128)}, f32[16,88,128]{2,1,0:T(8,128)S(1)}, u32[]{:S(2)}) copy-start(f32[16,88,128]{2,1,0:T(8,128)S(1)} %constant_dynamic-update-slice_fusion.refs_1_) | copy-start | bytes 2162692
  159.9 11.5 %collective-permute-start.25 = (f32[16,88,128]{2,1,0:T(8,128)S(1)}, f32[16,88,128]{2,1,0:T(8,128)S(1)}, u32[]{:S(2)}, u32[]{:S(2)}) collective-permute-start(f32[16,88,128]{2,1,0:T(8,128)S(1)} %constant_dynamic-update-slice_fusion.refs_1_), channel_id=1, source_target_pairs={{0,1},{1,0},{2,3},{3,2},{4,5},{5,4},{6,7},{7,6},{8,9},{9,8},{10,11... | collective-permute-start | bytes 2162696 | tf_op jit(solution)/shard_map/ppermute | solution.py:162
  (9 other events, 51.8 us)

commit v2 on v0

v2 whole, which is shorter than its diff:
```python
import jax
import jax.numpy as jnp
from jax import lax
from jax.experimental import pallas as pl
from jax.experimental.pallas import tpu as pltpu
from jax.sharding import Mesh
from jax.sharding import PartitionSpec as P

SUB = 4
RATIO = 4
ADAM_STEP = 10

BETA_ONE = 0.9
BETA_TWO = 0.99
ADAM_EPSILON = 1e-08
CLIP_RMS = 0.01
LOSS_VALUE = 0.25
MEAN_EPSILON = 1e-06

ROW = ("zl", "x")
COL = ("y", "zh", "c")
SR = 32
SC = 128
CH = 32
CR = 8
CC = 32
HID = 512
STEPS = 4
CHAINS = 2
BLOCK = SR * SC // STEPS
WIDTH = BLOCK // CHAINS
LINES = SR // STEPS
BANDS = CR // STEPS
F32 = jnp.float32
BF16 = jnp.bfloat16
MIB = 1 << 20


def axes_size(axes):
    total = 1
    for axis in axes:
        total *= lax.axis_size(axis)
    return total


def axes_index(axes):
    index = 0
    for axis in axes:
        index = index * lax.axis_size(axis) + lax.axis_index(axis)
    return index


def shifted(block, down, right):
    rows, cols = axes_size(ROW), axes_size(COL)
    if not right:
        return lax.ppermute(block, ROW, [(i, (i + down) % rows) for i in range(rows)])
    if not down:
        return lax.ppermute(block, COL, [(i, (i + right) % cols) for i in range(cols)])
    route = [
        (r * cols + c, (r + down) % rows * cols + (c + right) % cols)
        for r in range(rows)
        for c in range(cols)
    ]
    return lax.ppermute(block, ROW + COL, route)


def at_ends():
    row, col = axes_index(ROW), axes_index(COL)
    return row == 0, row == axes_size(ROW) - 1, col == 0, col == axes_size(COL) - 1


def swapped(block, axis, mask):
    size = lax.axis_size(axis)
    return lax.ppermute(block, axis, [(i, i ^ mask) for i in range(size)])


def pair_sum(values):
    values = list(values)
    while len(values) > 1:
        values = [values[i] + values[i + 1] for i in range(0, len(values), 2)]
    return values[0]


def exchange_sum(block, axis):
    return pair_sum([block] + [swapped(block, axis, d) for d in range(1, lax.axis_size(axis))])


def exchange_gather(block, axis):
    return [block] + [swapped(block, axis, d) for d in range(1, lax.axis_size(axis))]


def scatter_sum(blocks, axis):
    return pair_sum([blocks[0]] + [swapped(blocks[d], axis, d) for d in range(1, len(blocks))])


def vmem():
    return pl.BlockSpec(memory_space=pltpu.VMEM)


def smem():
    return pl.BlockSpec(memory_space=pltpu.SMEM)


def hbm():
    return pl.BlockSpec(memory_space=pltpu.HBM)


def in_hbm(array):
    return pltpu.with_memory_space_constraint(array, pltpu.HBM)


def whole(shape, memory_space=pltpu.VMEM):
    return pl.BlockSpec(shape, lambda b: (0,) * len(shape), memory_space=memory_space)


def lane_ids(rows):
    return lax.broadcasted_iota(jnp.int32, (rows, SC), 1)


def spread_lane(block, lane):
    return jnp.broadcast_to(block[:, lane : lane + 1], (block.shape[0], SC))


def dot(former, latter, former_dim=1, latter_dim=0, precision=None):
    return lax.dot_general(
        former,
        latter,
        (((former_dim,), (latter_dim,)), ((), ())),
        precision=precision,
        preferred_element_type=F32,
    )


def sigmoid(value):
    return 0.5 * jnp.tanh(0.5 * value) + 0.5


def coarse_table(shift_x):
    line = lax.broadcasted_iota(jnp.int32, (SC, SC), 0)
    sample = lax.broadcasted_iota(jnp.int32, (SC, SC), 1)
    base = sample >> 2
    fraction = ((sample & 3).astype(F32) + shift_x) * (1.0 / RATIO)
    return jnp.where(line == base, 1.0 - fraction, 0.0) + jnp.where(line == base + 1, fraction, 0.0)


def edges_kernel(fine_hbm, coarse_hbm, row_ref, col_ref, fine_ref, coarse_ref, fine, coarse, sems):
    copies = [
        pltpu.make_async_copy(fine_hbm, fine, sems.at[0]),
        pltpu.make_async_copy(coarse_hbm, coarse, sems.at[1]),
    ]
    for copy in copies:
        copy.start()
    for copy in copies:
        copy.wait()
    lane = lane_ids(CH)
    row_ref[:, 0:SC] = fine[:, 0, :]
    row_ref[:, SC:] = jnp.zeros((CH, SC), F32)
    row_ref[:, SC : SC + CC] = coarse[:, 0, :]
    coarse_ref[...] = jnp.zeros(coarse_ref.shape, F32)
    cols = jnp.zeros((CH, SC), F32)
    for i in range(SR):
        line = fine[:, i, :]
        fine_ref[i] = line
        cols = jnp.where(lane == i, spread_lane(line, 0), cols)
    for i in range(CR):
        line = coarse[:, i, :]
        coarse_ref[i, :, 0:CC] = line
        cols = jnp.where(lane == SR + i, spread_lane(line, 0), cols)
    col_ref[...] = cols


def edges(fine, coarse):
    shapes = ((CH, 2 * SC), (CH, SC), (SR, CH, SC), (CR, CH, SC))
    return pl.pallas_call(
        edges_kernel,
        out_shape=tuple(jax.ShapeDtypeStruct(d, F32) for d in shapes),
        in_specs=[hbm(), hbm()],
        out_specs=(vmem(),) * 4,
        scratch_shapes=[
            pltpu.VMEM(fine.shape, F32),
            pltpu.VMEM(coarse.shape, F32),
            pltpu.SemaphoreType.DMA((2,)),
        ],
        compiler_params=pltpu.CompilerParams(vmem_limit_bytes=8 * MIB),
        name="edges",
    )(in_hbm(fine), in_hbm(coarse))


def prepare_kernel(
    offset_ref,
    in_hbm,
    mid_hbm,
    out_hbm,
    target_hbm,
    shift_ref,
    in_ref,
    in_turned_ref,
    mid_ref,
    mid_turned_ref,
    out_ref,
    out_turned_ref,
    target_ref,
    ends_ref,
    w_in,
    w_mid,
    w_out,
    targets,
    sems,
):
    copies = [
        pltpu.make_async_copy(source, target, sems.at[i])
        for i, (source, target) in enumerate(
            ((in_hbm, w_in), (out_hbm, w_out), (target_hbm, targets), (mid_hbm, w_mid))
        )
    ]
    for copy in copies:
        copy.start()
    shift_ref[...] = jnp.zeros((8, SC), F32)
    for i in range(2):
        shift = offset_ref[0, 0, i].astype(F32) * (1.0 / SUB)
        shift_ref[i : i + 1, :] = jnp.full((1, SC), shift, F32)
    copies[0].wait()
    in_turned_ref[...] = w_in[...].astype(BF16)
    for block in range(4):
        cols = slice(block * 128, block * 128 + 128)
        in_ref[cols, :] = w_in[:, cols].T.astype(BF16)
    copies[1].wait()
    padded = jnp.concatenate([w_out[...], jnp.zeros((13, HID), F32)], axis=0)
    out_ref[...] = padded.astype(BF16)
    for block in range(4):
        cols = slice(block * 128, block * 128 + 128)
        out_turned_ref[cols, :] = padded[:, cols].T.astype(BF16)
    copies[2].wait()
    lane = lane_ids(3)
    ends = jnp.zeros((3, SC), F32)
    target_ref[...] = jnp.zeros(target_ref.shape, F32)
    for i in range(SR):
        for kind in range(3):
            line = targets[kind, :, i, :]
            target_ref[kind, 0:3, i * SC : i * SC + SC] = line
        ends = jnp.where(lane == i, spread_lane(line, SC - 1), ends)
    ends_ref[...] = jnp.zeros((8, SC), F32)
    ends_ref[0:3, :] = ends
    copies[3].wait()
    mid_ref[...] = w_mid[...].astype(BF16)
    for i in range(4):
        for j in range(4):
            rows = slice(i * 128, i * 128 + 128)
            cols = slice(j * 128, j * 128 + 128)
            mid_turned_ref[cols, rows] = w_mid[rows, cols].T.astype(BF16)


def prepare(offsets, w_in, w_mid, w_out, targets):
    outs = (
        jax.ShapeDtypeStruct((8, SC), F32),
        jax.ShapeDtypeStruct((HID, 2 * CH), BF16),
        jax.ShapeDtypeStruct((2 * CH, HID), BF16),
        jax.ShapeDtypeStruct((HID, HID), BF16),
        jax.ShapeDtypeStruct((HID, HID), BF16),
        jax.ShapeDtypeStruct((16, HID), BF16),
        jax.ShapeDtypeStruct((HID, 16), BF16),
        jax.ShapeDtypeStruct((3, 8, SR * SC), F32),
        jax.ShapeDtypeStruct((8, SC), F32),
    )
    return pl.pallas_call(
        prepare_kernel,
        out_shape=outs,
        in_specs=[smem(), hbm(), hbm(), hbm(), hbm()],
        out_specs=(vmem(),) * len(outs),
        scratch_shapes=[pltpu.VMEM(a.shape, F32) for a in (w_in, w_mid, w_out, targets)]
        + [pltpu.SemaphoreType.DMA((4,))],
        compiler_params=pltpu.CompilerParams(vmem_limit_bytes=8 * MIB),
        name="prepare",
    )(offsets, *(in_hbm(a) for a in (w_in, w_mid, w_out, targets)))


def forward_kernel(
    shift_ref,
    fine_ref,
    coarse_ref,
    row_ref,
    col_ref,
    corner_ref,
    target_ref,
    ends_ref,
    in_ref,
    mid_ref,
    out_ref,
    feat_ref,
    pre_ref,
    pred_ref,
    up_ref,
    left_ref,
    down_ref,
    right_ref,
    lines,
    bands,
):
    step = pl.program_id(0)
    shift_y = shift_ref[0:1, :]
    shift_x = shift_ref[1:2, :]

    @pl.when(step == 0)
    def _():
        lane = lane_ids(CH)
        unused_first_row, last_row, unused_first_col, last_col = at_ends()
        row_in = jnp.where(last_row, 0.0, row_ref[...])
        col_in = jnp.where(last_col, 0.0, col_ref[...])
        corner_in = jnp.where(jnp.logical_or(last_row, last_col), 0.0, corner_ref[...])

        def across(line, following):
            moved = jnp.where(lane == SC - 1, following, pltpu.roll(line, SC - 1, 1))
            return line * (1.0 - shift_x) + moved * shift_x

        stage = []
        for i in range(CR):
            stage.append(jnp.where(lane == CC, spread_lane(col_in, SR + i), coarse_ref[i]))
        stage.append(jnp.where(lane == CC, spread_lane(corner_in, SR), row_in[:, SC:]))
        bands[...] = dot(
            jnp.concatenate(stage, axis=0), coarse_table(shift_x), precision=lax.Precision.HIGHEST
        ).reshape(CR + 1, CH, SC)
        for i in range(SR):
            lines[i] = across(fine_ref[i], spread_lane(col_in, i))
        lines[SR] = across(row_in[:, 0:SC], spread_lane(corner_in, 0))
        left_ref[...] = jnp.zeros(left_ref.shape, F32)
        right_ref[...] = ends_ref[...]

    tiles = []
    for k in range(LINES):
        row = step * LINES + k
        band = step * BANDS + k // RATIO
        fine = lines[row] * (1.0 - shift_y) + lines[row + 1] * shift_y
        part = (k % RATIO + shift_y) * (1.0 / RATIO)
        coarse = bands[band] * (1.0 - part) + bands[band + 1] * part
        tiles.append(jnp.concatenate([fine, coarse], axis=0).astype(BF16))
    feat = jnp.concatenate(tiles, axis=1)
    feat_ref[...] = feat
    preds = []
    for chain in range(CHAINS):
        cols = slice(chain * WIDTH, chain * WIDTH + WIDTH)
        pre = dot(in_ref[...], feat[:, cols])
        act = (pre * sigmoid(pre)).astype(BF16)
        pre = dot(mid_ref[...], act)
        pre_ref[:, cols] = pre
        act = (pre * sigmoid(pre)).astype(BF16)
        preds.append(dot(out_ref[...], act)[0:8])
    pred = jnp.concatenate(preds, axis=1)
    pred_ref[...] = pred
    lane = lane_ids(8)
    left = left_ref[...]
    right = right_ref[...]
    for k in range(LINES):
        row = step * LINES + k
        tile = pred[:, k * SC : k * SC + SC]
        left = jnp.where(lane == row, spread_lane(tile, 0), left)
        right = right + jnp.where(lane == row, spread_lane(tile, SC - 1), 0.0)
    left_ref[...] = left
    right_ref[...] = right

    @pl.when(step == 0)
    def _():
        up_ref[...] = pred[:, 0:SC]

    @pl.when(step == STEPS - 1)
    def _():
        down_ref[...] = pred[:, BLOCK - SC :] + target_ref[1, :, SR * SC - SC :]


def forward(*args):
    edge = jax.ShapeDtypeStruct((8, SC), F32)
    return pl.pallas_call(
        forward_kernel,
        grid=(STEPS,),
        out_shape=(
            jax.ShapeDtypeStruct((2 * CH, SR * SC), BF16),
            jax.ShapeDtypeStruct((HID, SR * SC), F32),
            jax.ShapeDtypeStruct((8, SR * SC), F32),
            edge,
            edge,
            edge,
            edge,
        ),
        in_specs=[whole(a.shape) for a in args],
        out_specs=(
            pl.BlockSpec((2 * CH, BLOCK), lambda b: (0, b)),
            pl.BlockSpec((HID, BLOCK), lambda b: (0, b)),
            pl.BlockSpec((8, BLOCK), lambda b: (0, b)),
            whole((8, SC)),
            whole((8, SC)),
            whole((8, SC)),
            whole((8, SC)),
        ),
        scratch_shapes=[
            pltpu.VMEM((SR + 1, CH, SC), F32),
            pltpu.VMEM((CR + 1, CH, SC), F32),
        ],
        compiler_params=pltpu.CompilerParams(vmem_limit_bytes=24 * MIB),
        name="forward",
    )(*args)


def loss_cotangent(pred_ref, target_ref, below, beside, above, before, cot):
    first_row, last_row, first_col, last_col = at_ends()
    lane = lane_ids(3)
    cot[...] = jnp.zeros(cot.shape, F32)
    line = pred_ref[0:3, 0:SC]
    row_prior = jnp.where(first_row, 0.0, line - above[0:3, :])
    for i in range(SR):
        if i + 1 < SR:
            following = pred_ref[0:3, (i + 1) * SC : (i + 2) * SC]
        else:
            following = below[0:3, :]
        value_error = line - target_ref[0, 0:3, i * SC : i * SC + SC]
        row_error = following - line - target_ref[1, 0:3, i * SC : i * SC + SC]
        if i + 1 == SR:
            row_error = jnp.where(last_row, 0.0, row_error)
        beyond = jnp.where(lane == SC - 1, spread_lane(beside[0:3, :], i), pltpu.roll(line, SC - 1, 1))
        col_error = beyond - line - target_ref[2, 0:3, i * SC : i * SC + SC]
        col_error = jnp.where(jnp.logical_and(lane == SC - 1, last_col), 0.0, col_error)
        edge = jnp.where(first_col, 0.0, line - spread_lane(before[0:3, :], i))
        col_prior = jnp.where(lane == 0, edge, pltpu.roll(col_error, 1, 1))
        cot[0:3, i * SC : (i + 1) * SC] = (
            2.0 * LOSS_VALUE * value_error
            + 2.0 * (row_prior - row_error)
            + 2.0 * (col_prior - col_error)
        )
        line = following
        row_prior = row_error


def backward_kernel(
    shift_ref,
    feat_ref,
    pre_ref,
    pred_ref,
    below_ref,
    beside_ref,
    above_ref,
    before_ref,
    target_ref,
    in_ref,
    in_turned_ref,
    mid_turned_ref,
    out_turned_ref,
    keep_ref,
    send_ref,
    fine_ref,
    coarse_ref,
    row_ref,
    col_ref,
    corner_ref,
    cot,
    grad_mid,
    grad_in,
    grad_out,
    last_line,
    bands,
):
    step = pl.program_id(0)
    shift_y = shift_ref[0:1, :]
    shift_x = shift_ref[1:2, :]
    lane = lane_ids(CH)

    @pl.when(step == 0)
    def _():
        loss_cotangent(pred_ref, target_ref, below_ref, beside_ref, above_ref, before_ref, cot)
        grad_mid[...] = jnp.zeros(grad_mid.shape, F32)
        grad_in[...] = jnp.zeros(grad_in.shape, F32)
        grad_out[...] = jnp.zeros(grad_out.shape, F32)
        last_line[...] = jnp.zeros(last_line.shape, F32)
        bands[0] = jnp.zeros((CH, SC), F32)
        col_ref[...] = jnp.zeros((CH, SC), F32)

    feat_grads = []
    for chain in range(CHAINS):
        cols = slice(chain * WIDTH, chain * WIDTH + WIDTH)
        feat = feat_ref[:, cols]
        samples = pl.ds(pl.multiple_of(step * BLOCK + chain * WIDTH, WIDTH), WIDTH)
        out_cot = cot[:, samples].astype(BF16)
        pre = pre_ref[:, cols]
        gate = sigmoid(pre)
        act = (pre * gate).astype(BF16)
        grad_out[...] += dot(out_cot, act, 1, 1)
        upward = dot(out_turned_ref[...], out_cot)
        delta = (upward * (gate * (1.0 + pre * (1.0 - gate)))).astype(BF16)
        pre = dot(in_ref[...], feat)
        gate = sigmoid(pre)
        act = (pre * gate).astype(BF16)
        grad_mid[...] += dot(delta, act, 1, 1)
        upward = dot(mid_turned_ref[...], delta)
        delta = (upward * (gate * (1.0 + pre * (1.0 - gate)))).astype(BF16)
        grad_in[...] += dot(feat, delta, 1, 1)
        feat_grads.append(dot(in_turned_ref[...], delta))
    feat_grad = jnp.concatenate(feat_grads, axis=1)

    def along(line):
        moved = jnp.where(lane == 0, 0.0, pltpu.roll(line, 1, 1))
        return line * (1.0 - shift_x) + moved * shift_x

    prior = last_line[...]
    cols = col_ref[...]
    upper = bands[step * BANDS]
    lower = jnp.zeros((CH, SC), F32)
    for k in range(LINES):
        row = step * LINES + k
        fine = feat_grad[0:CH, k * SC : k * SC + SC]
        line = fine * (1.0 - shift_y) + prior * shift_y
        fine_ref[row] = along(line)
        cols = jnp.where(lane == row, spread_lane(line * shift_x, SC - 1), cols)
        prior = fine
        coarse = feat_grad[CH:, k * SC : k * SC + SC]
        part = (k % RATIO + shift_y) * (1.0 / RATIO)
        upper += coarse * (1.0 - part)
        lower += coarse * part
        if k % RATIO == RATIO - 1:
            bands[step * BANDS + k // RATIO] = upper
            upper = lower
            lower = jnp.zeros((CH, SC), F32)
    bands[step * BANDS + BANDS] = upper
    last_line[...] = prior
    col_ref[...] = cols

    @pl.when(step == STEPS - 1)
    def _():
        line = prior * shift_y
        row_ref[:, 0:SC] = along(line)
        corner = jnp.where(lane == 0, spread_lane(line * shift_x, SC - 1), 0.0)
        spread = dot(
            bands[...].reshape((CR + 1) * CH, SC),
            coarse_table(shift_x),
            1,
            1,
            precision=lax.Precision.HIGHEST,
        )
        ends = cols
        for i in range(CR):
            band = spread[i * CH : i * CH + CH]
            coarse_ref[i] = jnp.where(lane < CC, band, 0.0)
            ends = jnp.where(lane == SR + i, spread_lane(band, CC), ends)
        col_ref[...] = ends
        band = spread[CR * CH :]
        row_ref[:, SC:] = jnp.where(lane < CC, band, 0.0)
        corner_ref[...] = jnp.where(lane == SR, spread_lane(band, CC), corner)
        core = lax.axis_index("c")
        tile = axes_index(("x", "y"))
        for d in range(16):
            chunk = tile ^ d
            band = chunk >> 1
            side = chunk & 1
            for half, target in ((core, keep_ref), (1 - core, send_ref)):
                cols_at = pl.ds(pl.multiple_of((half * 2 + side) * 128, 128), 128)
                target[d, 0:64, :] = grad_mid[pl.ds(pl.multiple_of(band * 64, 64), 64), cols_at]
                target[d, 64:72, :] = grad_in[pl.ds(pl.multiple_of(band * 8, 8), 8), cols_at]
                target[d, 72:80, :] = jnp.where(band == 0, grad_out[0:8, cols_at], 0.0)


def backward(shifts, feat, pre, pred, *consts):
    part = jax.ShapeDtypeStruct((16, 80, 128), F32)
    consts = (pred, *consts)
    outs = (
        part,
        part,
        jax.ShapeDtypeStruct((SR, CH, SC), F32),
        jax.ShapeDtypeStruct((CR, CH, SC), F32),
        jax.ShapeDtypeStruct((CH, 2 * SC), F32),
        jax.ShapeDtypeStruct((CH, SC), F32),
        jax.ShapeDtypeStruct((CH, SC), F32),
    )
    return pl.pallas_call(
        backward_kernel,
        grid=(STEPS,),
        out_shape=outs,
        in_specs=[
            whole((8, SC)),
            pl.BlockSpec((2 * CH, BLOCK), lambda b: (0, b)),
            pl.BlockSpec((HID, BLOCK), lambda b: (0, b)),
        ]
        + [whole(a.shape) for a in consts],
        out_specs=tuple(whole(o.shape) for o in outs),
        scratch_shapes=[
            pltpu.VMEM((16, SR * SC), F32),
            pltpu.VMEM((HID, HID), F32),
            pltpu.VMEM((2 * CH, HID), F32),
            pltpu.VMEM((16, HID), F32),
            pltpu.VMEM((CH, SC), F32),
            pltpu.VMEM((CR + 1, CH, SC), F32),
        ],
        compiler_params=pltpu.CompilerParams(vmem_limit_bytes=32 * MIB),
        name="backward",
    )(shifts, feat, pre, *consts)


def join_kernel(fine_ref, coarse_ref, row_ref, col_ref, corner_ref, fine_out, coarse_out, total_ref):
    lane = lane_ids(CH)
    first_row, unused_last_row, first_col, unused_last_col = at_ends()
    rows = jnp.where(first_row, 0.0, row_ref[...])
    cols = jnp.where(first_col, 0.0, col_ref[...])
    corner = jnp.where(jnp.logical_or(first_row, first_col), 0.0, corner_ref[...])
    total = jnp.zeros((CH, SC), F32)
    for i in range(SR):
        line = fine_ref[i] + jnp.where(lane == 0, spread_lane(cols, i), 0.0)
        if i == 0:
            line += rows[:, 0:SC]
            line += jnp.where(lane == 0, spread_lane(corner, 0), 0.0)
        fine_out[:, i, :] = line
        total += line * line
    for i in range(CR):
        line = coarse_ref[i] + jnp.where(lane == 0, spread_lane(cols, SR + i), 0.0)
        if i == 0:
            line += rows[:, SC:]
            line += jnp.where(lane == 0, spread_lane(corner, SR), 0.0)
        coarse_out[:, i, :] = line[:, 0:CC]
        total += line * line
    total = jnp.sum(jnp.sum(total, axis=0, keepdims=True), axis=1, keepdims=True)
    total_ref[...] = jnp.broadcast_to(total, (8, SC))


def join(fine, coarse, row_in, col_in, corner_in):
    return pl.pallas_call(
        join_kernel,
        out_shape=(
            jax.ShapeDtypeStruct((CH, SR, SC), F32),
            jax.ShapeDtypeStruct((CH, CR, CC), F32),
            jax.ShapeDtypeStruct((8, SC), F32),
        ),
        in_specs=[vmem()] * 5,
        out_specs=(vmem(),) * 3,
        compiler_params=pltpu.CompilerParams(vmem_limit_bytes=8 * MIB),
        name="join",
    )(fine, coarse, row_in, col_in, corner_in)


def clip_factor(total, entries):
    return jnp.minimum(1.0, CLIP_RMS / jnp.sqrt(total / entries + MEAN_EPSILON))


def adam_step(gradient, moment_one, moment_two, clip_scale):
    clipped = gradient * clip_scale
    new_one = BETA_ONE * moment_one + (1.0 - BETA_ONE) * clipped
    new_two = BETA_TWO * moment_two + (1.0 - BETA_TWO) * clipped * clipped
    return (
        new_one
        * (1.0 / (1.0 - BETA_ONE**ADAM_STEP))
        / (jnp.sqrt(new_two * (1.0 / (1.0 - BETA_TWO**ADAM_STEP))) + ADAM_EPSILON)
    )


def steps_kernel(
    own_ref,
    other_ref,
    fine_ref,
    coarse_ref,
    mid_one_ref,
    mid_two_ref,
    in_one_ref,
    in_two_ref,
    out_one_ref,
    out_two_ref,
    fine_one_ref,
    fine_two_ref,
    coarse_one_ref,
    coarse_two_ref,
    mid_ref,
    in_ref,
    out_ref,
    fine_step_ref,
    coarse_step_ref,
    scales,
    *,
    decoder_entries,
    grid_entries,
):
    core = lax.axis_index("c")
    tile = axes_index(("x", "y"))
    band = pl.program_id(0)

    @pl.when(band == 0)
    def _():
        own_sum = pair_sum([own_ref[d, 80:88, :] for d in range(16)])
        other_sum = pair_sum([other_ref[d, 80:88, :] for d in range(16)])
        totals = own_sum + other_sum
        scales[0:1, :] = clip_factor(totals[0:1, :], grid_entries)
        scales[1:2, :] = clip_factor(totals[1:2, :], decoder_entries)

    grid_scale = scales[0:1, :]
    scale = scales[1:2, :]
    for block in range(4):
        half = block // 2
        d = tile ^ (band * 2 + block % 2)
        data = jnp.where(half == core, own_ref[d, 0:80, :], other_ref[d, 0:80, :])
        cols = slice(block * 128, block * 128 + 128)
        mid_ref[:, cols] = adam_step(data[0:64], mid_one_ref[:, cols], mid_two_ref[:, cols], scale)
        in_ref[:, cols] = adam_step(data[64:72], in_one_ref[:, cols], in_two_ref[:, cols], scale)

        @pl.when(band == 0)
        def _():
            out_ref[:, cols] = adam_step(
                data[72:75], out_one_ref[:, cols], out_two_ref[:, cols], scale
            )

    fine_step_ref[...] = adam_step(
        fine_ref[...], fine_one_ref[...], fine_two_ref[...], grid_scale[:, None, :]
    )
    coarse_step_ref[...] = adam_step(
        coarse_ref[...], coarse_one_ref[...], coarse_two_ref[...], grid_scale[:, None, 0:CC]
    )


def all_steps(own, other, fine, coarse, moments, decoder_entries, grid_entries):
    mid = pl.BlockSpec((64, 512), lambda b: (b, 0))
    inner = pl.BlockSpec((8, 512), lambda b: (b, 0))
    outer = whole((3, 512))
    fine_spec = pl.BlockSpec((CH // 8, SR, SC), lambda b: (b, 0, 0))
    coarse_spec = pl.BlockSpec((CH // 8, CR, CC), lambda b: (b, 0, 0))
    shapes = ((512, 512), (64, 512), (3, 512), fine.shape, coarse.shape)
    return pl.pallas_call(
        lambda *refs: steps_kernel(
            *refs, decoder_entries=decoder_entries, grid_entries=grid_entries
        ),
        grid=(8,),
        out_shape=tuple(jax.ShapeDtypeStruct(s, F32) for s in shapes),
        in_specs=[whole(own.shape), whole(other.shape), fine_spec, coarse_spec]
        + [mid, mid, inner, inner, outer, outer, fine_spec, fine_spec, coarse_spec, coarse_spec],
        out_specs=(mid, inner, outer, fine_spec, coarse_spec),
        scratch_shapes=[pltpu.VMEM((8, SC), F32)],
        compiler_params=pltpu.CompilerParams(vmem_limit_bytes=16 * MIB),
        name="steps",
    )(own, other, fine, coarse, *moments)


def reduce_grads(keep, send, grid_local):
    part = keep + swapped(send, "c", 1)
    part = scatter_sum([part[d * 4 : d * 4 + 4] for d in range(4)], "x")
    part = scatter_sum([part[d] for d in range(4)], "y")
    part = exchange_sum(jnp.concatenate([part, grid_local]), "zl")
    part = exchange_sum(part, "zh")
    squares = jnp.sum(part[:80] * part[:80])
    tail = jnp.where(jnp.arange(8)[:, None] == 1, squares, part[80:])
    part = jnp.concatenate([part[:80], tail])
    own = jnp.stack(exchange_gather(part, "y"))
    own = jnp.concatenate(exchange_gather(own, "x"))
    return own, swapped(own, "c", 1)


def local_grads(offsets, targets, grid_fine, grid_coarse, weight_in, weight_mid, weight_out):
    row_out, col_out, fine_lines, coarse_lines = edges(grid_fine, grid_coarse)
    row_in = shifted(row_out, -1, 0)
    col_in = shifted(col_out, 0, -1)
    corner_in = shifted(col_out, -1, -1)
    shifts, low_in, in_turned, low_mid, mid_turned, low_out, out_turned, lines, ends = prepare(
        offsets, weight_in.T, weight_mid[0], weight_out, targets
    )
    feat, pre, pred, up, left, down, right = forward(
        shifts, fine_lines, coarse_lines, row_in, col_in, corner_in, lines, ends, low_in, low_mid, low_out
    )
    halos = (shifted(up, -1, 0), shifted(left, 0, -1), shifted(down, 1, 0), shifted(right, 0, 1))
    keep, send, fine, coarse, row_out, col_out, corner_out = backward(
        shifts, feat, pre, pred, *halos, lines, low_in, in_turned, mid_turned, out_turned
    )
    row_in = shifted(row_out, 1, 0)
    col_in = shifted(col_out, 0, 1)
    corner_in = shifted(corner_out, 1, 1)
    return (keep, send, *join(fine, coarse, row_in, col_in, corner_in))


def shards(
    offsets,
    targets,
    grid_fine,
    grid_coarse,
    weight_in,
    weight_mid,
    weight_out,
    fine_first,
    fine_second,
    coarse_first,
    coarse_second,
    in_first,
    in_second,
    mid_first,
    mid_second,
    out_first,
    out_second,
):
    keep, send, fine_grad, coarse_grad, grid_local = local_grads(
        offsets, targets, grid_fine, grid_coarse, weight_in, weight_mid, weight_out
    )
    devices = axes_size(ROW) * axes_size(COL)
    grid_entries = (fine_grad.size + coarse_grad.size) * devices
    decoder_entries = weight_in.size + weight_mid.size + weight_out.size
    own, other = reduce_grads(keep, send, grid_local)
    middle_step, input_step, output_step, fine_step, coarse_step = all_steps(
        own,
        other,
        fine_grad,
        coarse_grad,
        (
            mid_first[0],
            mid_second[0],
            in_first.T,
            in_second.T,
            out_first,
            out_second,
            fine_first,
            fine_second,
            coarse_first,
            coarse_second,
        ),
        decoder_entries,
        grid_entries,
    )
    return (fine_step, coarse_step, input_step.T, middle_step[None], output_step)


def solution(mesh):
    sizes = {"zl": 4, "x": 4, "y": 4, "zh": 2, "c": 2}
    mesh = Mesh(mesh.devices.reshape(tuple(sizes.values())), tuple(sizes))
    placed = (
        P(ROW, COL, None),
        P(None, None, ROW, COL),
        P(None, ROW, COL),
        P(None, ROW, COL),
        P(),
        P(),
        P(),
        P(None, ROW, COL),
        P(None, ROW, COL),
        P(None, ROW, COL),
        P(None, ROW, COL),
        P(),
        P(),
        P(),
        P(),
        P(),
        P(),
    )
    return jax.shard_map(
        shards,
        mesh=mesh,
        in_specs=placed,
        out_specs=(P(None, ROW, COL), P(None, ROW, COL), P(), P(), P()),
        check_vma=False,
    )
```

time: 382 us -> 144 us (0.38)
  waiting for transfers between devices: 187 us -> 44 us
  blocking collectives: 80.8 us -> 0 us
  starting transfers between devices: 30.3 us -> 65.4 us
  matrix products: 31.7 us -> 0 us
  Pallas kernels: 0 us -> 30.9 us
  between operations: 19.8 us -> 1.11 us
  other arithmetic: 17.6 us -> 1.53 us
  local copies, waits for them, and re-layouts: 12.2 us -> 0.81 us
    psum x1 -> x0, waiting for transfers between devices: 173 us -> none  [shards(): lax.psum((grad_in, grad_mid, grad_out), ('row', 'col'))]
    psum x1 -> x0, blocking collectives: 80.8 us -> none  [grid_total_sum(): return lax.psum(grid_local, ('row', 'col'))]
    ppermute x8 -> x28, starting transfers between devices: 30.3 us -> 65.4 us  [the longest x18 39.4 us: swapped(): return lax.ppermute(block, axis, [(i, i ^ mask) for i in range(size)])]
    dot_general x17 -> x0, matrix products: 31.7 us -> none  [the longest x3 9.94 us: contract_cols(): lax.dot_general(former, latter, (((1,), (1,)), ((), ())), preferred_eleme...]
    pallas_call x0 -> x6, Pallas kernels: none -> 30.9 us  [the longest x1 13.8 us: backward(): pl.pallas_call(backward_kernel, grid=(STEPS,), out_shape=outs, in_specs=[...]
    ppermute x8 -> x28, waiting for transfers between devices: 14.6 us -> 44 us  [the longest x18 26.7 us: swapped(): return lax.ppermute(block, axis, [(i, i ^ mask) for i in range(size)])]
    div x7 -> x0, other arithmetic: 9.63 us -> none  [the longest x5 9.61 us: adam_step(): new_one / (1.0 - BETA_ONE ** ADAM_STEP)]
    slice x23 -> x1, local copies, waits for them, and re-layouts: 7.06 us -> 0.03 us  [reduce_grads(): part = scatter_sum([part[d * 4:d * 4 + 4] for d in range(4)], 'x')]
  transfers between devices with their start and end apart: 9 -> 28, of which waited for: 5 -> 16; matrix products, arithmetic and copies ran while one was open for 4% -> 0% of each run, Pallas kernels for 0% -> 2%
where the time goes in v2:
time: 144 us
  starting transfers between devices  65.4 us (45%)
  waiting for transfers between devices  44 us (31%)
  Pallas kernels  30.9 us (21%)
  other arithmetic  1.53 us (1%)
    ppermute x18, starting transfers between devices, swapped(): return lax.ppermute(block, axis, [(i, i ^ mask) for i in range(size)])  39.4 us
    ppermute x18, waiting for transfers between devices, swapped(): return lax.ppermute(block, axis, [(i, i ^ mask) for i in range(size)])  26.7 us
    pallas_call x1, Pallas kernels, backward(): pl.pallas_call(backward_kernel, grid=(STEPS,), out_shape=outs, in_specs=[...  13.8 us
    ppermute x2, waiting for transfers between devices, shifted(): return lax.ppermute(block, ROW + COL, route)  10.8 us
    ppermute x2, starting transfers between devices, shifted(): return lax.ppermute(block, ROW + COL, route)  10.1 us
    ppermute x4, starting transfers between devices, shifted(): lax.ppermute(block, COL, [(i, (i + right) % cols) for i in range(cols)])  8.1 us
    pallas_call x1, Pallas kernels, forward(): pl.pallas_call(forward_kernel, grid=(STEPS,), out_shape=(jax.ShapeDtypeSt...  7.85 us
    ppermute x4, starting transfers between devices, shifted(): lax.ppermute(block, ROW, [(i, (i + down) % rows) for i in range(rows)])  7.78 us
  transfers between devices with their start and end apart: 28, of which 16 were waited for; matrix products, arithmetic and copies ran while one was open for 0% of the time, Pallas kernels for 2%

profile of v2, /device:TPU:1, one launch (start us, length us, event | category | flops | bytes accessed | tf_op | source)
XLA Modules:
  0.0 143.7 jit_solution(5454099683791395154)
XLA Ops:
  0.6 2.5 %edges.1 = (f32[32,256]{1,0:T(8,128)S(1)}, f32[32,128]{1,0:T(8,128)S(1)}, f32[32,32,128]{2,1,0:T(8,128)S(1)}, f32[8,32,128]{2,1,0:T(8,128)S(1)}) custom-call(f32[32,32,128]{2,1,0:T(8,128)} %fine_hbm.1, f32[32,8,32]{2,1,0:T(8,128)} %coarse_hbm.1), custom_call_target="tpu_custom_call" | custom-call | tf_op jit(solution)/shard_map/edges/pallas_call | solution.py:174
  3.2 7.4 %collective-permute-start = (f32[32,256]{1,0:T(8,128)S(1)}, f32[32,256]{1,0:T(8,128)S(1)}, u32[]{:S(2)}, u32[]{:S(2)}) collective-permute-start(f32[32,256]{1,0:T(8,128)S(1)} %get-tuple-element.43), channel_id=1, source_target_pairs={{0,240},{16,0},{32,16},{48,32},{64,48},{80,64},{96,80},{112,96},{1... | collective-permute-start | bytes 98312 | tf_op jit(solution)/shard_map/ppermute | solution.py:56
  10.6 1.0 collective-permute-start.1
  11.6 6.5 %collective-permute-start.2 = (f32[32,128]{1,0:T(8,128)S(1)}, f32[32,128]{1,0:T(8,128)S(1)}, u32[]{:S(2)}, u32[]{:S(2)}) collective-permute-start(f32[32,128]{1,0:T(8,128)S(1)} %get-tuple-element.44), channel_id=1, source_target_pairs={{0,255},{1,240},{2,241},{3,242},{4,243},{5,244},{6,245},{7,246},{8... | collective-permute-start | bytes 49160 | tf_op jit(solution)/shard_map/ppermute | solution.py:64
  18.7 2.2 %prepare.1 = (f32[8,128]{1,0:T(8,128)S(1)}, bf16[512,64]{1,0:T(8,128)(2,1)S(1)}, bf16[64,512]{1,0:T(8,128)(2,1)S(1)}, bf16[512,512]{1,0:T(8,128)(2,1)S(1)}, bf16...) custom-call(s32[1,1,2]{2,1,0:T(1,128)S(1)} %copy-done.10, ...), custom_call_target="tpu_custom_call" | custom-call | tf_op jit(solution)/shard_map/prepare/pallas_call | solution.py:265
  21.0 7.8 %forward.1 = (bf16[64,4096]{1,0:T(8,128)(2,1)S(1)}, f32[512,4096]{1,0:T(8,128)S(1)}, f32[8,4096]{1,0:T(8,128)S(1)}, f32[8,128]{1,0:T(8,128)S(1)}, f32[8,128]{1,0...) custom-call(f32[8,128]{1,0:T(8,128)S(1)} %get-tuple-element.40.shift_ref, ...), custom_call_target="tpu_custom_call" | custom-call | tf_op jit(solution)/shard_map/forward/pallas_call | solution.py:371
  29.2 4.3 %collective-permute-start.4 = (f32[8,128]{1,0:T(8,128)S(1)}, f32[8,128]{1,0:T(8,128)S(1)}, u32[]{:S(2)}, u32[]{:S(2)}) collective-permute-start(f32[8,128]{1,0:T(8,128)S(1)} %get-tuple-element.54), channel_id=1, source_target_pairs={{0,15},{1,0},{2,1},{3,2},{4,3},{5,4},{6,5},{7,6},{8,7},{9,8},{10,9... | collective-permute-start | bytes 12296 | tf_op jit(solution)/shard_map/ppermute | solution.py:58
  33.5 2.9 %collective-permute-start.6 = (f32[8,128]{1,0:T(8,128)S(1)}, f32[8,128]{1,0:T(8,128)S(1)}, u32[]{:S(2)}, u32[]{:S(2)}) collective-permute-start(f32[8,128]{1,0:T(8,128)S(1)} %get-tuple-element.56), channel_id=1, source_target_pairs={{0,1},{1,2},{2,3},{3,4},{4,5},{5,6},{6,7},{7,8},{8,9},{9,10},{10,1... | collective-permute-start | bytes 12296 | tf_op jit(solution)/shard_map/ppermute | solution.py:58
  36.3 3.5 %collective-permute-done.5.above_ref = f32[8,128]{1,0:T(8,128)S(1)} collective-permute-done((f32[8,128]{1,0:T(8,128)S(1)}, f32[8,128]{1,0:T(8,128)S(1)}, u32[]{:S(2)}, u32[]{:S(2)}) %collective-permute-start.5) | collective-permute-done | bytes 4128 | tf_op jit(solution)/shard_map/ppermute | solution.py:56
  39.9 13.8 %backward.1 = (f32[16,80,128]{2,1,0:T(8,128)S(1)}, f32[16,80,128]{2,1,0:T(8,128)S(1)}, f32[32,32,128]{2,1,0:T(8,128)S(1)}, f32[8,32,128]{2,1,0:T(8,128)S(1)}, f3...) custom-call(f32[8,128]{1,0:T(8,128)S(1)} %get-tuple-element.40.shift_ref, ...), custom_call_target="tpu_custom_call" | custom-call | tf_op jit(solution)/shard_map/backward/pallas_call | solution.py:569
  53.7 7.6 %collective-permute-start.7 = (f32[16,80,128]{2,1,0:T(8,128)S(1)}, f32[16,80,128]{2,1,0:T(8,128)S(1)}, u32[]{:S(2)}, u32[]{:S(2)}) collective-permute-start(f32[16,80,128]{2,1,0:T(8,128)S(1)} %get-tuple-element.61), channel_id=1, source_target_pairs={{0,1},{1,0},{2,3},{3,2},{4,5},{5,4},{6,7},{7,6},{8,9},{9,8},{10,11... | collective-permute-start | bytes 1966088 | tf_op jit(solution)/shard_map/ppermute | solution.py:74
  61.3 1.7 %collective-permute-done.7 = f32[16,80,128]{2,1,0:T(8,128)S(1)} collective-permute-done((f32[16,80,128]{2,1,0:T(8,128)S(1)}, f32[16,80,128]{2,1,0:T(8,128)S(1)}, u32[]{:S(2)}, u32[]{:S(2)}) %collective-permute-start.7) | collective-permute-done | bytes 655392 | tf_op jit(solution)/shard_map/ppermute | solution.py:74
  63.2 1.7 %collective-permute-start.10 = (f32[4,80,128]{2,1,0:T(8,128)S(1)}, f32[4,80,128]{2,1,0:T(8,128)S(1)}, u32[]{:S(2)}, u32[]{:S(2)}) collective-permute-start(f32[4,80,128]{2,1,0:T(8,128)S(1)} %get-tuple-element.75), channel_id=1, source_target_pairs={{0,48},{16,32},{32,16},{48,0},{1,49},{17,33},{33,17},{49,1},{2,50}... | collective-permute-start | bytes 491528 | tf_op jit(solution)/shard_map/ppermute | solution.py:74
  64.9 2.3 %collective-permute-start.9 = (f32[4,80,128]{2,1,0:T(8,128)S(1)}, f32[4,80,128]{2,1,0:T(8,128)S(1)}, u32[]{:S(2)}, u32[]{:S(2)}) collective-permute-start(f32[4,80,128]{2,1,0:T(8,128)S(1)} %get-tuple-element.76), channel_id=1, source_target_pairs={{0,32},{16,48},{32,0},{48,16},{1,33},{17,49},{33,1},{49,17},{2,34}... | collective-permute-start | bytes 491528 | tf_op jit(solution)/shard_map/ppermute | solution.py:74
  67.1 2.8 %collective-permute-done.10 = f32[4,80,128]{2,1,0:T(8,128)S(1)} collective-permute-done((f32[4,80,128]{2,1,0:T(8,128)S(1)}, f32[4,80,128]{2,1,0:T(8,128)S(1)}, u32[]{:S(2)}, u32[]{:S(2)}) %collective-permute-start.10) | collective-permute-done | bytes 163872 | tf_op jit(solution)/shard_map/ppermute | solution.py:74
  70.0 4.3 %collective-permute-done.9 = f32[4,80,128]{2,1,0:T(8,128)S(1)} collective-permute-done((f32[4,80,128]{2,1,0:T(8,128)S(1)}, f32[4,80,128]{2,1,0:T(8,128)S(1)}, u32[]{:S(2)}, u32[]{:S(2)}) %collective-permute-start.9) | collective-permute-done | bytes 163872 | tf_op jit(solution)/shard_map/ppermute | solution.py:74
  74.5 3.7 %collective-permute-start.13 = (f32[80,128]{1,0:T(8,128)S(1)}, f32[80,128]{1,0:T(8,128)S(1)}, u32[]{:S(2)}, u32[]{:S(2)}) collective-permute-start(f32[80,128]{1,0:T(8,128)S(1)} %get-tuple-element.78), channel_id=1, source_target_pairs={{0,12},{4,8},{8,4},{12,0},{1,13},{5,9},{9,5},{13,1},{2,14},{6,10},... | collective-permute-start | bytes 122888 | tf_op jit(solution)/shard_map/ppermute | solution.py:74
  78.3 3.0 %collective-permute-done.15.col_ref = f32[32,128]{1,0:T(8,128)S(1)} collective-permute-done((f32[32,128]{1,0:T(8,128)S(1)}, f32[32,128]{1,0:T(8,128)S(1)}, u32[]{:S(2)}, u32[]{:S(2)}) %collective-permute-start.15) | collective-permute-done | bytes 16416 | tf_op jit(solution)/shard_map/ppermute | solution.py:58
  81.3 3.6 %collective-permute-start.16 = (f32[32,128]{1,0:T(8,128)S(1)}, f32[32,128]{1,0:T(8,128)S(1)}, u32[]{:S(2)}, u32[]{:S(2)}) collective-permute-start(f32[32,128]{1,0:T(8,128)S(1)} %get-tuple-element.66), channel_id=1, source_target_pairs={{0,17},{1,18},{2,19},{3,20},{4,21},{5,22},{6,23},{7,24},{8,25},{9,... | collective-permute-start | bytes 49160 | tf_op jit(solution)/shard_map/ppermute | solution.py:64
  84.9 10.8 %collective-permute-done.16.corner_ref = f32[32,128]{1,0:T(8,128)S(1)} collective-permute-done((f32[32,128]{1,0:T(8,128)S(1)}, f32[32,128]{1,0:T(8,128)S(1)}, u32[]{:S(2)}, u32[]{:S(2)}) %collective-permute-start.16) | collective-permute-done | bytes 16416 | tf_op jit(solution)/shard_map/ppermute | solution.py:64
  96.6 3.4 %collective-permute-start.19 = (f32[88,128]{1,0:T(8,128)S(1)}, f32[88,128]{1,0:T(8,128)S(1)}, u32[]{:S(2)}, u32[]{:S(2)}) collective-permute-start(f32[88,128]{1,0:T(8,128)S(1)} %pad_maximum_fusion.1), channel_id=1, source_target_pairs={{0,192},{64,128},{128,64},{192,0},{1,193},{65,129},{129,65},{193,1... | collective-permute-start | bytes 135176 | tf_op jit(solution)/shard_map/ppermute | solution.py:74
  100.4 1.6 %collective-permute-done.19 = f32[88,128]{1,0:T(8,128)S(1)} collective-permute-done((f32[88,128]{1,0:T(8,128)S(1)}, f32[88,128]{1,0:T(8,128)S(1)}, u32[]{:S(2)}, u32[]{:S(2)}) %collective-permute-start.19) | collective-permute-done | bytes 45088 | tf_op jit(solution)/shard_map/ppermute | solution.py:74
  102.3 6.8 %collective-permute-done.20 = f32[88,128]{1,0:T(8,128)S(1)} collective-permute-done((f32[88,128]{1,0:T(8,128)S(1)}, f32[88,128]{1,0:T(8,128)S(1)}, u32[]{:S(2)}, u32[]{:S(2)}) %collective-permute-start.20) | collective-permute-done | bytes 45088 | tf_op jit(solution)/shard_map/ppermute | solution.py:74
  110.6 3.7 %collective-permute-start.23 = (f32[88,128]{1,0:T(8,128)S(1)}, f32[88,128]{1,0:T(8,128)S(1)}, u32[]{:S(2)}, u32[]{:S(2)}) collective-permute-start(f32[88,128]{1,0:T(8,128)S(1)} %get-tuple-element.82), channel_id=1, source_target_pairs={{0,12},{4,8},{8,4},{12,0},{1,13},{5,9},{9,5},{13,1},{2,14},{6,10},... | collective-permute-start | bytes 135176 | tf_op jit(solution)/shard_map/ppermute | solution.py:74
  115.0 0.8 collective-permute-done.23
  116.3 2.5 %collective-permute-start.25 = (f32[4,88,128]{2,1,0:T(8,128)S(1)}, f32[4,88,128]{2,1,0:T(8,128)S(1)}, u32[]{:S(2)}, u32[]{:S(2)}) collective-permute-start(f32[4,88,128]{2,1,0:T(8,128)S(1)} %pad_maximum_fusion), channel_id=1, source_target_pairs={{0,32},{16,48},{32,0},{48,16},{1,33},{17,49},{33,1},{49,17},{2,34}... | collective-permute-start | bytes 540680 | tf_op jit(solution)/shard_map/ppermute | solution.py:74
  118.8 1.0 collective-permute-start.26
  120.3 3.3 %collective-permute-done.25 = f32[4,88,128]{2,1,0:T(8,128)S(1)} collective-permute-done((f32[4,88,128]{2,1,0:T(8,128)S(1)}, f32[4,88,128]{2,1,0:T(8,128)S(1)}, u32[]{:S(2)}, u32[]{:S(2)}) %collective-permute-start.25) | collective-permute-done | bytes 180256 | tf_op jit(solution)/shard_map/ppermute | solution.py:74
  123.6 2.1 %collective-permute-done.26 = f32[4,88,128]{2,1,0:T(8,128)S(1)} collective-permute-done((f32[4,88,128]{2,1,0:T(8,128)S(1)}, f32[4,88,128]{2,1,0:T(8,128)S(1)}, u32[]{:S(2)}, u32[]{:S(2)}) %collective-permute-start.26) | collective-permute-done | bytes 180256 | tf_op jit(solution)/shard_map/ppermute | solution.py:74
  125.7 12.1 %collective-permute-start.27 = (f32[16,88,128]{2,1,0:T(8,128)S(1)}, f32[16,88,128]{2,1,0:T(8,128)S(1)}, u32[]{:S(2)}, u32[]{:S(2)}) collective-permute-start(f32[16,88,128]{2,1,0:T(8,128)S(1)} %constant_dynamic-update-slice_fusion.refs_0_), channel_id=1, source_target_pairs={{0,1},{1,0},{2,3},{3,2},{4,5},{5,4},{6,7},{7,6},{8,9},{9,8},{10,11... | collective-permute-start | bytes 2162696 | tf_op jit(solution)/shard_map/ppermute | solution.py:74
  137.9 1.8 %collective-permute-done.27.refs_1_ = f32[16,88,128]{2,1,0:T(8,128)S(1)} collective-permute-done((f32[16,88,128]{2,1,0:T(8,128)S(1)}, f32[16,88,128]{2,1,0:T(8,128)S(1)}, u32[]{:S(2)}, u32[]{:S(2)}) %collective-permute-start.27) | collective-permute-done | bytes 720928 | tf_op jit(solution)/shard_map/ppermute | solution.py:74
  139.7 3.9 %steps.1 = (f32[512,512]{1,0:T(8,128)}, f32[64,512]{1,0:T(8,128)}, f32[3,512]{1,0:T(4,128)}, f32[32,32,128]{2,1,0:T(8,128)}, f32[32,8,32]{2,1,0:T(8,128)}) custom-call(f32[16,88,128]{2,1,0:T(8,128)S(1)} %constant_dynamic-update-slice_fusion.refs_0_, f32[16,88,128]{2,1,0:T(8,128)S(1)} %collective-permute-done.27.refs_1_, ...), custom_call_target="tpu_custom_call" | custom-call | tf_op jit(solution)/shard_map/steps/pallas_call | solution.py:716
  (72 shorter events, 6.2 us)
Async XLA Ops:
  3.2 17.8 %collective-permute-start = (f32[32,256]{1,0:T(8,128)S(1)}, f32[32,256]{1,0:T(8,128)S(1)}, u32[]{:S(2)}, u32[]{:S(2)}) collective-permute-start(f32[32,256]{1,0:T(8,128)S(1)} %get-tuple-element.43), channel_id=1, source_target_pairs={{0,240},{16,0},{32,16},{48,32},{64,48},{80,64},{96,80},{112,96},{1... | collective-permute-start | bytes 98312 | tf_op jit(solution)/shard_map/ppermute | solution.py:56
  10.6 10.4 %collective-permute-start.1 = (f32[32,128]{1,0:T(8,128)S(1)}, f32[32,128]{1,0:T(8,128)S(1)}, u32[]{:S(2)}, u32[]{:S(2)}) collective-permute-start(f32[32,128]{1,0:T(8,128)S(1)} %get-tuple-element.44), channel_id=1, source_target_pairs={{0,15},{1,0},{2,1},{3,2},{4,3},{5,4},{6,5},{7,6},{8,7},{9,8},{10,9... | collective-permute-start | bytes 49160 | tf_op jit(solution)/shard_map/ppermute | solution.py:58
  11.6 9.4 %collective-permute-start.2 = (f32[32,128]{1,0:T(8,128)S(1)}, f32[32,128]{1,0:T(8,128)S(1)}, u32[]{:S(2)}, u32[]{:S(2)}) collective-permute-start(f32[32,128]{1,0:T(8,128)S(1)} %get-tuple-element.44), channel_id=1, source_target_pairs={{0,255},{1,240},{2,241},{3,242},{4,243},{5,244},{6,245},{7,246},{8... | collective-permute-start | bytes 49160 | tf_op jit(solution)/shard_map/ppermute | solution.py:64
  28.9 7.5 %collective-permute-start.3 = (f32[8,128]{1,0:T(8,128)S(1)}, f32[8,128]{1,0:T(8,128)S(1)}, u32[]{:S(2)}, u32[]{:S(2)}) collective-permute-start(f32[8,128]{1,0:T(8,128)S(1)} %get-tuple-element.53), channel_id=1, source_target_pairs={{0,240},{16,0},{32,16},{48,32},{64,48},{80,64},{96,80},{112,96},{1... | collective-permute-start | bytes 12296 | tf_op jit(solution)/shard_map/ppermute | solution.py:56
  29.2 7.2 %collective-permute-start.4 = (f32[8,128]{1,0:T(8,128)S(1)}, f32[8,128]{1,0:T(8,128)S(1)}, u32[]{:S(2)}, u32[]{:S(2)}) collective-permute-start(f32[8,128]{1,0:T(8,128)S(1)} %get-tuple-element.54), channel_id=1, source_target_pairs={{0,15},{1,0},{2,1},{3,2},{4,3},{5,4},{6,5},{7,6},{8,7},{9,8},{10,9... | collective-permute-start | bytes 12296 | tf_op jit(solution)/shard_map/ppermute | solution.py:58
  33.5 6.4 %collective-permute-start.5 = (f32[8,128]{1,0:T(8,128)S(1)}, f32[8,128]{1,0:T(8,128)S(1)}, u32[]{:S(2)}, u32[]{:S(2)}) collective-permute-start(f32[8,128]{1,0:T(8,128)S(1)} %get-tuple-element.55), channel_id=1, source_target_pairs={{0,16},{16,32},{32,48},{48,64},{64,80},{80,96},{96,112},{112,128},... | collective-permute-start | bytes 12296 | tf_op jit(solution)/shard_map/ppermute | solution.py:56
  33.5 6.4 %collective-permute-start.6 = (f32[8,128]{1,0:T(8,128)S(1)}, f32[8,128]{1,0:T(8,128)S(1)}, u32[]{:S(2)}, u32[]{:S(2)}) collective-permute-start(f32[8,128]{1,0:T(8,128)S(1)} %get-tuple-element.56), channel_id=1, source_target_pairs={{0,1},{1,2},{2,3},{3,4},{4,5},{5,6},{6,7},{7,8},{8,9},{9,10},{10,1... | collective-permute-start | bytes 12296 | tf_op jit(solution)/shard_map/ppermute | solution.py:58
  39.8 99.8 %copy-start = (f32[1,512,512]{2,1,0:T(8,128)S(1)}, f32[1,512,512]{2,1,0:T(8,128)}, u32[]{:S(2)}) copy-start(f32[1,512,512]{2,1,0:T(8,128)} %param.30) | copy-start | bytes 3145732
  39.8 99.8 %copy-start.1 = (f32[1,512,512]{2,1,0:T(8,128)S(1)}, f32[1,512,512]{2,1,0:T(8,128)}, u32[]{:S(2)}) copy-start(f32[1,512,512]{2,1,0:T(8,128)} %param.31) | copy-start | bytes 3145732
  39.8 99.8 %copy-start.2 = (f32[32,32,128]{2,1,0:T(8,128)S(1)}, f32[32,32,128]{2,1,0:T(8,128)}, u32[]{:S(2)}) copy-start(f32[32,32,128]{2,1,0:T(8,128)} %refs_10_.1) | copy-start | bytes 1572868
  39.8 99.8 %copy-start.3 = (f32[32,32,128]{2,1,0:T(8,128)S(1)}, f32[32,32,128]{2,1,0:T(8,128)}, u32[]{:S(2)}) copy-start(f32[32,32,128]{2,1,0:T(8,128)} %refs_11_.1) | copy-start | bytes 1572868
  53.7 9.4 %collective-permute-start.7 = (f32[16,80,128]{2,1,0:T(8,128)S(1)}, f32[16,80,128]{2,1,0:T(8,128)S(1)}, u32[]{:S(2)}, u32[]{:S(2)}) collective-permute-start(f32[16,80,128]{2,1,0:T(8,128)S(1)} %get-tuple-element.61), channel_id=1, source_target_pairs={{0,1},{1,0},{2,3},{3,2},{4,5},{5,4},{6,7},{7,6},{8,9},{9,8},{10,11... | collective-permute-start | bytes 1966088 | tf_op jit(solution)/shard_map/ppermute | solution.py:74
  63.2 6.7 %collective-permute-start.10 = (f32[4,80,128]{2,1,0:T(8,128)S(1)}, f32[4,80,128]{2,1,0:T(8,128)S(1)}, u32[]{:S(2)}, u32[]{:S(2)}) collective-permute-start(f32[4,80,128]{2,1,0:T(8,128)S(1)} %get-tuple-element.75), channel_id=1, source_target_pairs={{0,48},{16,32},{32,16},{48,0},{1,49},{17,33},{33,17},{49,1},{2,50}... | collective-permute-start | bytes 491528 | tf_op jit(solution)/shard_map/ppermute | solution.py:74
  64.9 5.1 %collective-permute-start.8 = (f32[4,80,128]{2,1,0:T(8,128)S(1)}, f32[4,80,128]{2,1,0:T(8,128)S(1)}, u32[]{:S(2)}, u32[]{:S(2)}) collective-permute-start(f32[4,80,128]{2,1,0:T(8,128)S(1)} %get-tuple-element.77), channel_id=1, source_target_pairs={{0,16},{16,0},{32,48},{48,32},{1,17},{17,1},{33,49},{49,33},{2,18}... | collective-permute-start | bytes 491528 | tf_op jit(solution)/shard_map/ppermute | solution.py:74
  64.9 9.4 %collective-permute-start.9 = (f32[4,80,128]{2,1,0:T(8,128)S(1)}, f32[4,80,128]{2,1,0:T(8,128)S(1)}, u32[]{:S(2)}, u32[]{:S(2)}) collective-permute-start(f32[4,80,128]{2,1,0:T(8,128)S(1)} %get-tuple-element.76), channel_id=1, source_target_pairs={{0,32},{16,48},{32,0},{48,16},{1,33},{17,49},{33,1},{49,17},{2,34}... | collective-permute-start | bytes 491528 | tf_op jit(solution)/shard_map/ppermute | solution.py:74
  74.3 22.0 %collective-permute-start.11 = (f32[80,128]{1,0:T(8,128)S(1)}, f32[80,128]{1,0:T(8,128)S(1)}, u32[]{:S(2)}, u32[]{:S(2)}) collective-permute-start(f32[80,128]{1,0:T(8,128)S(1)} %get-tuple-element.80), channel_id=1, source_target_pairs={{0,4},{4,0},{8,12},{12,8},{1,5},{5,1},{9,13},{13,9},{2,6},{6,2},{1... | collective-permute-start | bytes 122888 | tf_op jit(solution)/shard_map/ppermute | solution.py:74
  74.4 21.9 %collective-permute-start.12 = (f32[80,128]{1,0:T(8,128)S(1)}, f32[80,128]{1,0:T(8,128)S(1)}, u32[]{:S(2)}, u32[]{:S(2)}) collective-permute-start(f32[80,128]{1,0:T(8,128)S(1)} %get-tuple-element.79), channel_id=1, source_target_pairs={{0,8},{4,12},{8,0},{12,4},{1,9},{5,13},{9,1},{13,5},{2,10},{6,14},... | collective-permute-start | bytes 122888 | tf_op jit(solution)/shard_map/ppermute | solution.py:74
  74.5 21.8 %collective-permute-start.13 = (f32[80,128]{1,0:T(8,128)S(1)}, f32[80,128]{1,0:T(8,128)S(1)}, u32[]{:S(2)}, u32[]{:S(2)}) collective-permute-start(f32[80,128]{1,0:T(8,128)S(1)} %get-tuple-element.78), channel_id=1, source_target_pairs={{0,12},{4,8},{8,4},{12,0},{1,13},{5,9},{9,5},{13,1},{2,14},{6,10},... | collective-permute-start | bytes 122888 | tf_op jit(solution)/shard_map/ppermute | solution.py:74
  78.3 3.0 %collective-permute-start.15 = (f32[32,128]{1,0:T(8,128)S(1)}, f32[32,128]{1,0:T(8,128)S(1)}, u32[]{:S(2)}, u32[]{:S(2)}) collective-permute-start(f32[32,128]{1,0:T(8,128)S(1)} %get-tuple-element.65), channel_id=1, source_target_pairs={{0,1},{1,2},{2,3},{3,4},{4,5},{5,6},{6,7},{7,8},{8,9},{9,10},{10,1... | collective-permute-start | bytes 49160 | tf_op jit(solution)/shard_map/ppermute | solution.py:58
  78.3 17.4 %collective-permute-start.14 = (f32[32,256]{1,0:T(8,128)S(1)}, f32[32,256]{1,0:T(8,128)S(1)}, u32[]{:S(2)}, u32[]{:S(2)}) collective-permute-start(f32[32,256]{1,0:T(8,128)S(1)} %get-tuple-element.64), channel_id=1, source_target_pairs={{0,16},{16,32},{32,48},{48,64},{64,80},{80,96},{96,112},{112,128},... | collective-permute-start | bytes 98312 | tf_op jit(solution)/shard_map/ppermute | solution.py:56
  81.3 14.4 %collective-permute-start.16 = (f32[32,128]{1,0:T(8,128)S(1)}, f32[32,128]{1,0:T(8,128)S(1)}, u32[]{:S(2)}, u32[]{:S(2)}) collective-permute-start(f32[32,128]{1,0:T(8,128)S(1)} %get-tuple-element.66), channel_id=1, source_target_pairs={{0,17},{1,18},{2,19},{3,20},{4,21},{5,22},{6,23},{7,24},{8,25},{9,... | collective-permute-start | bytes 49160 | tf_op jit(solution)/shard_map/ppermute | solution.py:64
  96.4 3.6 %collective-permute-start.17 = (f32[88,128]{1,0:T(8,128)S(1)}, f32[88,128]{1,0:T(8,128)S(1)}, u32[]{:S(2)}, u32[]{:S(2)}) collective-permute-start(f32[88,128]{1,0:T(8,128)S(1)} %pad_maximum_fusion.1), channel_id=1, source_target_pairs={{0,64},{64,0},{128,192},{192,128},{1,65},{65,1},{129,193},{193,129... | collective-permute-start | bytes 135176 | tf_op jit(solution)/shard_map/ppermute | solution.py:74
  96.5 3.9 %collective-permute-start.18 = (f32[88,128]{1,0:T(8,128)S(1)}, f32[88,128]{1,0:T(8,128)S(1)}, u32[]{:S(2)}, u32[]{:S(2)}) collective-permute-start(f32[88,128]{1,0:T(8,128)S(1)} %pad_maximum_fusion.1), channel_id=1, source_target_pairs={{0,128},{64,192},{128,0},{192,64},{1,129},{65,193},{129,1},{193,65... | collective-permute-start | bytes 135176 | tf_op jit(solution)/shard_map/ppermute | solution.py:74
  96.6 5.3 %collective-permute-start.19 = (f32[88,128]{1,0:T(8,128)S(1)}, f32[88,128]{1,0:T(8,128)S(1)}, u32[]{:S(2)}, u32[]{:S(2)}) collective-permute-start(f32[88,128]{1,0:T(8,128)S(1)} %pad_maximum_fusion.1), channel_id=1, source_target_pairs={{0,192},{64,128},{128,64},{192,0},{1,193},{65,129},{129,65},{193,1... | collective-permute-start | bytes 135176 | tf_op jit(solution)/shard_map/ppermute | solution.py:74
  102.0 7.1 %collective-permute-start.20 = (f32[88,128]{1,0:T(8,128)S(1)}, f32[88,128]{1,0:T(8,128)S(1)}, u32[]{:S(2)}, u32[]{:S(2)}) collective-permute-start(f32[88,128]{1,0:T(8,128)S(1)} %add_add_fusion), channel_id=1, source_target_pairs={{0,2},{2,0},{1,3},{3,1},{4,6},{6,4},{5,7},{7,5},{8,10},{10,8},{9,1... | collective-permute-start | bytes 135176 | tf_op jit(solution)/shard_map/ppermute | solution.py:74
  110.4 3.9 %collective-permute-start.21 = (f32[88,128]{1,0:T(8,128)S(1)}, f32[88,128]{1,0:T(8,128)S(1)}, u32[]{:S(2)}, u32[]{:S(2)}) collective-permute-start(f32[88,128]{1,0:T(8,128)S(1)} %get-tuple-element.82), channel_id=1, source_target_pairs={{0,4},{4,0},{8,12},{12,8},{1,5},{5,1},{9,13},{13,9},{2,6},{6,2},{1... | collective-permute-start | bytes 135176 | tf_op jit(solution)/shard_map/ppermute | solution.py:74
  110.5 4.5 %collective-permute-start.22 = (f32[88,128]{1,0:T(8,128)S(1)}, f32[88,128]{1,0:T(8,128)S(1)}, u32[]{:S(2)}, u32[]{:S(2)}) collective-permute-start(f32[88,128]{1,0:T(8,128)S(1)} %get-tuple-element.82), channel_id=1, source_target_pairs={{0,8},{4,12},{8,0},{12,4},{1,9},{5,13},{9,1},{13,5},{2,10},{6,14},... | collective-permute-start | bytes 135176 | tf_op jit(solution)/shard_map/ppermute | solution.py:74
  110.6 5.2 %collective-permute-start.23 = (f32[88,128]{1,0:T(8,128)S(1)}, f32[88,128]{1,0:T(8,128)S(1)}, u32[]{:S(2)}, u32[]{:S(2)}) collective-permute-start(f32[88,128]{1,0:T(8,128)S(1)} %get-tuple-element.82), channel_id=1, source_target_pairs={{0,12},{4,8},{8,4},{12,0},{1,13},{5,9},{9,5},{13,1},{2,14},{6,10},... | collective-permute-start | bytes 135176 | tf_op jit(solution)/shard_map/ppermute | solution.py:74
  115.8 4.4 %collective-permute-start.24 = (f32[4,88,128]{2,1,0:T(8,128)S(1)}, f32[4,88,128]{2,1,0:T(8,128)S(1)}, u32[]{:S(2)}, u32[]{:S(2)}) collective-permute-start(f32[4,88,128]{2,1,0:T(8,128)S(1)} %pad_maximum_fusion), channel_id=1, source_target_pairs={{0,16},{16,0},{32,48},{48,32},{1,17},{17,1},{33,49},{49,33},{2,18}... | collective-permute-start | bytes 540680 | tf_op jit(solution)/shard_map/ppermute | solution.py:74
  116.3 7.3 %collective-permute-start.25 = (f32[4,88,128]{2,1,0:T(8,128)S(1)}, f32[4,88,128]{2,1,0:T(8,128)S(1)}, u32[]{:S(2)}, u32[]{:S(2)}) collective-permute-start(f32[4,88,128]{2,1,0:T(8,128)S(1)} %pad_maximum_fusion), channel_id=1, source_target_pairs={{0,32},{16,48},{32,0},{48,16},{1,33},{17,49},{33,1},{49,17},{2,34}... | collective-permute-start | bytes 540680 | tf_op jit(solution)/shard_map/ppermute | solution.py:74
  118.8 6.9 %collective-permute-start.26 = (f32[4,88,128]{2,1,0:T(8,128)S(1)}, f32[4,88,128]{2,1,0:T(8,128)S(1)}, u32[]{:S(2)}, u32[]{:S(2)}) collective-permute-start(f32[4,88,128]{2,1,0:T(8,128)S(1)} %pad_maximum_fusion), channel_id=1, source_target_pairs={{0,48},{16,32},{32,16},{48,0},{1,49},{17,33},{33,17},{49,1},{2,50}... | collective-permute-start | bytes 540680 | tf_op jit(solution)/shard_map/ppermute | solution.py:74
  125.7 13.9 %collective-permute-start.27 = (f32[16,88,128]{2,1,0:T(8,128)S(1)}, f32[16,88,128]{2,1,0:T(8,128)S(1)}, u32[]{:S(2)}, u32[]{:S(2)}) collective-permute-start(f32[16,88,128]{2,1,0:T(8,128)S(1)} %constant_dynamic-update-slice_fusion.refs_0_), channel_id=1, source_target_pairs={{0,1},{1,0},{2,3},{3,2},{4,5},{5,4},{6,7},{7,6},{8,9},{9,8},{10,11... | collective-permute-start | bytes 2162696 | tf_op jit(solution)/shard_map/ppermute | solution.py:74
  (7 other events, 599.7 us)

commit v3 on v2

--- a/solution.py
+++ b/solution.py
@@ -25,12 +25,10 @@
 CR = 8
 CC = 32
 HID = 512
-STEPS = 4
-CHAINS = 2
-BLOCK = SR * SC // STEPS
-WIDTH = BLOCK // CHAINS
-LINES = SR // STEPS
-BANDS = CR // STEPS
+CHAINS = 4
+WIDTH = SR * SC // CHAINS
+LINES = SR // CHAINS
+PARTS = 2
 F32 = jnp.float32
 BF16 = jnp.bfloat16
 MIB = 1 << 20
@@ -62,6 +60,13 @@
         for c in range(cols)
     ]
     return lax.ppermute(block, ROW + COL, route)
+
+
+def meetings(block_one, block_two, axes):
+    size = axes_size(axes)
+    one = [(i, i ^ 1) for i in range(size)]
+    two = [(i, (i + 1 if i % 2 else i - 1) % size) for i in range(size)]
+    return lax.ppermute(block_one, axes, one), lax.ppermute(block_two, axes, two)
 
 
 def at_ends():
@@ -289,111 +294,91 @@
     feat_ref,
     pre_ref,
     pred_ref,
-    up_ref,
-    left_ref,
-    down_ref,
-    right_ref,
-    lines,
-    bands,
+    row_one_ref,
+    row_two_ref,
+    col_one_ref,
+    col_two_ref,
 ):
-    step = pl.program_id(0)
     shift_y = shift_ref[0:1, :]
     shift_x = shift_ref[1:2, :]
-
-    @pl.when(step == 0)
-    def _():
-        lane = lane_ids(CH)
-        unused_first_row, last_row, unused_first_col, last_col = at_ends()
-        row_in = jnp.where(last_row, 0.0, row_ref[...])
-        col_in = jnp.where(last_col, 0.0, col_ref[...])
-        corner_in = jnp.where(jnp.logical_or(last_row, last_col), 0.0, corner_ref[...])
-
-        def across(line, following):
-            moved = jnp.where(lane == SC - 1, following, pltpu.roll(line, SC - 1, 1))
-            return line * (1.0 - shift_x) + moved * shift_x
-
-        stage = []
-        for i in range(CR):
-            stage.append(jnp.where(lane == CC, spread_lane(col_in, SR + i), coarse_ref[i]))
-        stage.append(jnp.where(lane == CC, spread_lane(corner_in, SR), row_in[:, SC:]))
-        bands[...] = dot(
-            jnp.concatenate(stage, axis=0), coarse_table(shift_x), precision=lax.Precision.HIGHEST
-        ).reshape(CR + 1, CH, SC)
-        for i in range(SR):
-            lines[i] = across(fine_ref[i], spread_lane(col_in, i))
-        lines[SR] = across(row_in[:, 0:SC], spread_lane(corner_in, 0))
-        left_ref[...] = jnp.zeros(left_ref.shape, F32)
-        right_ref[...] = ends_ref[...]
-
-    tiles = []
-    for k in range(LINES):
-        row = step * LINES + k
-        band = step * BANDS + k // RATIO
-        fine = lines[row] * (1.0 - shift_y) + lines[row + 1] * shift_y
-        part = (k % RATIO + shift_y) * (1.0 / RATIO)
-        coarse = bands[band] * (1.0 - part) + bands[band + 1] * part
-        tiles.append(jnp.concatenate([fine, coarse], axis=0).astype(BF16))
-    feat = jnp.concatenate(tiles, axis=1)
-    feat_ref[...] = feat
-    preds = []
+    lane = lane_ids(CH)
+    unused_first_row, last_row, unused_first_col, last_col = at_ends()
+    row_in = jnp.where(last_row, 0.0, row_ref[...])
+    col_in = jnp.where(last_col, 0.0, col_ref[...])
+    corner_in = jnp.where(jnp.logical_or(last_row, last_col), 0.0, corner_ref[...])
+
+    def across(line, following):
+        moved = jnp.where(lane == SC - 1, following, pltpu.roll(line, SC - 1, 1))
+        return line * (1.0 - shift_x) + moved * shift_x
+
+    stage = []
+    for i in range(CR):
+        stage.append(jnp.where(lane == CC, spread_lane(col_in, SR + i), coarse_ref[i]))
+    stage.append(jnp.where(lane == CC, spread_lane(corner_in, SR), row_in[:, SC:]))
+    bands = dot(
+        jnp.concatenate(stage, axis=0), coarse_table(shift_x), precision=lax.Precision.HIGHEST
+    )
+    bands = [bands[i * CH : i * CH + CH] for i in range(CR + 1)]
+    lane8 = lane_ids(8)
+    left = jnp.zeros((8, SC), F32)
+    right = ends_ref[...]
+    line = across(fine_ref[0], spread_lane(col_in, 0))
     for chain in range(CHAINS):
+        tiles = []
+        for k in range(LINES):
+            row = chain * LINES + k
+            if row + 1 < SR:
+                following = across(fine_ref[row + 1], spread_lane(col_in, row + 1))
+            else:
+                following = across(row_in[:, 0:SC], spread_lane(corner_in, 0))
+            fine = line * (1.0 - shift_y) + following * shift_y
+            line = following
+            band = row // RATIO
+            part = (row % RATIO + shift_y) * (1.0 / RATIO)
+            coarse = bands[band] * (1.0 - part) + bands[band + 1] * part
+            tiles.append(jnp.concatenate([fine, coarse], axis=0).astype(BF16))
+        feat = jnp.concatenate(tiles, axis=1)
         cols = slice(chain * WIDTH, chain * WIDTH + WIDTH)
-        pre = dot(in_ref[...], feat[:, cols])
+        feat_ref[:, cols] = feat
+        pre = dot(in_ref[...], feat)
         act = (pre * sigmoid(pre)).astype(BF16)
         pre = dot(mid_ref[...], act)
         pre_ref[:, cols] = pre
         act = (pre * sigmoid(pre)).astype(BF16)
-        preds.append(dot(out_ref[...], act)[0:8])
-    pred = jnp.concatenate(preds, axis=1)
-    pred_ref[...] = pred
-    lane = lane_ids(8)
-    left = left_ref[...]
-    right = right_ref[...]
-    for k in range(LINES):
-        row = step * LINES + k
-        tile = pred[:, k * SC : k * SC + SC]
-        left = jnp.where(lane == row, spread_lane(tile, 0), left)
-        right = right + jnp.where(lane == row, spread_lane(tile, SC - 1), 0.0)
-    left_ref[...] = left
-    right_ref[...] = right
-
-    @pl.when(step == 0)
-    def _():
-        up_ref[...] = pred[:, 0:SC]
-
-    @pl.when(step == STEPS - 1)
-    def _():
-        down_ref[...] = pred[:, BLOCK - SC :] + target_ref[1, :, SR * SC - SC :]
+        pred = dot(out_ref[...], act)[0:8]
+        pred_ref[:, cols] = pred
+        for k in range(LINES):
+            row = chain * LINES + k
+            tile = pred[:, k * SC : k * SC + SC]
+            left = jnp.where(lane8 == row, spread_lane(tile, 0), left)
+            right = right + jnp.where(lane8 == row, spread_lane(tile, SC - 1), 0.0)
+        if chain == 0:
+            up = pred[:, 0:SC]
+    down = pred[:, WIDTH - SC :] + target_ref[1, :, SR * SC - SC :]
+    odd_row = axes_index(ROW) % 2 == 1
+    odd_col = axes_index(COL) % 2 == 1
+    row_one_ref[...] = jnp.where(odd_row, up, down)
+    row_two_ref[...] = jnp.where(odd_row, down, up)
+    col_one_ref[...] = jnp.where(odd_col, left, right)
+    col_two_ref[...] = jnp.where(odd_col, right, left)
 
 
 def forward(*args):
     edge = jax.ShapeDtypeStruct((8, SC), F32)
+    outs = (
+        jax.ShapeDtypeStruct((2 * CH, SR * SC), BF16),
+        jax.ShapeDtypeStruct((HID, SR * SC), F32),
+        jax.ShapeDtypeStruct((8, SR * SC), F32),
+        edge,
+        edge,
+        edge,
+        edge,
+    )
     return pl.pallas_call(
         forward_kernel,
-        grid=(STEPS,),
-        out_shape=(
-            jax.ShapeDtypeStruct((2 * CH, SR * SC), BF16),
-            jax.ShapeDtypeStruct((HID, SR * SC), F32),
-            jax.ShapeDtypeStruct((8, SR * SC), F32),
-            edge,
-            edge,
-            edge,
-            edge,
-        ),
-        in_specs=[whole(a.shape) for a in args],
-        out_specs=(
-            pl.BlockSpec((2 * CH, BLOCK), lambda b: (0, b)),
-            pl.BlockSpec((HID, BLOCK), lambda b: (0, b)),
-            pl.BlockSpec((8, BLOCK), lambda b: (0, b)),
-            whole((8, SC)),
-            whole((8, SC)),
-            whole((8, SC)),
-            whole((8, SC)),
-        ),
-        scratch_shapes=[
-            pltpu.VMEM((SR + 1, CH, SC), F32),
-            pltpu.VMEM((CR + 1, CH, SC), F32),
-        ],
+        out_shape=outs,
+        in_specs=[vmem()] * len(args),
+        out_specs=(vmem(),) * len(outs),
         compiler_params=pltpu.CompilerParams(vmem_limit_bytes=24 * MIB),
         name="forward",
     )(*args)
@@ -404,20 +389,20 @@
     lane = lane_ids(3)
     cot[...] = jnp.zeros(cot.shape, F32)
     line = pred_ref[0:3, 0:SC]
-    row_prior = jnp.where(first_row, 0.0, line - above[0:3, :])
+    row_prior = jnp.where(first_row, 0.0, line - above)
     for i in range(SR):
         if i + 1 < SR:
             following = pred_ref[0:3, (i + 1) * SC : (i + 2) * SC]
         else:
-            following = below[0:3, :]
+            following = below
         value_error = line - target_ref[0, 0:3, i * SC : i * SC + SC]
         row_error = following - line - target_ref[1, 0:3, i * SC : i * SC + SC]
         if i + 1 == SR:
             row_error = jnp.where(last_row, 0.0, row_error)
-        beyond = jnp.where(lane == SC - 1, spread_lane(beside[0:3, :], i), pltpu.roll(line, SC - 1, 1))
+        beyond = jnp.where(lane == SC - 1, spread_lane(beside, i), pltpu.roll(line, SC - 1, 1))
         col_error = beyond - line - target_ref[2, 0:3, i * SC : i * SC + SC]
         col_error = jnp.where(jnp.logical_and(lane == SC - 1, last_col), 0.0, col_error)
-        edge = jnp.where(first_col, 0.0, line - spread_lane(before[0:3, :], i))
+        edge = jnp.where(first_col, 0.0, line - spread_lane(before, i))
         col_prior = jnp.where(lane == 0, edge, pltpu.roll(col_error, 1, 1))
         cot[0:3, i * SC : (i + 1) * SC] = (
             2.0 * LOSS_VALUE * value_error
@@ -433,10 +418,10 @@
     feat_ref,
     pre_ref,
     pred_ref,
-    below_ref,
-    beside_ref,
-    above_ref,
-    before_ref,
+    row_one_ref,
+    row_two_ref,
+    col_one_ref,
+    col_two_ref,
     target_ref,
     in_ref,
     in_turned_ref,
@@ -453,110 +438,103 @@
     grad_mid,
     grad_in,
     grad_out,
-    last_line,
-    bands,
 ):
-    step = pl.program_id(0)
     shift_y = shift_ref[0:1, :]
     shift_x = shift_ref[1:2, :]
     lane = lane_ids(CH)
-
-    @pl.when(step == 0)
-    def _():
-        loss_cotangent(pred_ref, target_ref, below_ref, beside_ref, above_ref, before_ref, cot)
-        grad_mid[...] = jnp.zeros(grad_mid.shape, F32)
-        grad_in[...] = jnp.zeros(grad_in.shape, F32)
-        grad_out[...] = jnp.zeros(grad_out.shape, F32)
-        last_line[...] = jnp.zeros(last_line.shape, F32)
-        bands[0] = jnp.zeros((CH, SC), F32)
-        col_ref[...] = jnp.zeros((CH, SC), F32)
-
-    feat_grads = []
+    odd_row = axes_index(ROW) % 2 == 1
+    odd_col = axes_index(COL) % 2 == 1
+    row_one, row_two = row_one_ref[0:3, :], row_two_ref[0:3, :]
+    col_one, col_two = col_one_ref[0:3, :], col_two_ref[0:3, :]
+    loss_cotangent(
+        pred_ref,
+        target_ref,
+        jnp.where(odd_row, row_two, row_one),
+        jnp.where(odd_col, col_two, col_one),
+        jnp.where(odd_row, row_one, row_two),
+        jnp.where(odd_col, col_one, col_two),
+        cot,
+    )
+
+    def along(line):
+        moved = jnp.where(lane == 0, 0.0, pltpu.roll(line, 1, 1))
+        return line * (1.0 - shift_x) + moved * shift_x
+
+    prior = jnp.zeros((CH, SC), F32)
+    ends = jnp.zeros((CH, SC), F32)
+    upper = jnp.zeros((CH, SC), F32)
+    lower = jnp.zeros((CH, SC), F32)
+    bands = []
     for chain in range(CHAINS):
         cols = slice(chain * WIDTH, chain * WIDTH + WIDTH)
         feat = feat_ref[:, cols]
-        samples = pl.ds(pl.multiple_of(step * BLOCK + chain * WIDTH, WIDTH), WIDTH)
-        out_cot = cot[:, samples].astype(BF16)
+        out_cot = cot[:, cols].astype(BF16)
         pre = pre_ref[:, cols]
         gate = sigmoid(pre)
         act = (pre * gate).astype(BF16)
-        grad_out[...] += dot(out_cot, act, 1, 1)
+        part = dot(out_cot, act, 1, 1)
+        grad_out[...] = part if chain == 0 else grad_out[...] + part
         upward = dot(out_turned_ref[...], out_cot)
         delta = (upward * (gate * (1.0 + pre * (1.0 - gate)))).astype(BF16)
         pre = dot(in_ref[...], feat)
         gate = sigmoid(pre)
         act = (pre * gate).astype(BF16)
-        grad_mid[...] += dot(delta, act, 1, 1)
+        part = dot(delta, act, 1, 1)
+        grad_mid[...] = part if chain == 0 else grad_mid[...] + part
         upward = dot(mid_turned_ref[...], delta)
         delta = (upward * (gate * (1.0 + pre * (1.0 - gate)))).astype(BF16)
-        grad_in[...] += dot(feat, delta, 1, 1)
-        feat_grads.append(dot(in_turned_ref[...], delta))
-    feat_grad = jnp.concatenate(feat_grads, axis=1)
-
-    def along(line):
-        moved = jnp.where(lane == 0, 0.0, pltpu.roll(line, 1, 1))
-        return line * (1.0 - shift_x) + moved * shift_x
-
-    prior = last_line[...]
-    cols = col_ref[...]
-    upper = bands[step * BANDS]
-    lower = jnp.zeros((CH, SC), F32)
-    for k in range(LINES):
-        row = step * LINES + k
-        fine = feat_grad[0:CH, k * SC : k * SC + SC]
-        line = fine * (1.0 - shift_y) + prior * shift_y
-        fine_ref[row] = along(line)
-        cols = jnp.where(lane == row, spread_lane(line * shift_x, SC - 1), cols)
-        prior = fine
-        coarse = feat_grad[CH:, k * SC : k * SC + SC]
-        part = (k % RATIO + shift_y) * (1.0 / RATIO)
-        upper += coarse * (1.0 - part)
-        lower += coarse * part
-        if k % RATIO == RATIO - 1:
-            bands[step * BANDS + k // RATIO] = upper
-            upper = lower
-            lower = jnp.zeros((CH, SC), F32)
-    bands[step * BANDS + BANDS] = upper
-    last_line[...] = prior
-    col_ref[...] = cols
-
-    @pl.when(step == STEPS - 1)
-    def _():
-        line = prior * shift_y
-        row_ref[:, 0:SC] = along(line)
-        corner = jnp.where(lane == 0, spread_lane(line * shift_x, SC - 1), 0.0)
-        spread = dot(
-            bands[...].reshape((CR + 1) * CH, SC),
-            coarse_table(shift_x),
-            1,
-            1,
-            precision=lax.Precision.HIGHEST,
-        )
-        ends = cols
-        for i in range(CR):
-            band = spread[i * CH : i * CH + CH]
-            coarse_ref[i] = jnp.where(lane < CC, band, 0.0)
-            ends = jnp.where(lane == SR + i, spread_lane(band, CC), ends)
-        col_ref[...] = ends
-        band = spread[CR * CH :]
-        row_ref[:, SC:] = jnp.where(lane < CC, band, 0.0)
-        corner_ref[...] = jnp.where(lane == SR, spread_lane(band, CC), corner)
-        core = lax.axis_index("c")
-        tile = axes_index(("x", "y"))
-        for d in range(16):
-            chunk = tile ^ d
-            band = chunk >> 1
-            side = chunk & 1
-            for half, target in ((core, keep_ref), (1 - core, send_ref)):
-                cols_at = pl.ds(pl.multiple_of((half * 2 + side) * 128, 128), 128)
-                target[d, 0:64, :] = grad_mid[pl.ds(pl.multiple_of(band * 64, 64), 64), cols_at]
-                target[d, 64:72, :] = grad_in[pl.ds(pl.multiple_of(band * 8, 8), 8), cols_at]
-                target[d, 72:80, :] = jnp.where(band == 0, grad_out[0:8, cols_at], 0.0)
-
-
-def backward(shifts, feat, pre, pred, *consts):
+        part = dot(feat, delta, 1, 1)
+        grad_in[...] = part if chain == 0 else grad_in[...] + part
+        feat_grad = dot(in_turned_ref[...], delta)
+        for k in range(LINES):
+            row = chain * LINES + k
+            fine = feat_grad[0:CH, k * SC : k * SC + SC]
+            line = fine * (1.0 - shift_y) + prior * shift_y
+            fine_ref[row] = along(line)
+            ends = jnp.where(lane == row, spread_lane(line * shift_x, SC - 1), ends)
+            prior = fine
+            coarse = feat_grad[CH:, k * SC : k * SC + SC]
+            weight = (row % RATIO + shift_y) * (1.0 / RATIO)
+            upper += coarse * (1.0 - weight)
+            lower += coarse * weight
+            if row % RATIO == RATIO - 1:
+                bands.append(upper)
+                upper = lower
+                lower = jnp.zeros((CH, SC), F32)
+    bands.append(upper)
+    line = prior * shift_y
+    row_ref[:, 0:SC] = along(line)
+    corner = jnp.where(lane == 0, spread_lane(line * shift_x, SC - 1), 0.0)
+    spread = dot(
+        jnp.concatenate(bands, axis=0),
+        coarse_table(shift_x),
+        1,
+        1,
+        precision=lax.Precision.HIGHEST,
+    )
+    for i in range(CR):
+        band = spread[i * CH : i * CH + CH]
+        coarse_ref[i] = jnp.where(lane < CC, band, 0.0)
+        ends = jnp.where(lane == SR + i, spread_lane(band, CC), ends)
+    col_ref[...] = ends
+    band = spread[CR * CH :]
+    row_ref[:, SC:] = jnp.where(lane < CC, band, 0.0)
+    corner_ref[...] = jnp.where(lane == SR, spread_lane(band, CC), corner)
+    core = lax.axis_index("c")
+    tile = axes_index(("x", "y"))
+    for d in range(16):
+        chunk = tile ^ d
+        band = chunk >> 1
+        side = chunk & 1
+        for half, target in ((core, keep_ref), (1 - core, send_ref)):
+            cols = pl.ds(pl.multiple_of((half * 2 + side) * 128, 128), 128)
+            target[d, 0:64, :] = grad_mid[pl.ds(pl.multiple_of(band * 64, 64), 64), cols]
+            target[d, 64:72, :] = grad_in[pl.ds(pl.multiple_of(band * 8, 8), 8), cols]
+            target[d, 72:80, :] = jnp.where(band == 0, grad_out[0:8, cols], 0.0)
+
+
+def backward(*args):
     part = jax.ShapeDtypeStruct((16, 80, 128), F32)
-    consts = (pred, *consts)
     outs = (
         part,
         part,
@@ -568,26 +546,18 @@
     )
     return pl.pallas_call(
         backward_kernel,
-        grid=(STEPS,),
         out_shape=outs,
-        in_specs=[
-            whole((8, SC)),
-            pl.BlockSpec((2 * CH, BLOCK), lambda b: (0, b)),
-            pl.BlockSpec((HID, BLOCK), lambda b: (0, b)),
-        ]
-        + [whole(a.shape) for a in consts],
-        out_specs=tuple(whole(o.shape) for o in outs),
+        in_specs=[vmem()] * len(args),
+        out_specs=(vmem(),) * len(outs),
         scratch_shapes=[
             pltpu.VMEM((16, SR * SC), F32),
             pltpu.VMEM((HID, HID), F32),
             pltpu.VMEM((2 * CH, HID), F32),
             pltpu.VMEM((16, HID), F32),
-            pltpu.VMEM((CH, SC), F32),
-            pltpu.VMEM((CR + 1, CH, SC), F32),
         ],
         compiler_params=pltpu.CompilerParams(vmem_limit_bytes=32 * MIB),
         name="backward",
-    )(shifts, feat, pre, *consts)
+    )(*args)
 
 
 def join_kernel(fine_ref, coarse_ref, row_ref, col_ref, corner_ref, fine_out, coarse_out, total_ref):
@@ -672,32 +642,33 @@
 ):
     core = lax.axis_index("c")
     tile = axes_index(("x", "y"))
-    band = pl.program_id(0)
-
-    @pl.when(band == 0)
+    step = pl.program_id(0)
+
+    @pl.when(step == 0)
     def _():
         own_sum = pair_sum([own_ref[d, 80:88, :] for d in range(16)])
         other_sum = pair_sum([other_ref[d, 80:88, :] for d in range(16)])
         totals = own_sum + other_sum
         scales[0:1, :] = clip_factor(totals[0:1, :], grid_entries)
         scales[1:2, :] = clip_factor(totals[1:2, :], decoder_entries)
+        for block in range(4):
+            d = tile ^ (block % 2)
+            data = jnp.where(block // 2 == core, own_ref[d, 72:80, :], other_ref[d, 72:80, :])
+            cols = slice(block * 128, block * 128 + 128)
+            out_ref[:, cols] = adam_step(
+                data[0:3], out_one_ref[:, cols], out_two_ref[:, cols], scales[1:2, :]
+            )
 
     grid_scale = scales[0:1, :]
     scale = scales[1:2, :]
-    for block in range(4):
-        half = block // 2
-        d = tile ^ (band * 2 + block % 2)
-        data = jnp.where(half == core, own_ref[d, 0:80, :], other_ref[d, 0:80, :])
-        cols = slice(block * 128, block * 128 + 128)
-        mid_ref[:, cols] = adam_step(data[0:64], mid_one_ref[:, cols], mid_two_ref[:, cols], scale)
-        in_ref[:, cols] = adam_step(data[64:72], in_one_ref[:, cols], in_two_ref[:, cols], scale)
-
-        @pl.when(band == 0)
-        def _():
-            out_ref[:, cols] = adam_step(
-                data[72:75], out_one_ref[:, cols], out_two_ref[:, cols], scale
-            )
-
+    for k in range(8 // PARTS):
+        for block in range(4):
+            d = tile ^ ((step * (8 // PARTS) + k) * 2 + block % 2)
+            data = jnp.where(block // 2 == core, own_ref[d, 0:72, :], other_ref[d, 0:72, :])
+            at = (slice(k * 64, k * 64 + 64), slice(block * 128, block * 128 + 128))
+            mid_ref[at] = adam_step(data[0:64], mid_one_ref[at], mid_two_ref[at], scale)
+            at = (slice(k * 8, k * 8 + 8), slice(block * 128, block * 128 + 128))
+            in_ref[at] = adam_step(data[64:72], in_one_ref[at], in_two_ref[at], scale)
     fine_step_ref[...] = adam_step(
         fine_ref[...], fine_one_ref[...], fine_two_ref[...], grid_scale[:, None, :]
     )
@@ -707,17 +678,17 @@
 
 
 def all_steps(own, other, fine, coarse, moments, decoder_entries, grid_entries):
-    mid = pl.BlockSpec((64, 512), lambda b: (b, 0))
-    inner = pl.BlockSpec((8, 512), lambda b: (b, 0))
+    mid = pl.BlockSpec((512 // PARTS, 512), lambda b: (b, 0))
+    inner = pl.BlockSpec((64 // PARTS, 512), lambda b: (b, 0))
     outer = whole((3, 512))
-    fine_spec = pl.BlockSpec((CH // 8, SR, SC), lambda b: (b, 0, 0))
-    coarse_spec = pl.BlockSpec((CH // 8, CR, CC), lambda b: (b, 0, 0))
+    fine_spec = pl.BlockSpec((CH // PARTS, SR, SC), lambda b: (b, 0, 0))
+    coarse_spec = pl.BlockSpec((CH // PARTS, CR, CC), lambda b: (b, 0, 0))
     shapes = ((512, 512), (64, 512), (3, 512), fine.shape, coarse.shape)
     return pl.pallas_call(
         lambda *refs: steps_kernel(
             *refs, decoder_entries=decoder_entries, grid_entries=grid_entries
         ),
-        grid=(8,),
+        grid=(PARTS,),
         out_shape=tuple(jax.ShapeDtypeStruct(s, F32) for s in shapes),
         in_specs=[whole(own.shape), whole(other.shape), fine_spec, coarse_spec]
         + [mid, mid, inner, inner, outer, outer, fine_spec, fine_spec, coarse_spec, coarse_spec],
@@ -728,18 +699,37 @@
     )(own, other, fine, coarse, *moments)
 
 
-def reduce_grads(keep, send, grid_local):
+def tally_kernel(one_ref, two_ref, out_ref):
+    total = one_ref[...] + two_ref[...]
+    grads = total[0:80]
+    squares = jnp.sum(grads * grads, axis=0, keepdims=True)
+    squares = jnp.broadcast_to(jnp.sum(squares, axis=1, keepdims=True), (1, SC))
+    out_ref[...] = total
+    out_ref[81:82, :] = squares
+
+
+def tally(one, two):
+    return pl.pallas_call(
+        tally_kernel,
+        out_shape=jax.ShapeDtypeStruct(one.shape, F32),
+        in_specs=[vmem(), vmem()],
+        out_specs=vmem(),
+        compiler_params=pltpu.CompilerParams(vmem_limit_bytes=4 * MIB),
+        name="tally",
+    )(one, two)
+
+
+def reduce_grads(keep, send, fine, coarse, halos):
     part = keep + swapped(send, "c", 1)
     part = scatter_sum([part[d * 4 : d * 4 + 4] for d in range(4)], "x")
+    part, *halos = lax.optimization_barrier((part, *halos))
+    fine, coarse, grid_local = join(fine, coarse, *halos)
     part = scatter_sum([part[d] for d in range(4)], "y")
     part = exchange_sum(jnp.concatenate([part, grid_local]), "zl")
-    part = exchange_sum(part, "zh")
-    squares = jnp.sum(part[:80] * part[:80])
-    tail = jnp.where(jnp.arange(8)[:, None] == 1, squares, part[80:])
-    part = jnp.concatenate([part[:80], tail])
+    part = tally(part, swapped(part, "zh", 1))
     own = jnp.stack(exchange_gather(part, "y"))
     own = jnp.concatenate(exchange_gather(own, "x"))
-    return own, swapped(own, "c", 1)
+    return own, swapped(own, "c", 1), fine, coarse
 
 
 def local_grads(offsets, targets, grid_fine, grid_coarse, weight_in, weight_mid, weight_out):
@@ -750,17 +740,15 @@
     shifts, low_in, in_turned, low_mid, mid_turned, low_out, out_turned, lines, ends = prepare(
         offsets, weight_in.T, weight_mid[0], weight_out, targets
     )
-    feat, pre, pred, up, left, down, right = forward(
+    feat, pre, pred, row_one, row_two, col_one, col_two = forward(
         shifts, fine_lines, coarse_lines, row_in, col_in, corner_in, lines, ends, low_in, low_mid, low_out
     )
-    halos = (shifted(up, -1, 0), shifted(left, 0, -1), shifted(down, 1, 0), shifted(right, 0, 1))
+    halos = (*meetings(row_one, row_two, ROW), *meetings(col_one, col_two, COL))
     keep, send, fine, coarse, row_out, col_out, corner_out = backward(
         shifts, feat, pre, pred, *halos, lines, low_in, in_turned, mid_turned, out_turned
     )
-    row_in = shifted(row_out, 1, 0)
-    col_in = shifted(col_out, 0, 1)
-    corner_in = shifted(corner_out, 1, 1)
-    return (keep, send, *join(fine, coarse, row_in, col_in, corner_in))
+    halos = (shifted(row_out, 1, 0), shifted(col_out, 0, 1), shifted(corner_out, 1, 1))
+    return keep, send, fine, coarse, halos
 
 
 def shards(
@@ -782,13 +770,13 @@
     out_first,
     out_second,
 ):
-    keep, send, fine_grad, coarse_grad, grid_local = local_grads(
+    keep, send, fine, coarse, halos = local_grads(
         offsets, targets, grid_fine, grid_coarse, weight_in, weight_mid, weight_out
     )
+    own, other, fine_grad, coarse_grad = reduce_grads(keep, send, fine, coarse, halos)
     devices = axes_size(ROW) * axes_size(COL)
     grid_entries = (fine_grad.size + coarse_grad.size) * devices
     decoder_entries = weight_in.size + weight_mid.size + weight_out.size
-    own, other = reduce_grads(keep, send, grid_local)
     middle_step, input_step, output_step, fine_step, coarse_step = all_steps(
         own,
         other,

time: 144 us -> 113 us (0.78)
  starting transfers between devices: 65.4 us -> 53.4 us
  waiting for transfers between devices: 44 us -> 33.7 us
  Pallas kernels: 30.9 us -> 24.4 us
    ppermute x2, waiting for transfers between devices: 10.8 us -> 2.27 us  [shifted(): return lax.ppermute(block, ROW + COL, route)]
    ppermute x2, starting transfers between devices: 10.1 us -> 1.69 us  [shifted(): return lax.ppermute(block, ROW + COL, route)]
    ppermute x18, starting transfers between devices: 39.4 us -> 32.6 us  [swapped(): return lax.ppermute(block, axis, [(i, i ^ mask) for i in range(size)])]
    ppermute x0 -> x4, starting transfers between devices: none -> 6.5 us  [the longest x2 4.17 us: meetings(): lax.ppermute(block_one, axes, one)]
    ppermute x18, waiting for transfers between devices: 26.7 us -> 21.5 us  [swapped(): return lax.ppermute(block, axis, [(i, i ^ mask) for i in range(size)])]
    pallas_call x2 -> x3, Pallas kernels: 21.6 us -> 16.8 us  [the longest x1 11.6 us: backward(): pl.pallas_call(backward_kernel, out_shape=outs, in_specs=[vmem()] * len(a...]
    ppermute x0 -> x4, waiting for transfers between devices: none -> 4.78 us  [the longest x2 4.78 us: meetings(): lax.ppermute(block_two, axes, two)]
    ppermute x4 -> x2, starting transfers between devices: 8.1 us -> 5.08 us  [shifted(): lax.ppermute(block, COL, [(i, (i + right) % cols) for i in range(cols)])]
  transfers between devices with their start and end apart: 28 -> 28, of which waited for: 16 -> 19; matrix products, arithmetic and copies ran while one was open for 0% -> 0% of each run, Pallas kernels for 2% -> 3%
where the time goes in v3:
time: 113 us
  starting transfers between devices  53.4 us (47%)
  waiting for transfers between devices  33.7 us (30%)
  Pallas kernels  24.4 us (22%)
    ppermute x18, starting transfers between devices, swapped(): return lax.ppermute(block, axis, [(i, i ^ mask) for i in range(size)])  32.6 us
    ppermute x18, waiting for transfers between devices, swapped(): return lax.ppermute(block, axis, [(i, i ^ mask) for i in range(size)])  21.5 us
    pallas_call x1, Pallas kernels, backward(): pl.pallas_call(backward_kernel, out_shape=outs, in_specs=[vmem()] * len(a...  11.6 us
    ppermute x2, starting transfers between devices, shifted(): lax.ppermute(block, ROW, [(i, (i + down) % rows) for i in range(rows)])  7.45 us
    ppermute x2, starting transfers between devices, shifted(): lax.ppermute(block, COL, [(i, (i + right) % cols) for i in range(cols)])  5.08 us
    pallas_call x1, Pallas kernels, forward(): pl.pallas_call(forward_kernel, out_shape=outs, in_specs=[vmem()] * len(ar...  5.05 us
    ppermute x2, waiting for transfers between devices, meetings(): lax.ppermute(block_two, axes, two)  4.78 us
    ppermute x2, waiting for transfers between devices, shifted(): lax.ppermute(block, ROW, [(i, (i + down) % rows) for i in range(rows)])  4.61 us
  transfers between devices with their start and end apart: 28, of which 19 were waited for; matrix products, arithmetic and copies ran while one was open for 0% of the time, Pallas kernels for 3%

profile of v3, /device:TPU:1, one launch (start us, length us, event | category | flops | bytes accessed | tf_op | source)
XLA Modules:
  0.0 113.3 jit_solution(2455317671952688981)
XLA Ops:
  0.6 2.5 %edges.1 = (f32[32,256]{1,0:T(8,128)S(1)}, f32[32,128]{1,0:T(8,128)S(1)}, f32[32,32,128]{2,1,0:T(8,128)S(1)}, f32[8,32,128]{2,1,0:T(8,128)S(1)}) custom-call(f32[32,32,128]{2,1,0:T(8,128)} %fine_hbm.1, f32[32,8,32]{2,1,0:T(8,128)} %coarse_hbm.1), custom_call_target="tpu_custom_call" | custom-call | tf_op jit(solution)/shard_map/edges/pallas_call | solution.py:179
  3.2 7.4 %collective-permute-start = (f32[32,256]{1,0:T(8,128)S(1)}, f32[32,256]{1,0:T(8,128)S(1)}, u32[]{:S(2)}, u32[]{:S(2)}) collective-permute-start(f32[32,256]{1,0:T(8,128)S(1)} %get-tuple-element.47), channel_id=1, source_target_pairs={{0,240},{16,0},{32,16},{48,32},{64,48},{80,64},{96,80},{112,96},{1... | collective-permute-start | bytes 98312 | tf_op jit(solution)/shard_map/ppermute | solution.py:54
  10.6 1.4 %collective-permute-start.2 = (f32[32,128]{1,0:T(8,128)S(1)}, f32[32,128]{1,0:T(8,128)S(1)}, u32[]{:S(2)}, u32[]{:S(2)}) collective-permute-start(f32[32,128]{1,0:T(8,128)S(1)} %get-tuple-element.48), channel_id=1, source_target_pairs={{0,255},{1,240},{2,241},{3,242},{4,243},{5,244},{6,245},{7,246},{8... | collective-permute-start | bytes 49160 | tf_op jit(solution)/shard_map/ppermute | solution.py:62
  12.0 3.2 %collective-permute-start.1 = (f32[32,128]{1,0:T(8,128)S(1)}, f32[32,128]{1,0:T(8,128)S(1)}, u32[]{:S(2)}, u32[]{:S(2)}) collective-permute-start(f32[32,128]{1,0:T(8,128)S(1)} %get-tuple-element.48), channel_id=1, source_target_pairs={{0,15},{1,0},{2,1},{3,2},{4,3},{5,4},{6,5},{7,6},{8,7},{9,8},{10,9... | collective-permute-start | bytes 49160 | tf_op jit(solution)/shard_map/ppermute | solution.py:56
  15.9 2.2 %prepare.1 = (f32[8,128]{1,0:T(8,128)S(1)}, bf16[512,64]{1,0:T(8,128)(2,1)S(1)}, bf16[64,512]{1,0:T(8,128)(2,1)S(1)}, bf16[512,512]{1,0:T(8,128)(2,1)S(1)}, bf16...) custom-call(s32[1,1,2]{2,1,0:T(1,128)S(1)} %copy-done.10, ...), custom_call_target="tpu_custom_call" | custom-call | tf_op jit(solution)/shard_map/prepare/pallas_call | solution.py:270
  19.1 5.1 %forward.1 = (bf16[64,4096]{1,0:T(8,128)(2,1)S(1)}, f32[512,4096]{1,0:T(8,128)S(1)}, f32[8,4096]{1,0:T(8,128)S(1)}, f32[8,128]{1,0:T(8,128)S(1)}, f32[8,128]{1,0...) custom-call(f32[8,128]{1,0:T(8,128)S(1)} %get-tuple-element.44.shift_ref, ...), custom_call_target="tpu_custom_call" | custom-call | tf_op jit(solution)/shard_map/forward/pallas_call | solution.py:377
  24.1 2.8 %collective-permute-start.3 = (f32[8,128]{1,0:T(8,128)S(1)}, f32[8,128]{1,0:T(8,128)S(1)}, u32[]{:S(2)}, u32[]{:S(2)}) collective-permute-start(f32[8,128]{1,0:T(8,128)S(1)} %get-tuple-element.57), channel_id=1, source_target_pairs={{0,16},{16,0},{32,48},{48,32},{64,80},{80,64},{96,112},{112,96},{1... | collective-permute-start | bytes 12296 | tf_op jit(solution)/shard_map/ppermute | solution.py:69
  26.9 1.4 %collective-permute-start.5 = (f32[8,128]{1,0:T(8,128)S(1)}, f32[8,128]{1,0:T(8,128)S(1)}, u32[]{:S(2)}, u32[]{:S(2)}) collective-permute-start(f32[8,128]{1,0:T(8,128)S(1)} %get-tuple-element.59), channel_id=1, source_target_pairs={{0,1},{1,0},{2,3},{3,2},{4,5},{5,4},{6,7},{7,6},{8,9},{9,8},{10,11... | collective-permute-start | bytes 12296 | tf_op jit(solution)/shard_map/ppermute | solution.py:69
  28.3 2.3 %collective-permute-start.6 = (f32[8,128]{1,0:T(8,128)S(1)}, f32[8,128]{1,0:T(8,128)S(1)}, u32[]{:S(2)}, u32[]{:S(2)}) collective-permute-start(f32[8,128]{1,0:T(8,128)S(1)} %get-tuple-element.60), channel_id=1, source_target_pairs={{0,15},{1,2},{2,1},{3,4},{4,3},{5,6},{6,5},{7,8},{8,7},{9,10},{10,... | collective-permute-start | bytes 12296 | tf_op jit(solution)/shard_map/ppermute | solution.py:69
  30.6 2.6 %collective-permute-done.4.row_two_ref = f32[8,128]{1,0:T(8,128)S(1)} collective-permute-done((f32[8,128]{1,0:T(8,128)S(1)}, f32[8,128]{1,0:T(8,128)S(1)}, u32[]{:S(2)}, u32[]{:S(2)}) %collective-permute-start.4) | collective-permute-done | bytes 4128 | tf_op jit(solution)/shard_map/ppermute | solution.py:69
  33.2 2.2 %collective-permute-done.6.col_two_ref = f32[8,128]{1,0:T(8,128)S(1)} collective-permute-done((f32[8,128]{1,0:T(8,128)S(1)}, f32[8,128]{1,0:T(8,128)S(1)}, u32[]{:S(2)}, u32[]{:S(2)}) %collective-permute-start.6) | collective-permute-done | bytes 4128 | tf_op jit(solution)/shard_map/ppermute | solution.py:69
  35.5 11.6 %backward.1 = (f32[16,80,128]{2,1,0:T(8,128)S(1)}, f32[16,80,128]{2,1,0:T(8,128)S(1)}, f32[32,32,128]{2,1,0:T(8,128)S(1)}, f32[8,32,128]{2,1,0:T(8,128)S(1)}, f3...) custom-call(f32[8,128]{1,0:T(8,128)S(1)} %get-tuple-element.44.shift_ref, ...), custom_call_target="tpu_custom_call" | custom-call | tf_op jit(solution)/shard_map/backward/pallas_call | solution.py:547
  47.1 2.0 %collective-permute-start.7 = (f32[16,80,128]{2,1,0:T(8,128)S(1)}, f32[16,80,128]{2,1,0:T(8,128)S(1)}, u32[]{:S(2)}, u32[]{:S(2)}) collective-permute-start(f32[16,80,128]{2,1,0:T(8,128)S(1)} %get-tuple-element.65), channel_id=1, source_target_pairs={{0,1},{1,0},{2,3},{3,2},{4,5},{5,4},{6,7},{7,6},{8,9},{9,8},{10,11... | collective-permute-start | bytes 1966088 | tf_op jit(solution)/shard_map/ppermute | solution.py:79
  49.2 1.7 %collective-permute-done.7 = f32[16,80,128]{2,1,0:T(8,128)S(1)} collective-permute-done((f32[16,80,128]{2,1,0:T(8,128)S(1)}, f32[16,80,128]{2,1,0:T(8,128)S(1)}, u32[]{:S(2)}, u32[]{:S(2)}) %collective-permute-start.7) | collective-permute-done | bytes 655392 | tf_op jit(solution)/shard_map/ppermute | solution.py:79
  51.0 2.6 %collective-permute-start.10 = (f32[4,80,128]{2,1,0:T(8,128)S(1)}, f32[4,80,128]{2,1,0:T(8,128)S(1)}, u32[]{:S(2)}, u32[]{:S(2)}) collective-permute-start(f32[4,80,128]{2,1,0:T(8,128)S(1)} %get-tuple-element.83), channel_id=1, source_target_pairs={{0,48},{16,32},{32,16},{48,0},{1,49},{17,33},{33,17},{49,1},{2,50}... | collective-permute-start | bytes 491528 | tf_op jit(solution)/shard_map/ppermute | solution.py:79
  54.5 1.8 %collective-permute-start.12 = (f32[32,128]{1,0:T(8,128)S(1)}, f32[32,128]{1,0:T(8,128)S(1)}, u32[]{:S(2)}, u32[]{:S(2)}) collective-permute-start(f32[32,128]{1,0:T(8,128)S(1)} %get-tuple-element.67), channel_id=1, source_target_pairs={{0,1},{1,2},{2,3},{3,4},{4,5},{5,6},{6,7},{7,8},{8,9},{9,10},{10,1... | collective-permute-start | bytes 49160 | tf_op jit(solution)/shard_map/ppermute | solution.py:56
  56.6 3.7 %collective-permute-done.10 = f32[4,80,128]{2,1,0:T(8,128)S(1)} collective-permute-done((f32[4,80,128]{2,1,0:T(8,128)S(1)}, f32[4,80,128]{2,1,0:T(8,128)S(1)}, u32[]{:S(2)}, u32[]{:S(2)}) %collective-permute-start.10) | collective-permute-done | bytes 163872 | tf_op jit(solution)/shard_map/ppermute | solution.py:79
  60.3 1.5 %collective-permute-done.8 = f32[4,80,128]{2,1,0:T(8,128)S(1)} collective-permute-done((f32[4,80,128]{2,1,0:T(8,128)S(1)}, f32[4,80,128]{2,1,0:T(8,128)S(1)}, u32[]{:S(2)}, u32[]{:S(2)}) %collective-permute-start.8) | collective-permute-done | bytes 163872 | tf_op jit(solution)/shard_map/ppermute | solution.py:79
  61.9 1.8 %collective-permute-done.13.corner_ref = f32[32,128]{1,0:T(8,128)S(1)} collective-permute-done((f32[32,128]{1,0:T(8,128)S(1)}, f32[32,128]{1,0:T(8,128)S(1)}, u32[]{:S(2)}, u32[]{:S(2)}) %collective-permute-start.13) | collective-permute-done | bytes 16416 | tf_op jit(solution)/shard_map/ppermute | solution.py:62
  63.7 4.6 %collective-permute-done.11.row_ref = f32[32,256]{1,0:T(8,128)S(1)} collective-permute-done((f32[32,256]{1,0:T(8,128)S(1)}, f32[32,256]{1,0:T(8,128)S(1)}, u32[]{:S(2)}, u32[]{:S(2)}) %collective-permute-start.11) | collective-permute-done | bytes 32800 | tf_op jit(solution)/shard_map/ppermute | solution.py:54
  68.8 2.9 %collective-permute-start.14 = (f32[80,128]{1,0:T(8,128)S(1)}, f32[80,128]{1,0:T(8,128)S(1)}, u32[]{:S(2)}, u32[]{:S(2)}) collective-permute-start(f32[80,128]{1,0:T(8,128)S(1)} %get-tuple-element.88), channel_id=1, source_target_pairs={{0,4},{4,0},{8,12},{12,8},{1,5},{5,1},{9,13},{13,9},{2,6},{6,2},{1... | collective-permute-start | bytes 122888 | tf_op jit(solution)/shard_map/ppermute | solution.py:79
  74.5 1.7 %collective-permute-start.17 = (f32[88,128]{1,0:T(8,128)S(1)}, f32[88,128]{1,0:T(8,128)S(1)}, u32[]{:S(2)}, u32[]{:S(2)}) collective-permute-start(f32[88,128]{1,0:T(8,128)S(1)} %pad_maximum_fusion.1), channel_id=1, source_target_pairs={{0,64},{64,0},{128,192},{192,128},{1,65},{65,1},{129,193},{193,129... | collective-permute-start | bytes 135176 | tf_op jit(solution)/shard_map/ppermute | solution.py:79
  76.3 1.2 %collective-permute-done.18 = f32[88,128]{1,0:T(8,128)S(1)} collective-permute-done((f32[88,128]{1,0:T(8,128)S(1)}, f32[88,128]{1,0:T(8,128)S(1)}, u32[]{:S(2)}, u32[]{:S(2)}) %collective-permute-start.18) | collective-permute-done | bytes 45088 | tf_op jit(solution)/shard_map/ppermute | solution.py:79
  78.4 5.5 %collective-permute-start.20 = (f32[88,128]{1,0:T(8,128)S(1)}, f32[88,128]{1,0:T(8,128)S(1)}, u32[]{:S(2)}, u32[]{:S(2)}) collective-permute-start(f32[88,128]{1,0:T(8,128)S(1)} %add_add_fusion.one_ref), channel_id=1, source_target_pairs={{0,2},{2,0},{1,3},{3,1},{4,6},{6,4},{5,7},{7,5},{8,10},{10,8},{9,1... | collective-permute-start | bytes 135176 | tf_op jit(solution)/shard_map/ppermute | solution.py:79
  83.9 2.0 %collective-permute-done.20.two_ref = f32[88,128]{1,0:T(8,128)S(1)} collective-permute-done((f32[88,128]{1,0:T(8,128)S(1)}, f32[88,128]{1,0:T(8,128)S(1)}, u32[]{:S(2)}, u32[]{:S(2)}) %collective-permute-start.20) | collective-permute-done | bytes 45088 | tf_op jit(solution)/shard_map/ppermute | solution.py:79
  86.0 1.5 %collective-permute-start.23 = (f32[88,128]{1,0:T(8,128)S(1)}, f32[88,128]{1,0:T(8,128)S(1)}, u32[]{:S(2)}, u32[]{:S(2)}) collective-permute-start(f32[88,128]{1,0:T(8,128)S(1)} %tally.1), channel_id=1, source_target_pairs={{0,12},{4,8},{8,4},{12,0},{1,13},{5,9},{9,5},{13,1},{2,14},{6,10},... | collective-permute-start | bytes 135176 | tf_op jit(solution)/shard_map/ppermute | solution.py:79
  90.4 1.5 %collective-permute-done.22 = f32[88,128]{1,0:T(8,128)S(1)} collective-permute-done((f32[88,128]{1,0:T(8,128)S(1)}, f32[88,128]{1,0:T(8,128)S(1)}, u32[]{:S(2)}, u32[]{:S(2)}) %collective-permute-start.22) | collective-permute-done | bytes 45088 | tf_op jit(solution)/shard_map/ppermute | solution.py:79
  92.6 2.7 %collective-permute-start.24 = (f32[4,88,128]{2,1,0:T(8,128)S(1)}, f32[4,88,128]{2,1,0:T(8,128)S(1)}, u32[]{:S(2)}, u32[]{:S(2)}) collective-permute-start(f32[4,88,128]{2,1,0:T(8,128)S(1)} %pad_maximum_fusion), channel_id=1, source_target_pairs={{0,16},{16,0},{32,48},{48,32},{1,17},{17,1},{33,49},{49,33},{2,18}... | collective-permute-start | bytes 540680 | tf_op jit(solution)/shard_map/ppermute | solution.py:79
  95.3 4.8 %collective-permute-done.24 = f32[4,88,128]{2,1,0:T(8,128)S(1)} collective-permute-done((f32[4,88,128]{2,1,0:T(8,128)S(1)}, f32[4,88,128]{2,1,0:T(8,128)S(1)}, u32[]{:S(2)}, u32[]{:S(2)}) %collective-permute-start.24) | collective-permute-done | bytes 180256 | tf_op jit(solution)/shard_map/ppermute | solution.py:79
  100.2 9.0 %collective-permute-start.27 = (f32[16,88,128]{2,1,0:T(8,128)S(1)}, f32[16,88,128]{2,1,0:T(8,128)S(1)}, u32[]{:S(2)}, u32[]{:S(2)}) collective-permute-start(f32[16,88,128]{2,1,0:T(8,128)S(1)} %constant_dynamic-update-slice_fusion.refs_0_), channel_id=1, source_target_pairs={{0,1},{1,0},{2,3},{3,2},{4,5},{5,4},{6,7},{7,6},{8,9},{9,8},{10,11... | collective-permute-start | bytes 2162696 | tf_op jit(solution)/shard_map/ppermute | solution.py:79
  109.2 1.8 %collective-permute-done.27.refs_1_ = f32[16,88,128]{2,1,0:T(8,128)S(1)} collective-permute-done((f32[16,88,128]{2,1,0:T(8,128)S(1)}, f32[16,88,128]{2,1,0:T(8,128)S(1)}, u32[]{:S(2)}, u32[]{:S(2)}) %collective-permute-start.27) | collective-permute-done | bytes 720928 | tf_op jit(solution)/shard_map/ppermute | solution.py:79
  111.1 2.2 %steps.1 = (f32[512,512]{1,0:T(8,128)}, f32[64,512]{1,0:T(8,128)}, f32[3,512]{1,0:T(4,128)}, f32[32,32,128]{2,1,0:T(8,128)}, f32[32,8,32]{2,1,0:T(8,128)}) custom-call(f32[16,88,128]{2,1,0:T(8,128)S(1)} %constant_dynamic-update-slice_fusion.refs_0_, f32[16,88,128]{2,1,0:T(8,128)S(1)} %collective-permute-done.27.refs_1_, ...), custom_call_target="tpu_custom_call" | custom-call | tf_op jit(solution)/shard_map/steps/pallas_call | solution.py:687
  (68 shorter events, 11.0 us)
Async XLA Ops:
  3.2 15.9 %collective-permute-start = (f32[32,256]{1,0:T(8,128)S(1)}, f32[32,256]{1,0:T(8,128)S(1)}, u32[]{:S(2)}, u32[]{:S(2)}) collective-permute-start(f32[32,256]{1,0:T(8,128)S(1)} %get-tuple-element.47), channel_id=1, source_target_pairs={{0,240},{16,0},{32,16},{48,32},{64,48},{80,64},{96,80},{112,96},{1... | collective-permute-start | bytes 98312 | tf_op jit(solution)/shard_map/ppermute | solution.py:54
  10.6 8.0 %collective-permute-start.2 = (f32[32,128]{1,0:T(8,128)S(1)}, f32[32,128]{1,0:T(8,128)S(1)}, u32[]{:S(2)}, u32[]{:S(2)}) collective-permute-start(f32[32,128]{1,0:T(8,128)S(1)} %get-tuple-element.48), channel_id=1, source_target_pairs={{0,255},{1,240},{2,241},{3,242},{4,243},{5,244},{6,245},{7,246},{8... | collective-permute-start | bytes 49160 | tf_op jit(solution)/shard_map/ppermute | solution.py:62
  12.0 7.1 %collective-permute-start.1 = (f32[32,128]{1,0:T(8,128)S(1)}, f32[32,128]{1,0:T(8,128)S(1)}, u32[]{:S(2)}, u32[]{:S(2)}) collective-permute-start(f32[32,128]{1,0:T(8,128)S(1)} %get-tuple-element.48), channel_id=1, source_target_pairs={{0,15},{1,0},{2,1},{3,2},{4,3},{5,4},{6,5},{7,6},{8,7},{9,8},{10,9... | collective-permute-start | bytes 49160 | tf_op jit(solution)/shard_map/ppermute | solution.py:56
  24.1 6.5 %collective-permute-start.3 = (f32[8,128]{1,0:T(8,128)S(1)}, f32[8,128]{1,0:T(8,128)S(1)}, u32[]{:S(2)}, u32[]{:S(2)}) collective-permute-start(f32[8,128]{1,0:T(8,128)S(1)} %get-tuple-element.57), channel_id=1, source_target_pairs={{0,16},{16,0},{32,48},{48,32},{64,80},{80,64},{96,112},{112,96},{1... | collective-permute-start | bytes 12296 | tf_op jit(solution)/shard_map/ppermute | solution.py:69
  26.9 6.4 %collective-permute-start.4 = (f32[8,128]{1,0:T(8,128)S(1)}, f32[8,128]{1,0:T(8,128)S(1)}, u32[]{:S(2)}, u32[]{:S(2)}) collective-permute-start(f32[8,128]{1,0:T(8,128)S(1)} %get-tuple-element.58), channel_id=1, source_target_pairs={{0,240},{16,32},{32,16},{48,64},{64,48},{80,96},{96,80},{112,128},... | collective-permute-start | bytes 12296 | tf_op jit(solution)/shard_map/ppermute | solution.py:69
  26.9 6.4 %collective-permute-start.5 = (f32[8,128]{1,0:T(8,128)S(1)}, f32[8,128]{1,0:T(8,128)S(1)}, u32[]{:S(2)}, u32[]{:S(2)}) collective-permute-start(f32[8,128]{1,0:T(8,128)S(1)} %get-tuple-element.59), channel_id=1, source_target_pairs={{0,1},{1,0},{2,3},{3,2},{4,5},{5,4},{6,7},{7,6},{8,9},{9,8},{10,11... | collective-permute-start | bytes 12296 | tf_op jit(solution)/shard_map/ppermute | solution.py:69
  28.3 7.1 %collective-permute-start.6 = (f32[8,128]{1,0:T(8,128)S(1)}, f32[8,128]{1,0:T(8,128)S(1)}, u32[]{:S(2)}, u32[]{:S(2)}) collective-permute-start(f32[8,128]{1,0:T(8,128)S(1)} %get-tuple-element.60), channel_id=1, source_target_pairs={{0,15},{1,2},{2,1},{3,4},{4,3},{5,6},{6,5},{7,8},{8,7},{9,10},{10,... | collective-permute-start | bytes 12296 | tf_op jit(solution)/shard_map/ppermute | solution.py:69
  35.4 75.6 %copy-start.1 = (f32[1,512,512]{2,1,0:T(8,128)S(1)}, f32[1,512,512]{2,1,0:T(8,128)}, u32[]{:S(2)}) copy-start(f32[1,512,512]{2,1,0:T(8,128)} %param.31) | copy-start | bytes 3145732
  35.4 75.6 %copy-start.2 = (f32[32,32,128]{2,1,0:T(8,128)S(1)}, f32[32,32,128]{2,1,0:T(8,128)}, u32[]{:S(2)}) copy-start(f32[32,32,128]{2,1,0:T(8,128)} %refs_10_.1) | copy-start | bytes 1572868
  35.4 75.6 %copy-start.3 = (f32[32,32,128]{2,1,0:T(8,128)S(1)}, f32[32,32,128]{2,1,0:T(8,128)}, u32[]{:S(2)}) copy-start(f32[32,32,128]{2,1,0:T(8,128)} %refs_11_.1) | copy-start | bytes 1572868
  35.4 75.6 %copy-start.4 = (f32[512,64]{0,1:T(8,128)S(1)}, f32[512,64]{0,1:T(8,128)}, u32[]{:S(2)}) copy-start(f32[512,64]{0,1:T(8,128)} %param.28) | copy-start | bytes 393220
  47.1 3.7 %collective-permute-start.7 = (f32[16,80,128]{2,1,0:T(8,128)S(1)}, f32[16,80,128]{2,1,0:T(8,128)S(1)}, u32[]{:S(2)}, u32[]{:S(2)}) collective-permute-start(f32[16,80,128]{2,1,0:T(8,128)S(1)} %get-tuple-element.65), channel_id=1, source_target_pairs={{0,1},{1,0},{2,3},{3,2},{4,5},{5,4},{6,7},{7,6},{8,9},{9,8},{10,11... | collective-permute-start | bytes 1966088 | tf_op jit(solution)/shard_map/ppermute | solution.py:79
  51.0 9.3 %collective-permute-start.10 = (f32[4,80,128]{2,1,0:T(8,128)S(1)}, f32[4,80,128]{2,1,0:T(8,128)S(1)}, u32[]{:S(2)}, u32[]{:S(2)}) collective-permute-start(f32[4,80,128]{2,1,0:T(8,128)S(1)} %get-tuple-element.83), channel_id=1, source_target_pairs={{0,48},{16,32},{32,16},{48,0},{1,49},{17,33},{33,17},{49,1},{2,50}... | collective-permute-start | bytes 491528 | tf_op jit(solution)/shard_map/ppermute | solution.py:79
  53.6 6.7 %collective-permute-start.9 = (f32[4,80,128]{2,1,0:T(8,128)S(1)}, f32[4,80,128]{2,1,0:T(8,128)S(1)}, u32[]{:S(2)}, u32[]{:S(2)}) collective-permute-start(f32[4,80,128]{2,1,0:T(8,128)S(1)} %get-tuple-element.84), channel_id=1, source_target_pairs={{0,32},{16,48},{32,0},{48,16},{1,33},{17,49},{33,1},{49,17},{2,34}... | collective-permute-start | bytes 491528 | tf_op jit(solution)/shard_map/ppermute | solution.py:79
  54.0 7.8 %collective-permute-start.8 = (f32[4,80,128]{2,1,0:T(8,128)S(1)}, f32[4,80,128]{2,1,0:T(8,128)S(1)}, u32[]{:S(2)}, u32[]{:S(2)}) collective-permute-start(f32[4,80,128]{2,1,0:T(8,128)S(1)} %get-tuple-element.85), channel_id=1, source_target_pairs={{0,16},{16,0},{32,48},{48,32},{1,17},{17,1},{33,49},{49,33},{2,18}... | collective-permute-start | bytes 491528 | tf_op jit(solution)/shard_map/ppermute | solution.py:79
  54.5 7.4 %collective-permute-start.12 = (f32[32,128]{1,0:T(8,128)S(1)}, f32[32,128]{1,0:T(8,128)S(1)}, u32[]{:S(2)}, u32[]{:S(2)}) collective-permute-start(f32[32,128]{1,0:T(8,128)S(1)} %get-tuple-element.67), channel_id=1, source_target_pairs={{0,1},{1,2},{2,3},{3,4},{4,5},{5,6},{6,7},{7,8},{8,9},{9,10},{10,1... | collective-permute-start | bytes 49160 | tf_op jit(solution)/shard_map/ppermute | solution.py:56
  56.3 7.4 %collective-permute-start.13 = (f32[32,128]{1,0:T(8,128)S(1)}, f32[32,128]{1,0:T(8,128)S(1)}, u32[]{:S(2)}, u32[]{:S(2)}) collective-permute-start(f32[32,128]{1,0:T(8,128)S(1)} %get-tuple-element.68), channel_id=1, source_target_pairs={{0,17},{1,18},{2,19},{3,20},{4,21},{5,22},{6,23},{7,24},{8,25},{9,... | collective-permute-start | bytes 49160 | tf_op jit(solution)/shard_map/ppermute | solution.py:62
  60.3 8.0 %collective-permute-start.11 = (f32[32,256]{1,0:T(8,128)S(1)}, f32[32,256]{1,0:T(8,128)S(1)}, u32[]{:S(2)}, u32[]{:S(2)}) collective-permute-start(f32[32,256]{1,0:T(8,128)S(1)} %get-tuple-element.66), channel_id=1, source_target_pairs={{0,16},{16,32},{32,48},{48,64},{64,80},{80,96},{96,112},{112,128},... | collective-permute-start | bytes 98312 | tf_op jit(solution)/shard_map/ppermute | solution.py:54
  68.3 4.2 %collective-permute-start.16 = (f32[80,128]{1,0:T(8,128)S(1)}, f32[80,128]{1,0:T(8,128)S(1)}, u32[]{:S(2)}, u32[]{:S(2)}) collective-permute-start(f32[80,128]{1,0:T(8,128)S(1)} %get-tuple-element.86), channel_id=1, source_target_pairs={{0,12},{4,8},{8,4},{12,0},{1,13},{5,9},{9,5},{13,1},{2,14},{6,10},... | collective-permute-start | bytes 122888 | tf_op jit(solution)/shard_map/ppermute | solution.py:79
  68.8 4.4 %collective-permute-start.15 = (f32[80,128]{1,0:T(8,128)S(1)}, f32[80,128]{1,0:T(8,128)S(1)}, u32[]{:S(2)}, u32[]{:S(2)}) collective-permute-start(f32[80,128]{1,0:T(8,128)S(1)} %get-tuple-element.87), channel_id=1, source_target_pairs={{0,8},{4,12},{8,0},{12,4},{1,9},{5,13},{9,1},{13,5},{2,10},{6,14},... | collective-permute-start | bytes 122888 | tf_op jit(solution)/shard_map/ppermute | solution.py:79
  68.8 4.7 %collective-permute-start.14 = (f32[80,128]{1,0:T(8,128)S(1)}, f32[80,128]{1,0:T(8,128)S(1)}, u32[]{:S(2)}, u32[]{:S(2)}) collective-permute-start(f32[80,128]{1,0:T(8,128)S(1)} %get-tuple-element.88), channel_id=1, source_target_pairs={{0,4},{4,0},{8,12},{12,8},{1,5},{5,1},{9,13},{13,9},{2,6},{6,2},{1... | collective-permute-start | bytes 122888 | tf_op jit(solution)/shard_map/ppermute | solution.py:79
  73.5 3.9 %collective-permute-start.18 = (f32[88,128]{1,0:T(8,128)S(1)}, f32[88,128]{1,0:T(8,128)S(1)}, u32[]{:S(2)}, u32[]{:S(2)}) collective-permute-start(f32[88,128]{1,0:T(8,128)S(1)} %pad_maximum_fusion.1), channel_id=1, source_target_pairs={{0,128},{64,192},{128,0},{192,64},{1,129},{65,193},{129,1},{193,65... | collective-permute-start | bytes 135176 | tf_op jit(solution)/shard_map/ppermute | solution.py:79
  73.6 4.8 %collective-permute-start.19 = (f32[88,128]{1,0:T(8,128)S(1)}, f32[88,128]{1,0:T(8,128)S(1)}, u32[]{:S(2)}, u32[]{:S(2)}) collective-permute-start(f32[88,128]{1,0:T(8,128)S(1)} %pad_maximum_fusion.1), channel_id=1, source_target_pairs={{0,192},{64,128},{128,64},{192,0},{1,193},{65,129},{129,65},{193,1... | collective-permute-start | bytes 135176 | tf_op jit(solution)/shard_map/ppermute | solution.py:79
  74.5 3.9 %collective-permute-start.17 = (f32[88,128]{1,0:T(8,128)S(1)}, f32[88,128]{1,0:T(8,128)S(1)}, u32[]{:S(2)}, u32[]{:S(2)}) collective-permute-start(f32[88,128]{1,0:T(8,128)S(1)} %pad_maximum_fusion.1), channel_id=1, source_target_pairs={{0,64},{64,0},{128,192},{192,128},{1,65},{65,1},{129,193},{193,129... | collective-permute-start | bytes 135176 | tf_op jit(solution)/shard_map/ppermute | solution.py:79
  78.4 7.5 %collective-permute-start.20 = (f32[88,128]{1,0:T(8,128)S(1)}, f32[88,128]{1,0:T(8,128)S(1)}, u32[]{:S(2)}, u32[]{:S(2)}) collective-permute-start(f32[88,128]{1,0:T(8,128)S(1)} %add_add_fusion.one_ref), channel_id=1, source_target_pairs={{0,2},{2,0},{1,3},{3,1},{4,6},{6,4},{5,7},{7,5},{8,10},{10,8},{9,1... | collective-permute-start | bytes 135176 | tf_op jit(solution)/shard_map/ppermute | solution.py:79
  86.0 4.4 %collective-permute-start.23 = (f32[88,128]{1,0:T(8,128)S(1)}, f32[88,128]{1,0:T(8,128)S(1)}, u32[]{:S(2)}, u32[]{:S(2)}) collective-permute-start(f32[88,128]{1,0:T(8,128)S(1)} %tally.1), channel_id=1, source_target_pairs={{0,12},{4,8},{8,4},{12,0},{1,13},{5,9},{9,5},{13,1},{2,14},{6,10},... | collective-permute-start | bytes 135176 | tf_op jit(solution)/shard_map/ppermute | solution.py:79
  87.5 4.4 %collective-permute-start.22 = (f32[88,128]{1,0:T(8,128)S(1)}, f32[88,128]{1,0:T(8,128)S(1)}, u32[]{:S(2)}, u32[]{:S(2)}) collective-permute-start(f32[88,128]{1,0:T(8,128)S(1)} %tally.1), channel_id=1, source_target_pairs={{0,8},{4,12},{8,0},{12,4},{1,9},{5,13},{9,1},{13,5},{2,10},{6,14},... | collective-permute-start | bytes 135176 | tf_op jit(solution)/shard_map/ppermute | solution.py:79
  88.3 3.6 %collective-permute-start.21 = (f32[88,128]{1,0:T(8,128)S(1)}, f32[88,128]{1,0:T(8,128)S(1)}, u32[]{:S(2)}, u32[]{:S(2)}) collective-permute-start(f32[88,128]{1,0:T(8,128)S(1)} %tally.1), channel_id=1, source_target_pairs={{0,4},{4,0},{8,12},{12,8},{1,5},{5,1},{9,13},{13,9},{2,6},{6,2},{1... | collective-permute-start | bytes 135176 | tf_op jit(solution)/shard_map/ppermute | solution.py:79
  92.0 8.2 %collective-permute-start.26 = (f32[4,88,128]{2,1,0:T(8,128)S(1)}, f32[4,88,128]{2,1,0:T(8,128)S(1)}, u32[]{:S(2)}, u32[]{:S(2)}) collective-permute-start(f32[4,88,128]{2,1,0:T(8,128)S(1)} %pad_maximum_fusion), channel_id=1, source_target_pairs={{0,48},{16,32},{32,16},{48,0},{1,49},{17,33},{33,17},{49,1},{2,50}... | collective-permute-start | bytes 540680 | tf_op jit(solution)/shard_map/ppermute | solution.py:79
  92.5 7.6 %collective-permute-start.25 = (f32[4,88,128]{2,1,0:T(8,128)S(1)}, f32[4,88,128]{2,1,0:T(8,128)S(1)}, u32[]{:S(2)}, u32[]{:S(2)}) collective-permute-start(f32[4,88,128]{2,1,0:T(8,128)S(1)} %pad_maximum_fusion), channel_id=1, source_target_pairs={{0,32},{16,48},{32,0},{48,16},{1,33},{17,49},{33,1},{49,17},{2,34}... | collective-permute-start | bytes 540680 | tf_op jit(solution)/shard_map/ppermute | solution.py:79
  92.6 7.6 %collective-permute-start.24 = (f32[4,88,128]{2,1,0:T(8,128)S(1)}, f32[4,88,128]{2,1,0:T(8,128)S(1)}, u32[]{:S(2)}, u32[]{:S(2)}) collective-permute-start(f32[4,88,128]{2,1,0:T(8,128)S(1)} %pad_maximum_fusion), channel_id=1, source_target_pairs={{0,16},{16,0},{32,48},{48,32},{1,17},{17,1},{33,49},{49,33},{2,18}... | collective-permute-start | bytes 540680 | tf_op jit(solution)/shard_map/ppermute | solution.py:79
  100.2 10.8 %collective-permute-start.27 = (f32[16,88,128]{2,1,0:T(8,128)S(1)}, f32[16,88,128]{2,1,0:T(8,128)S(1)}, u32[]{:S(2)}, u32[]{:S(2)}) collective-permute-start(f32[16,88,128]{2,1,0:T(8,128)S(1)} %constant_dynamic-update-slice_fusion.refs_0_), channel_id=1, source_target_pairs={{0,1},{1,0},{2,3},{3,2},{4,5},{5,4},{6,7},{7,6},{8,9},{9,8},{10,11... | collective-permute-start | bytes 2162696 | tf_op jit(solution)/shard_map/ppermute | solution.py:79
  (7 other events, 454.3 us)

commit v4 on v3

--- a/solution.py
+++ b/solution.py
@@ -29,6 +29,8 @@
 WIDTH = SR * SC // CHAINS
 LINES = SR // CHAINS
 PARTS = 2
+FINE_CORNER = 64
+COARSE_CORNER = 65
 F32 = jnp.float32
 BF16 = jnp.bfloat16
 MIB = 1 << 20
@@ -66,7 +68,8 @@
     size = axes_size(axes)
     one = [(i, i ^ 1) for i in range(size)]
     two = [(i, (i + 1 if i % 2 else i - 1) % size) for i in range(size)]
-    return lax.ppermute(block_one, axes, one), lax.ppermute(block_two, axes, two)
+    block_two = lax.ppermute(block_two, axes, two)
+    return lax.ppermute(block_one, axes, one), block_two
 
 
 def at_ends():
@@ -90,8 +93,8 @@
     return pair_sum([block] + [swapped(block, axis, d) for d in range(1, lax.axis_size(axis))])
 
 
-def exchange_gather(block, axis):
-    return [block] + [swapped(block, axis, d) for d in range(1, lax.axis_size(axis))]
+def all_to_all(blocks):
+    return lax.all_to_all(blocks, ("x", "y"), 0, 0, tiled=True)
 
 
 def scatter_sum(blocks, axis):
@@ -433,7 +436,6 @@
     coarse_ref,
     row_ref,
     col_ref,
-    corner_ref,
     cot,
     grad_mid,
     grad_in,
@@ -504,7 +506,7 @@
     bands.append(upper)
     line = prior * shift_y
     row_ref[:, 0:SC] = along(line)
-    corner = jnp.where(lane == 0, spread_lane(line * shift_x, SC - 1), 0.0)
+    ends = jnp.where(lane == FINE_CORNER, spread_lane(line * shift_x, SC - 1), ends)
     spread = dot(
         jnp.concatenate(bands, axis=0),
         coarse_table(shift_x),
@@ -516,10 +518,9 @@
         band = spread[i * CH : i * CH + CH]
         coarse_ref[i] = jnp.where(lane < CC, band, 0.0)
         ends = jnp.where(lane == SR + i, spread_lane(band, CC), ends)
-    col_ref[...] = ends
     band = spread[CR * CH :]
     row_ref[:, SC:] = jnp.where(lane < CC, band, 0.0)
-    corner_ref[...] = jnp.where(lane == SR, spread_lane(band, CC), corner)
+    col_ref[...] = jnp.where(lane == COARSE_CORNER, spread_lane(band, CC), ends)
     core = lax.axis_index("c")
     tile = axes_index(("x", "y"))
     for d in range(16):
@@ -541,7 +542,6 @@
         jax.ShapeDtypeStruct((SR, CH, SC), F32),
         jax.ShapeDtypeStruct((CR, CH, SC), F32),
         jax.ShapeDtypeStruct((CH, 2 * SC), F32),
-        jax.ShapeDtypeStruct((CH, SC), F32),
         jax.ShapeDtypeStruct((CH, SC), F32),
     )
     return pl.pallas_call(
@@ -560,32 +560,50 @@
     )(*args)
 
 
-def join_kernel(fine_ref, coarse_ref, row_ref, col_ref, corner_ref, fine_out, coarse_out, total_ref):
+def turn_kernel(row_ref, col_ref, out_ref):
+    lane = lane_ids(CH)
+    unused_first_row, unused_last_row, first_col, unused_last_col = at_ends()
+    cols = jnp.where(first_col, 0.0, col_ref[...])
+    fine = jnp.where(lane == 0, spread_lane(cols, FINE_CORNER), 0.0)
+    coarse = jnp.where(lane == 0, spread_lane(cols, COARSE_CORNER), 0.0)
+    out_ref[:, 0:SC] = row_ref[:, 0:SC] + fine
+    out_ref[:, SC:] = row_ref[:, SC:] + coarse
+
+
+def turn(row_out, col_in):
+    return pl.pallas_call(
+        turn_kernel,
+        out_shape=jax.ShapeDtypeStruct(row_out.shape, F32),
+        in_specs=[vmem(), vmem()],
+        out_specs=vmem(),
+        compiler_params=pltpu.CompilerParams(vmem_limit_bytes=4 * MIB),
+        name="turn",
+    )(row_out, col_in)
+
+
+def join_kernel(fine_ref, coarse_ref, row_ref, col_ref, fine_out, coarse_out, total_ref):
     lane = lane_ids(CH)
     first_row, unused_last_row, first_col, unused_last_col = at_ends()
     rows = jnp.where(first_row, 0.0, row_ref[...])
     cols = jnp.where(first_col, 0.0, col_ref[...])
-    corner = jnp.where(jnp.logical_or(first_row, first_col), 0.0, corner_ref[...])
     total = jnp.zeros((CH, SC), F32)
     for i in range(SR):
         line = fine_ref[i] + jnp.where(lane == 0, spread_lane(cols, i), 0.0)
         if i == 0:
             line += rows[:, 0:SC]
-            line += jnp.where(lane == 0, spread_lane(corner, 0), 0.0)
         fine_out[:, i, :] = line
         total += line * line
     for i in range(CR):
         line = coarse_ref[i] + jnp.where(lane == 0, spread_lane(cols, SR + i), 0.0)
         if i == 0:
             line += rows[:, SC:]
-            line += jnp.where(lane == 0, spread_lane(corner, SR), 0.0)
         coarse_out[:, i, :] = line[:, 0:CC]
         total += line * line
     total = jnp.sum(jnp.sum(total, axis=0, keepdims=True), axis=1, keepdims=True)
     total_ref[...] = jnp.broadcast_to(total, (8, SC))
 
 
-def join(fine, coarse, row_in, col_in, corner_in):
+def join(fine, coarse, row_in, col_in):
     return pl.pallas_call(
         join_kernel,
         out_shape=(
@@ -593,11 +611,11 @@
             jax.ShapeDtypeStruct((CH, CR, CC), F32),
             jax.ShapeDtypeStruct((8, SC), F32),
         ),
-        in_specs=[vmem()] * 5,
+        in_specs=[vmem()] * 4,
         out_specs=(vmem(),) * 3,
         compiler_params=pltpu.CompilerParams(vmem_limit_bytes=8 * MIB),
         name="join",
-    )(fine, coarse, row_in, col_in, corner_in)
+    )(fine, coarse, row_in, col_in)
 
 
 def clip_factor(total, entries):
@@ -641,7 +659,6 @@
     grid_entries,
 ):
     core = lax.axis_index("c")
-    tile = axes_index(("x", "y"))
     step = pl.program_id(0)
 
     @pl.when(step == 0)
@@ -652,7 +669,7 @@
         scales[0:1, :] = clip_factor(totals[0:1, :], grid_entries)
         scales[1:2, :] = clip_factor(totals[1:2, :], decoder_entries)
         for block in range(4):
-            d = tile ^ (block % 2)
+            d = block % 2
             data = jnp.where(block // 2 == core, own_ref[d, 72:80, :], other_ref[d, 72:80, :])
             cols = slice(block * 128, block * 128 + 128)
             out_ref[:, cols] = adam_step(
@@ -663,7 +680,7 @@
     scale = scales[1:2, :]
     for k in range(8 // PARTS):
         for block in range(4):
-            d = tile ^ ((step * (8 // PARTS) + k) * 2 + block % 2)
+            d = (step * (8 // PARTS) + k) * 2 + block % 2
             data = jnp.where(block // 2 == core, own_ref[d, 0:72, :], other_ref[d, 0:72, :])
             at = (slice(k * 64, k * 64 + 64), slice(block * 128, block * 128 + 128))
             mid_ref[at] = adam_step(data[0:64], mid_one_ref[at], mid_two_ref[at], scale)
@@ -719,36 +736,37 @@
     )(one, two)
 
 
-def reduce_grads(keep, send, fine, coarse, halos):
+def reduce_grads(keep, send, fine, coarse, row_out, col_in):
     part = keep + swapped(send, "c", 1)
     part = scatter_sum([part[d * 4 : d * 4 + 4] for d in range(4)], "x")
-    part, *halos = lax.optimization_barrier((part, *halos))
-    fine, coarse, grid_local = join(fine, coarse, *halos)
+    part, col_in = lax.optimization_barrier((part, col_in))
+    row_in = shifted(turn(row_out, col_in), 1, 0)
     part = scatter_sum([part[d] for d in range(4)], "y")
+    fine, coarse, grid_local = join(fine, coarse, row_in, col_in)
     part = exchange_sum(jnp.concatenate([part, grid_local]), "zl")
-    part = tally(part, swapped(part, "zh", 1))
-    own = jnp.stack(exchange_gather(part, "y"))
-    own = jnp.concatenate(exchange_gather(own, "x"))
+    across = [(i, i ^ 5) for i in range(axes_size(("zl", "zh")))]
+    part = tally(part, lax.ppermute(part, ("zl", "zh"), across))
+    own = all_to_all(jnp.broadcast_to(part, (16, *part.shape)))
     return own, swapped(own, "c", 1), fine, coarse
 
 
 def local_grads(offsets, targets, grid_fine, grid_coarse, weight_in, weight_mid, weight_out):
     row_out, col_out, fine_lines, coarse_lines = edges(grid_fine, grid_coarse)
+    corner_in = shifted(col_out, -1, -1)
+    col_in = shifted(col_out, 0, -1)
     row_in = shifted(row_out, -1, 0)
-    col_in = shifted(col_out, 0, -1)
-    corner_in = shifted(col_out, -1, -1)
     shifts, low_in, in_turned, low_mid, mid_turned, low_out, out_turned, lines, ends = prepare(
         offsets, weight_in.T, weight_mid[0], weight_out, targets
     )
     feat, pre, pred, row_one, row_two, col_one, col_two = forward(
         shifts, fine_lines, coarse_lines, row_in, col_in, corner_in, lines, ends, low_in, low_mid, low_out
     )
-    halos = (*meetings(row_one, row_two, ROW), *meetings(col_one, col_two, COL))
-    keep, send, fine, coarse, row_out, col_out, corner_out = backward(
+    cols = meetings(col_one, col_two, COL)
+    halos = (*meetings(row_one, row_two, ROW), *cols)
+    keep, send, fine, coarse, row_out, col_out = backward(
         shifts, feat, pre, pred, *halos, lines, low_in, in_turned, mid_turned, out_turned
     )
-    halos = (shifted(row_out, 1, 0), shifted(col_out, 0, 1), shifted(corner_out, 1, 1))
-    return keep, send, fine, coarse, halos
+    return keep, send, fine, coarse, row_out, shifted(col_out, 0, 1)
 
 
 def shards(
@@ -770,10 +788,10 @@
     out_first,
     out_second,
 ):
-    keep, send, fine, coarse, halos = local_grads(
+    keep, send, fine, coarse, row_out, col_in = local_grads(
         offsets, targets, grid_fine, grid_coarse, weight_in, weight_mid, weight_out
     )
-    own, other, fine_grad, coarse_grad = reduce_grads(keep, send, fine, coarse, halos)
+    own, other, fine_grad, coarse_grad = reduce_grads(keep, send, fine, coarse, row_out, col_in)
     devices = axes_size(ROW) * axes_size(COL)
     grid_entries = (fine_grad.size + coarse_grad.size) * devices
     decoder_entries = weight_in.size + weight_mid.size + weight_out.size

time: 113 us -> 109 us (0.965)
  blocking collectives: 0 us -> 12.4 us
  starting transfers between devices: 53.4 us -> 44.6 us
  waiting for transfers between devices: 33.7 us -> 25.2 us
    ppermute x18 -> x11, starting transfers between devices: 32.6 us -> 19.5 us  [swapped(): return lax.ppermute(block, axis, [(i, i ^ mask) for i in range(size)])]
    all_to_all x0 -> x1, blocking collectives: none -> 12.4 us  [all_to_all(): return lax.all_to_all(blocks, ('x', 'y'), 0, 0, tiled=True)]
    ppermute x18 -> x11, waiting for transfers between devices: 21.5 us -> 11.7 us  [swapped(): return lax.ppermute(block, axis, [(i, i ^ mask) for i in range(size)])]
    ppermute x4 -> x5, starting transfers between devices: 6.5 us -> 10 us  [the longest x2 4.17 us: meetings(): return (lax.ppermute(block_one, axes, one), block_two)]
    ppermute x4 -> x5, waiting for transfers between devices: 4.78 us -> 7.05 us  [the longest x2 4.78 us: meetings(): block_two = lax.ppermute(block_two, axes, two)]
    ppermute x2 -> x1, waiting for transfers between devices: 2.27 us -> 0.46 us  [shifted(): return lax.ppermute(block, ROW + COL, route)]
    ppermute x2, starting transfers between devices: 7.45 us -> 8.62 us  [shifted(): lax.ppermute(block, ROW, [(i, (i + down) % rows) for i in range(rows)])]
  transfers between devices with their start and end apart: 28 -> 21, of which waited for: 19 -> 13; matrix products, arithmetic and copies ran while one was open for 0% -> 0% of each run, Pallas kernels for 3% -> 3%
where the time goes in v4:
time: 109 us
  starting transfers between devices  44.6 us (41%)
  waiting for transfers between devices  25.2 us (23%)
  Pallas kernels  24.5 us (22%)
  blocking collectives  12.4 us (11%)
    ppermute x11, starting transfers between devices, swapped(): return lax.ppermute(block, axis, [(i, i ^ mask) for i in range(size)])  19.5 us
    all_to_all x1, blocking collectives, all_to_all(): return lax.all_to_all(blocks, ('x', 'y'), 0, 0, tiled=True)  12.4 us
    ppermute x11, waiting for transfers between devices, swapped(): return lax.ppermute(block, axis, [(i, i ^ mask) for i in range(size)])  11.7 us
    pallas_call x1, Pallas kernels, backward(): pl.pallas_call(backward_kernel, out_shape=outs, in_specs=[vmem()] * len(a...  11.6 us
    ppermute x2, starting transfers between devices, shifted(): lax.ppermute(block, ROW, [(i, (i + down) % rows) for i in range(rows)])  8.62 us
    ppermute x2, waiting for transfers between devices, shifted(): lax.ppermute(block, ROW, [(i, (i + down) % rows) for i in range(rows)])  5.54 us
    ppermute x2, starting transfers between devices, shifted(): lax.ppermute(block, COL, [(i, (i + right) % cols) for i in range(cols)])  5.07 us
    pallas_call x1, Pallas kernels, forward(): pl.pallas_call(forward_kernel, out_shape=outs, in_specs=[vmem()] * len(ar...  5.05 us
  transfers between devices with their start and end apart: 21, of which 13 were waited for; matrix products, arithmetic and copies ran while one was open for 0% of the time, Pallas kernels for 3%

profile of v4, /device:TPU:1, one launch (start us, length us, event | category | flops | bytes accessed | tf_op | source)
XLA Modules:
  0.0 108.6 jit_solution(18057321198145972666)
XLA Ops:
  0.6 2.5 %edges.1 = (f32[32,256]{1,0:T(8,128)S(1)}, f32[32,128]{1,0:T(8,128)S(1)}, f32[32,32,128]{2,1,0:T(8,128)S(1)}, f32[8,32,128]{2,1,0:T(8,128)S(1)}) custom-call(f32[32,32,128]{2,1,0:T(8,128)} %fine_hbm.1, f32[32,8,32]{2,1,0:T(8,128)} %coarse_hbm.1), custom_call_target="tpu_custom_call" | custom-call | tf_op jit(solution)/shard_map/edges/pallas_call | solution.py:182
  3.2 7.4 %collective-permute-start = (f32[32,256]{1,0:T(8,128)S(1)}, f32[32,256]{1,0:T(8,128)S(1)}, u32[]{:S(2)}, u32[]{:S(2)}) collective-permute-start(f32[32,256]{1,0:T(8,128)S(1)} %get-tuple-element.44), channel_id=1, source_target_pairs={{0,240},{16,0},{32,16},{48,32},{64,48},{80,64},{96,80},{112,96},{1... | collective-permute-start | bytes 98312 | tf_op jit(solution)/shard_map/ppermute | solution.py:56
  10.6 1.4 %collective-permute-start.2 = (f32[32,128]{1,0:T(8,128)S(1)}, f32[32,128]{1,0:T(8,128)S(1)}, u32[]{:S(2)}, u32[]{:S(2)}) collective-permute-start(f32[32,128]{1,0:T(8,128)S(1)} %get-tuple-element.45), channel_id=1, source_target_pairs={{0,255},{1,240},{2,241},{3,242},{4,243},{5,244},{6,245},{7,246},{8... | collective-permute-start | bytes 49160 | tf_op jit(solution)/shard_map/ppermute | solution.py:64
  12.0 3.2 %collective-permute-start.1 = (f32[32,128]{1,0:T(8,128)S(1)}, f32[32,128]{1,0:T(8,128)S(1)}, u32[]{:S(2)}, u32[]{:S(2)}) collective-permute-start(f32[32,128]{1,0:T(8,128)S(1)} %get-tuple-element.45), channel_id=1, source_target_pairs={{0,15},{1,0},{2,1},{3,2},{4,3},{5,4},{6,5},{7,6},{8,7},{9,8},{10,9... | collective-permute-start | bytes 49160 | tf_op jit(solution)/shard_map/ppermute | solution.py:58
  15.2 0.7 copy-done.10
  15.9 2.2 %prepare.1 = (f32[8,128]{1,0:T(8,128)S(1)}, bf16[512,64]{1,0:T(8,128)(2,1)S(1)}, bf16[64,512]{1,0:T(8,128)(2,1)S(1)}, bf16[512,512]{1,0:T(8,128)(2,1)S(1)}, bf16...) custom-call(s32[1,1,2]{2,1,0:T(1,128)S(1)} %copy-done.10, ...), custom_call_target="tpu_custom_call" | custom-call | tf_op jit(solution)/shard_map/prepare/pallas_call | solution.py:273
  19.1 5.1 %forward.1 = (bf16[64,4096]{1,0:T(8,128)(2,1)S(1)}, f32[512,4096]{1,0:T(8,128)S(1)}, f32[8,4096]{1,0:T(8,128)S(1)}, f32[8,128]{1,0:T(8,128)S(1)}, f32[8,128]{1,0...) custom-call(f32[8,128]{1,0:T(8,128)S(1)} %get-tuple-element.41.shift_ref, ...), custom_call_target="tpu_custom_call" | custom-call | tf_op jit(solution)/shard_map/forward/pallas_call | solution.py:380
  24.1 2.8 %collective-permute-start.3 = (f32[8,128]{1,0:T(8,128)S(1)}, f32[8,128]{1,0:T(8,128)S(1)}, u32[]{:S(2)}, u32[]{:S(2)}) collective-permute-start(f32[8,128]{1,0:T(8,128)S(1)} %get-tuple-element.54), channel_id=1, source_target_pairs={{0,16},{16,0},{32,48},{48,32},{64,80},{80,64},{96,112},{112,96},{1... | collective-permute-start | bytes 12296 | tf_op jit(solution)/shard_map/ppermute | solution.py:72
  26.9 1.4 %collective-permute-start.5 = (f32[8,128]{1,0:T(8,128)S(1)}, f32[8,128]{1,0:T(8,128)S(1)}, u32[]{:S(2)}, u32[]{:S(2)}) collective-permute-start(f32[8,128]{1,0:T(8,128)S(1)} %get-tuple-element.56), channel_id=1, source_target_pairs={{0,1},{1,0},{2,3},{3,2},{4,5},{5,4},{6,7},{7,6},{8,9},{9,8},{10,11... | collective-permute-start | bytes 12296 | tf_op jit(solution)/shard_map/ppermute | solution.py:72
  28.3 2.3 %collective-permute-start.6 = (f32[8,128]{1,0:T(8,128)S(1)}, f32[8,128]{1,0:T(8,128)S(1)}, u32[]{:S(2)}, u32[]{:S(2)}) collective-permute-start(f32[8,128]{1,0:T(8,128)S(1)} %get-tuple-element.57), channel_id=1, source_target_pairs={{0,15},{1,2},{2,1},{3,4},{4,3},{5,6},{6,5},{7,8},{8,7},{9,10},{10,... | collective-permute-start | bytes 12296 | tf_op jit(solution)/shard_map/ppermute | solution.py:71
  30.6 2.6 %collective-permute-done.4.row_two_ref = f32[8,128]{1,0:T(8,128)S(1)} collective-permute-done((f32[8,128]{1,0:T(8,128)S(1)}, f32[8,128]{1,0:T(8,128)S(1)}, u32[]{:S(2)}, u32[]{:S(2)}) %collective-permute-start.4) | collective-permute-done | bytes 4128 | tf_op jit(solution)/shard_map/ppermute | solution.py:71
  33.2 2.2 %collective-permute-done.6.col_two_ref = f32[8,128]{1,0:T(8,128)S(1)} collective-permute-done((f32[8,128]{1,0:T(8,128)S(1)}, f32[8,128]{1,0:T(8,128)S(1)}, u32[]{:S(2)}, u32[]{:S(2)}) %collective-permute-start.6) | collective-permute-done | bytes 4128 | tf_op jit(solution)/shard_map/ppermute | solution.py:71
  35.5 11.6 %backward.1 = (f32[16,80,128]{2,1,0:T(8,128)S(1)}, f32[16,80,128]{2,1,0:T(8,128)S(1)}, f32[32,32,128]{2,1,0:T(8,128)S(1)}, f32[8,32,128]{2,1,0:T(8,128)S(1)}, f3...) custom-call(f32[8,128]{1,0:T(8,128)S(1)} %get-tuple-element.41.shift_ref, bf16[64,4096]{1,0:T(8,128)(2,1)S(1)} %get-tuple-element.51.feat_ref, ...), custom_call_target="tpu_custom_call" | custom-call | tf_op jit(solution)/shard_map/backward/pallas_call | solution.py:547
  47.1 2.0 %collective-permute-start.7 = (f32[16,80,128]{2,1,0:T(8,128)S(1)}, f32[16,80,128]{2,1,0:T(8,128)S(1)}, u32[]{:S(2)}, u32[]{:S(2)}) collective-permute-start(f32[16,80,128]{2,1,0:T(8,128)S(1)} %get-tuple-element.62), channel_id=1, source_target_pairs={{0,1},{1,0},{2,3},{3,2},{4,5},{5,4},{6,7},{7,6},{8,9},{9,8},{10,11... | collective-permute-start | bytes 1966088 | tf_op jit(solution)/shard_map/ppermute | solution.py:82
  49.2 1.7 %collective-permute-done.7 = f32[16,80,128]{2,1,0:T(8,128)S(1)} collective-permute-done((f32[16,80,128]{2,1,0:T(8,128)S(1)}, f32[16,80,128]{2,1,0:T(8,128)S(1)}, u32[]{:S(2)}, u32[]{:S(2)}) %collective-permute-start.7) | collective-permute-done | bytes 655392 | tf_op jit(solution)/shard_map/ppermute | solution.py:82
  51.0 2.6 %collective-permute-start.10 = (f32[4,80,128]{2,1,0:T(8,128)S(1)}, f32[4,80,128]{2,1,0:T(8,128)S(1)}, u32[]{:S(2)}, u32[]{:S(2)}) collective-permute-start(f32[4,80,128]{2,1,0:T(8,128)S(1)} %get-tuple-element.77), channel_id=1, source_target_pairs={{0,48},{16,32},{32,16},{48,0},{1,49},{17,33},{33,17},{49,1},{2,50}... | collective-permute-start | bytes 491528 | tf_op jit(solution)/shard_map/ppermute | solution.py:82
  54.5 1.8 %collective-permute-start.11 = (f32[32,128]{1,0:T(8,128)S(1)}, f32[32,128]{1,0:T(8,128)S(1)}, u32[]{:S(2)}, u32[]{:S(2)}) collective-permute-start(f32[32,128]{1,0:T(8,128)S(1)} %get-tuple-element.63), channel_id=1, source_target_pairs={{0,1},{1,2},{2,3},{3,4},{4,5},{5,6},{6,7},{7,8},{8,9},{9,10},{10,1... | collective-permute-start | bytes 49160 | tf_op jit(solution)/shard_map/ppermute | solution.py:58
  56.3 4.0 %collective-permute-done.10 = f32[4,80,128]{2,1,0:T(8,128)S(1)} collective-permute-done((f32[4,80,128]{2,1,0:T(8,128)S(1)}, f32[4,80,128]{2,1,0:T(8,128)S(1)}, u32[]{:S(2)}, u32[]{:S(2)}) %collective-permute-start.10) | collective-permute-done | bytes 163872 | tf_op jit(solution)/shard_map/ppermute | solution.py:82
  60.3 1.6 %collective-permute-done.8 = f32[4,80,128]{2,1,0:T(8,128)S(1)} collective-permute-done((f32[4,80,128]{2,1,0:T(8,128)S(1)}, f32[4,80,128]{2,1,0:T(8,128)S(1)}, u32[]{:S(2)}, u32[]{:S(2)}) %collective-permute-start.8) | collective-permute-done | bytes 163872 | tf_op jit(solution)/shard_map/ppermute | solution.py:82
  62.5 2.8 %collective-permute-start.12 = (f32[80,128]{1,0:T(8,128)S(1)}, f32[80,128]{1,0:T(8,128)S(1)}, u32[]{:S(2)}, u32[]{:S(2)}) collective-permute-start(f32[80,128]{1,0:T(8,128)S(1)} %get-tuple-element.82), channel_id=1, source_target_pairs={{0,4},{4,0},{8,12},{12,8},{1,5},{5,1},{9,13},{13,9},{2,6},{6,2},{1... | collective-permute-start | bytes 122888 | tf_op jit(solution)/shard_map/ppermute | solution.py:82
  65.3 1.2 %collective-permute-start.15 = (f32[32,256]{1,0:T(8,128)S(1)}, f32[32,256]{1,0:T(8,128)S(1)}, u32[]{:S(2)}, u32[]{:S(2)}) collective-permute-start(f32[32,256]{1,0:T(8,128)S(1)} %turn.1), channel_id=1, source_target_pairs={{0,16},{16,32},{32,48},{48,64},{64,80},{80,96},{96,112},{112,128},... | collective-permute-start | bytes 98312 | tf_op jit(solution)/shard_map/ppermute | solution.py:56
  66.5 5.5 %collective-permute-done.15.row_ref = f32[32,256]{1,0:T(8,128)S(1)} collective-permute-done((f32[32,256]{1,0:T(8,128)S(1)}, f32[32,256]{1,0:T(8,128)S(1)}, u32[]{:S(2)}, u32[]{:S(2)}) %collective-permute-start.15) | collective-permute-done | bytes 32800 | tf_op jit(solution)/shard_map/ppermute | solution.py:56
  72.8 1.9 %collective-permute-start.18 = (f32[88,128]{1,0:T(8,128)S(1)}, f32[88,128]{1,0:T(8,128)S(1)}, u32[]{:S(2)}, u32[]{:S(2)}) collective-permute-start(f32[88,128]{1,0:T(8,128)S(1)} %pad_maximum_fusion), channel_id=1, source_target_pairs={{0,192},{64,128},{128,64},{192,0},{1,193},{65,129},{129,65},{193,1... | collective-permute-start | bytes 135176 | tf_op jit(solution)/shard_map/ppermute | solution.py:82
  74.7 0.8 collective-permute-start.16
  75.5 1.1 %collective-permute-done.17 = f32[88,128]{1,0:T(8,128)S(1)} collective-permute-done((f32[88,128]{1,0:T(8,128)S(1)}, f32[88,128]{1,0:T(8,128)S(1)}, u32[]{:S(2)}, u32[]{:S(2)}) %collective-permute-start.17) | collective-permute-done | bytes 45088 | tf_op jit(solution)/shard_map/ppermute | solution.py:82
  76.6 1.1 %collective-permute-done.18 = f32[88,128]{1,0:T(8,128)S(1)} collective-permute-done((f32[88,128]{1,0:T(8,128)S(1)}, f32[88,128]{1,0:T(8,128)S(1)}, u32[]{:S(2)}, u32[]{:S(2)}) %collective-permute-start.18) | collective-permute-done | bytes 45088 | tf_op jit(solution)/shard_map/ppermute | solution.py:82
  78.1 3.5 %collective-permute-start.19 = (f32[88,128]{1,0:T(8,128)S(1)}, f32[88,128]{1,0:T(8,128)S(1)}, u32[]{:S(2)}, u32[]{:S(2)}) collective-permute-start(f32[88,128]{1,0:T(8,128)S(1)} %add_add_fusion.one_ref), channel_id=1, source_target_pairs={{0,130},{2,128},{64,194},{66,192},{128,2},{130,0},{192,66},{194,64... | collective-permute-start | bytes 135176 | tf_op jit(solution)/shard_map/ppermute | solution.py:748
  81.6 2.3 %collective-permute-done.19.two_ref = f32[88,128]{1,0:T(8,128)S(1)} collective-permute-done((f32[88,128]{1,0:T(8,128)S(1)}, f32[88,128]{1,0:T(8,128)S(1)}, u32[]{:S(2)}, u32[]{:S(2)}) %collective-permute-start.19) | collective-permute-done | bytes 45088 | tf_op jit(solution)/shard_map/ppermute | solution.py:748
  84.0 12.4 %all_to_all.5.refs_0_ = f32[16,88,128]{2,1,0:T(8,128)S(1)} all-to-all(f32[16,88,128]{2,1,0:T(8,128)S(1)} %broadcast_in_dim.6), channel_id=1, replica_groups=mesh['zl'=4,'x'=4,'y'=4,'zh'=2,'c'=2] {'x','y'}, dimensions={0} | all-to-all | bytes 1441792 | tf_op jit(solution)/shard_map/all_to_all | solution.py:97
  96.5 8.0 %collective-permute-start.20 = (f32[16,88,128]{2,1,0:T(8,128)S(1)}, f32[16,88,128]{2,1,0:T(8,128)S(1)}, u32[]{:S(2)}, u32[]{:S(2)}) collective-permute-start(f32[16,88,128]{2,1,0:T(8,128)S(1)} %all_to_all.5.refs_0_), channel_id=1, source_target_pairs={{0,1},{1,0},{2,3},{3,2},{4,5},{5,4},{6,7},{7,6},{8,9},{9,8},{10,11... | collective-permute-start | bytes 2162696 | tf_op jit(solution)/shard_map/ppermute | solution.py:82
  104.4 1.8 %collective-permute-done.20.refs_1_ = f32[16,88,128]{2,1,0:T(8,128)S(1)} collective-permute-done((f32[16,88,128]{2,1,0:T(8,128)S(1)}, f32[16,88,128]{2,1,0:T(8,128)S(1)}, u32[]{:S(2)}, u32[]{:S(2)}) %collective-permute-start.20) | collective-permute-done | bytes 720928 | tf_op jit(solution)/shard_map/ppermute | solution.py:82
  106.3 2.3 %steps.1 = (f32[512,512]{1,0:T(8,128)}, f32[64,512]{1,0:T(8,128)}, f32[3,512]{1,0:T(4,128)}, f32[32,32,128]{2,1,0:T(8,128)}, f32[32,8,32]{2,1,0:T(8,128)}) custom-call(f32[16,88,128]{2,1,0:T(8,128)S(1)} %all_to_all.5.refs_0_, f32[16,88,128]{2,1,0:T(8,128)S(1)} %collective-permute-done.20.refs_1_, f32[32,32,128]{2,1,0:T(8,128)S(1)} %get-tuple-element.70.refs_2_, ...), custom_call_target="tpu_custom_call" | custom-call | tf_op jit(solution)/shard_map/steps/pallas_call | solution.py:704
  (49 shorter events, 3.9 us)
Async XLA Ops:
  3.2 15.9 %collective-permute-start = (f32[32,256]{1,0:T(8,128)S(1)}, f32[32,256]{1,0:T(8,128)S(1)}, u32[]{:S(2)}, u32[]{:S(2)}) collective-permute-start(f32[32,256]{1,0:T(8,128)S(1)} %get-tuple-element.44), channel_id=1, source_target_pairs={{0,240},{16,0},{32,16},{48,32},{64,48},{80,64},{96,80},{112,96},{1... | collective-permute-start | bytes 98312 | tf_op jit(solution)/shard_map/ppermute | solution.py:56
  10.6 8.0 %collective-permute-start.2 = (f32[32,128]{1,0:T(8,128)S(1)}, f32[32,128]{1,0:T(8,128)S(1)}, u32[]{:S(2)}, u32[]{:S(2)}) collective-permute-start(f32[32,128]{1,0:T(8,128)S(1)} %get-tuple-element.45), channel_id=1, source_target_pairs={{0,255},{1,240},{2,241},{3,242},{4,243},{5,244},{6,245},{7,246},{8... | collective-permute-start | bytes 49160 | tf_op jit(solution)/shard_map/ppermute | solution.py:64
  12.0 7.1 %collective-permute-start.1 = (f32[32,128]{1,0:T(8,128)S(1)}, f32[32,128]{1,0:T(8,128)S(1)}, u32[]{:S(2)}, u32[]{:S(2)}) collective-permute-start(f32[32,128]{1,0:T(8,128)S(1)} %get-tuple-element.45), channel_id=1, source_target_pairs={{0,15},{1,0},{2,1},{3,2},{4,3},{5,4},{6,5},{7,6},{8,7},{9,8},{10,9... | collective-permute-start | bytes 49160 | tf_op jit(solution)/shard_map/ppermute | solution.py:58
  15.2 0.7 copy-start.10
  24.1 6.5 %collective-permute-start.3 = (f32[8,128]{1,0:T(8,128)S(1)}, f32[8,128]{1,0:T(8,128)S(1)}, u32[]{:S(2)}, u32[]{:S(2)}) collective-permute-start(f32[8,128]{1,0:T(8,128)S(1)} %get-tuple-element.54), channel_id=1, source_target_pairs={{0,16},{16,0},{32,48},{48,32},{64,80},{80,64},{96,112},{112,96},{1... | collective-permute-start | bytes 12296 | tf_op jit(solution)/shard_map/ppermute | solution.py:72
  26.9 6.4 %collective-permute-start.4 = (f32[8,128]{1,0:T(8,128)S(1)}, f32[8,128]{1,0:T(8,128)S(1)}, u32[]{:S(2)}, u32[]{:S(2)}) collective-permute-start(f32[8,128]{1,0:T(8,128)S(1)} %get-tuple-element.55), channel_id=1, source_target_pairs={{0,240},{16,32},{32,16},{48,64},{64,48},{80,96},{96,80},{112,128},... | collective-permute-start | bytes 12296 | tf_op jit(solution)/shard_map/ppermute | solution.py:71
  26.9 6.4 %collective-permute-start.5 = (f32[8,128]{1,0:T(8,128)S(1)}, f32[8,128]{1,0:T(8,128)S(1)}, u32[]{:S(2)}, u32[]{:S(2)}) collective-permute-start(f32[8,128]{1,0:T(8,128)S(1)} %get-tuple-element.56), channel_id=1, source_target_pairs={{0,1},{1,0},{2,3},{3,2},{4,5},{5,4},{6,7},{7,6},{8,9},{9,8},{10,11... | collective-permute-start | bytes 12296 | tf_op jit(solution)/shard_map/ppermute | solution.py:72
  28.3 7.1 %collective-permute-start.6 = (f32[8,128]{1,0:T(8,128)S(1)}, f32[8,128]{1,0:T(8,128)S(1)}, u32[]{:S(2)}, u32[]{:S(2)}) collective-permute-start(f32[8,128]{1,0:T(8,128)S(1)} %get-tuple-element.57), channel_id=1, source_target_pairs={{0,15},{1,2},{2,1},{3,4},{4,3},{5,6},{6,5},{7,8},{8,7},{9,10},{10,... | collective-permute-start | bytes 12296 | tf_op jit(solution)/shard_map/ppermute | solution.py:71
  35.4 70.8 %copy-start = (f32[1,512,512]{2,1,0:T(8,128)S(1)}, f32[1,512,512]{2,1,0:T(8,128)}, u32[]{:S(2)}) copy-start(f32[1,512,512]{2,1,0:T(8,128)} %param.30) | copy-start | bytes 3145732
  35.4 70.8 %copy-start.1 = (f32[1,512,512]{2,1,0:T(8,128)S(1)}, f32[1,512,512]{2,1,0:T(8,128)}, u32[]{:S(2)}) copy-start(f32[1,512,512]{2,1,0:T(8,128)} %param.31) | copy-start | bytes 3145732
  35.4 70.8 %copy-start.2 = (f32[32,32,128]{2,1,0:T(8,128)S(1)}, f32[32,32,128]{2,1,0:T(8,128)}, u32[]{:S(2)}) copy-start(f32[32,32,128]{2,1,0:T(8,128)} %refs_10_.1) | copy-start | bytes 1572868
  35.4 70.8 %copy-start.3 = (f32[32,32,128]{2,1,0:T(8,128)S(1)}, f32[32,32,128]{2,1,0:T(8,128)}, u32[]{:S(2)}) copy-start(f32[32,32,128]{2,1,0:T(8,128)} %refs_11_.1) | copy-start | bytes 1572868
  35.4 70.8 %copy-start.4 = (f32[512,64]{0,1:T(8,128)S(1)}, f32[512,64]{0,1:T(8,128)}, u32[]{:S(2)}) copy-start(f32[512,64]{0,1:T(8,128)} %param.28) | copy-start | bytes 393220
  35.4 70.8 %copy-start.5 = (f32[512,64]{0,1:T(8,128)S(1)}, f32[512,64]{0,1:T(8,128)}, u32[]{:S(2)}) copy-start(f32[512,64]{0,1:T(8,128)} %param.29) | copy-start | bytes 393220
  35.4 70.8 %copy-start.6 = (f32[32,8,32]{2,1,0:T(8,128)S(1)}, f32[32,8,32]{2,1,0:T(8,128)}, u32[]{:S(2)}) copy-start(f32[32,8,32]{2,1,0:T(8,128)} %refs_12_.1) | copy-start | bytes 98308
  35.5 70.8 %copy-start.7 = (f32[32,8,32]{2,1,0:T(8,128)S(1)}, f32[32,8,32]{2,1,0:T(8,128)}, u32[]{:S(2)}) copy-start(f32[32,8,32]{2,1,0:T(8,128)} %refs_13_.1) | copy-start | bytes 98308
  35.5 70.8 %copy-start.8 = (f32[3,512]{1,0:T(4,128)S(1)}, f32[3,512]{1,0:T(4,128)}, u32[]{:S(2)}) copy-start(f32[3,512]{1,0:T(4,128)} %refs_8_.1) | copy-start | bytes 18436
  35.5 70.8 %copy-start.9 = (f32[3,512]{1,0:T(4,128)S(1)}, f32[3,512]{1,0:T(4,128)}, u32[]{:S(2)}) copy-start(f32[3,512]{1,0:T(4,128)} %refs_9_.1) | copy-start | bytes 18436
  47.1 3.7 %collective-permute-start.7 = (f32[16,80,128]{2,1,0:T(8,128)S(1)}, f32[16,80,128]{2,1,0:T(8,128)S(1)}, u32[]{:S(2)}, u32[]{:S(2)}) collective-permute-start(f32[16,80,128]{2,1,0:T(8,128)S(1)} %get-tuple-element.62), channel_id=1, source_target_pairs={{0,1},{1,0},{2,3},{3,2},{4,5},{5,4},{6,7},{7,6},{8,9},{9,8},{10,11... | collective-permute-start | bytes 1966088 | tf_op jit(solution)/shard_map/ppermute | solution.py:82
  51.0 9.3 %collective-permute-start.10 = (f32[4,80,128]{2,1,0:T(8,128)S(1)}, f32[4,80,128]{2,1,0:T(8,128)S(1)}, u32[]{:S(2)}, u32[]{:S(2)}) collective-permute-start(f32[4,80,128]{2,1,0:T(8,128)S(1)} %get-tuple-element.77), channel_id=1, source_target_pairs={{0,48},{16,32},{32,16},{48,0},{1,49},{17,33},{33,17},{49,1},{2,50}... | collective-permute-start | bytes 491528 | tf_op jit(solution)/shard_map/ppermute | solution.py:82
  53.6 6.7 %collective-permute-start.9 = (f32[4,80,128]{2,1,0:T(8,128)S(1)}, f32[4,80,128]{2,1,0:T(8,128)S(1)}, u32[]{:S(2)}, u32[]{:S(2)}) collective-permute-start(f32[4,80,128]{2,1,0:T(8,128)S(1)} %get-tuple-element.78), channel_id=1, source_target_pairs={{0,32},{16,48},{32,0},{48,16},{1,33},{17,49},{33,1},{49,17},{2,34}... | collective-permute-start | bytes 491528 | tf_op jit(solution)/shard_map/ppermute | solution.py:82
  54.0 7.8 %collective-permute-start.8 = (f32[4,80,128]{2,1,0:T(8,128)S(1)}, f32[4,80,128]{2,1,0:T(8,128)S(1)}, u32[]{:S(2)}, u32[]{:S(2)}) collective-permute-start(f32[4,80,128]{2,1,0:T(8,128)S(1)} %get-tuple-element.79), channel_id=1, source_target_pairs={{0,16},{16,0},{32,48},{48,32},{1,17},{17,1},{33,49},{49,33},{2,18}... | collective-permute-start | bytes 491528 | tf_op jit(solution)/shard_map/ppermute | solution.py:82
  54.5 7.4 %collective-permute-start.11 = (f32[32,128]{1,0:T(8,128)S(1)}, f32[32,128]{1,0:T(8,128)S(1)}, u32[]{:S(2)}, u32[]{:S(2)}) collective-permute-start(f32[32,128]{1,0:T(8,128)S(1)} %get-tuple-element.63), channel_id=1, source_target_pairs={{0,1},{1,2},{2,3},{3,4},{4,5},{5,6},{6,7},{7,8},{8,9},{9,10},{10,1... | collective-permute-start | bytes 49160 | tf_op jit(solution)/shard_map/ppermute | solution.py:58
  61.9 10.8 %collective-permute-start.14 = (f32[80,128]{1,0:T(8,128)S(1)}, f32[80,128]{1,0:T(8,128)S(1)}, u32[]{:S(2)}, u32[]{:S(2)}) collective-permute-start(f32[80,128]{1,0:T(8,128)S(1)} %get-tuple-element.80), channel_id=1, source_target_pairs={{0,12},{4,8},{8,4},{12,0},{1,13},{5,9},{9,5},{13,1},{2,14},{6,10},... | collective-permute-start | bytes 122888 | tf_op jit(solution)/shard_map/ppermute | solution.py:82
  62.4 10.3 %collective-permute-start.13 = (f32[80,128]{1,0:T(8,128)S(1)}, f32[80,128]{1,0:T(8,128)S(1)}, u32[]{:S(2)}, u32[]{:S(2)}) collective-permute-start(f32[80,128]{1,0:T(8,128)S(1)} %get-tuple-element.81), channel_id=1, source_target_pairs={{0,8},{4,12},{8,0},{12,4},{1,9},{5,13},{9,1},{13,5},{2,10},{6,14},... | collective-permute-start | bytes 122888 | tf_op jit(solution)/shard_map/ppermute | solution.py:82
  62.5 10.3 %collective-permute-start.12 = (f32[80,128]{1,0:T(8,128)S(1)}, f32[80,128]{1,0:T(8,128)S(1)}, u32[]{:S(2)}, u32[]{:S(2)}) collective-permute-start(f32[80,128]{1,0:T(8,128)S(1)} %get-tuple-element.82), channel_id=1, source_target_pairs={{0,4},{4,0},{8,12},{12,8},{1,5},{5,1},{9,13},{13,9},{2,6},{6,2},{1... | collective-permute-start | bytes 122888 | tf_op jit(solution)/shard_map/ppermute | solution.py:82
  65.3 6.7 %collective-permute-start.15 = (f32[32,256]{1,0:T(8,128)S(1)}, f32[32,256]{1,0:T(8,128)S(1)}, u32[]{:S(2)}, u32[]{:S(2)}) collective-permute-start(f32[32,256]{1,0:T(8,128)S(1)} %turn.1), channel_id=1, source_target_pairs={{0,16},{16,32},{32,48},{48,64},{64,80},{80,96},{96,112},{112,128},... | collective-permute-start | bytes 98312 | tf_op jit(solution)/shard_map/ppermute | solution.py:56
  72.7 3.9 %collective-permute-start.17 = (f32[88,128]{1,0:T(8,128)S(1)}, f32[88,128]{1,0:T(8,128)S(1)}, u32[]{:S(2)}, u32[]{:S(2)}) collective-permute-start(f32[88,128]{1,0:T(8,128)S(1)} %pad_maximum_fusion), channel_id=1, source_target_pairs={{0,128},{64,192},{128,0},{192,64},{1,129},{65,193},{129,1},{193,65... | collective-permute-start | bytes 135176 | tf_op jit(solution)/shard_map/ppermute | solution.py:82
  72.8 4.9 %collective-permute-start.18 = (f32[88,128]{1,0:T(8,128)S(1)}, f32[88,128]{1,0:T(8,128)S(1)}, u32[]{:S(2)}, u32[]{:S(2)}) collective-permute-start(f32[88,128]{1,0:T(8,128)S(1)} %pad_maximum_fusion), channel_id=1, source_target_pairs={{0,192},{64,128},{128,64},{192,0},{1,193},{65,129},{129,65},{193,1... | collective-permute-start | bytes 135176 | tf_op jit(solution)/shard_map/ppermute | solution.py:82
  74.7 3.4 %collective-permute-start.16 = (f32[88,128]{1,0:T(8,128)S(1)}, f32[88,128]{1,0:T(8,128)S(1)}, u32[]{:S(2)}, u32[]{:S(2)}) collective-permute-start(f32[88,128]{1,0:T(8,128)S(1)} %pad_maximum_fusion), channel_id=1, source_target_pairs={{0,64},{64,0},{128,192},{192,128},{1,65},{65,1},{129,193},{193,129... | collective-permute-start | bytes 135176 | tf_op jit(solution)/shard_map/ppermute | solution.py:82
  78.1 5.8 %collective-permute-start.19 = (f32[88,128]{1,0:T(8,128)S(1)}, f32[88,128]{1,0:T(8,128)S(1)}, u32[]{:S(2)}, u32[]{:S(2)}) collective-permute-start(f32[88,128]{1,0:T(8,128)S(1)} %add_add_fusion.one_ref), channel_id=1, source_target_pairs={{0,130},{2,128},{64,194},{66,192},{128,2},{130,0},{192,66},{194,64... | collective-permute-start | bytes 135176 | tf_op jit(solution)/shard_map/ppermute | solution.py:748
  96.5 9.8 %collective-permute-start.20 = (f32[16,88,128]{2,1,0:T(8,128)S(1)}, f32[16,88,128]{2,1,0:T(8,128)S(1)}, u32[]{:S(2)}, u32[]{:S(2)}) collective-permute-start(f32[16,88,128]{2,1,0:T(8,128)S(1)} %all_to_all.5.refs_0_), channel_id=1, source_target_pairs={{0,1},{1,0},{2,3},{3,2},{4,5},{5,4},{6,7},{7,6},{8,9},{9,8},{10,11... | collective-permute-start | bytes 2162696 | tf_op jit(solution)/shard_map/ppermute | solution.py:82

commit v5 on v4

--- a/solution.py
+++ b/solution.py
@@ -195,62 +195,113 @@
 
 
 def prepare_kernel(
-    offset_ref,
+    offset_hbm,
     in_hbm,
     mid_hbm,
     out_hbm,
     target_hbm,
     shift_ref,
     in_ref,
+    mid_ref,
+    out_ref,
+    floor_ref,
+    ends_ref,
+    w_in,
+    w_mid,
+    w_out,
+    targets,
+    offsets,
+    sems,
+):
+    sources = (target_hbm, in_hbm, out_hbm, offset_hbm, mid_hbm)
+    copies = [
+        pltpu.make_async_copy(source, target, sems.at[i])
+        for i, (source, target) in enumerate(zip(sources, (targets, w_in, w_out, offsets, w_mid)))
+    ]
+    for copy in copies:
+        copy.start()
+    copies[0].wait()
+    lane = lane_ids(3)
+    ends = jnp.zeros((3, SC), F32)
+    for i in range(SR):
+        ends = jnp.where(lane == i, spread_lane(targets[2, :, i, :], SC - 1), ends)
+    ends_ref[...] = jnp.zeros((8, SC), F32)
+    ends_ref[0:3, :] = ends
+    floor_ref[...] = jnp.zeros((8, SC), F32)
+    floor_ref[0:3, :] = targets[1, :, SR - 1, :]
+    copies[1].wait()
+    for block in range(4):
+        cols = slice(block * 128, block * 128 + 128)
+        in_ref[cols, :] = w_in[:, cols].T.astype(BF16)
+    copies[2].wait()
+    padded = jnp.concatenate([w_out[...], jnp.zeros((13, HID), F32)], axis=0)
+    out_ref[...] = padded.astype(BF16)
+    copies[3].wait()
+    shift_ref[...] = jnp.zeros((8, SC), F32)
+    for i in range(2):
+        shift = offsets[0, 0, i].astype(F32) * (1.0 / SUB)
+        shift_ref[i : i + 1, :] = jnp.full((1, SC), shift, F32)
+    copies[4].wait()
+    mid_ref[...] = w_mid[...].astype(BF16)
+
+
+def prepare(offsets, w_in, w_mid, w_out, targets):
+    outs = (
+        jax.ShapeDtypeStruct((8, SC), F32),
+        jax.ShapeDtypeStruct((HID, 2 * CH), BF16),
+        jax.ShapeDtypeStruct((HID, HID), BF16),
+        jax.ShapeDtypeStruct((16, HID), BF16),
+        jax.ShapeDtypeStruct((8, SC), F32),
+        jax.ShapeDtypeStruct((8, SC), F32),
+    )
+    return pl.pallas_call(
+        prepare_kernel,
+        out_shape=outs,
+        in_specs=[hbm()] * 5,
+        out_specs=(vmem(),) * len(outs),
+        scratch_shapes=[pltpu.VMEM(a.shape, F32) for a in (w_in, w_mid, w_out, targets)]
+        + [pltpu.SMEM(offsets.shape, jnp.int32), pltpu.SemaphoreType.DMA((5,))],
+        compiler_params=pltpu.CompilerParams(vmem_limit_bytes=8 * MIB),
+        name="prepare",
+    )(*(in_hbm(a) for a in (offsets, w_in, w_mid, w_out, targets)))
+
+
+def turned_kernel(
+    in_hbm,
+    mid_hbm,
+    out_hbm,
+    target_hbm,
+    unused_pred_ref,
     in_turned_ref,
-    mid_ref,
     mid_turned_ref,
-    out_ref,
     out_turned_ref,
     target_ref,
-    ends_ref,
     w_in,
     w_mid,
     w_out,
     targets,
     sems,
 ):
+    sources = (target_hbm, in_hbm, out_hbm, mid_hbm)
     copies = [
         pltpu.make_async_copy(source, target, sems.at[i])
-        for i, (source, target) in enumerate(
-            ((in_hbm, w_in), (out_hbm, w_out), (target_hbm, targets), (mid_hbm, w_mid))
-        )
+        for i, (source, target) in enumerate(zip(sources, (targets, w_in, w_out, w_mid)))
     ]
     for copy in copies:
         copy.start()
-    shift_ref[...] = jnp.zeros((8, SC), F32)
-    for i in range(2):
-        shift = offset_ref[0, 0, i].astype(F32) * (1.0 / SUB)
-        shift_ref[i : i + 1, :] = jnp.full((1, SC), shift, F32)
+    target_ref[...] = jnp.zeros(target_ref.shape, F32)
     copies[0].wait()
+    for i in range(SR):
+        for kind in range(3):
+            target_ref[kind, 0:3, i * SC : i * SC + SC] = targets[kind, :, i, :]
+    copies[1].wait()
     in_turned_ref[...] = w_in[...].astype(BF16)
-    for block in range(4):
-        cols = slice(block * 128, block * 128 + 128)
-        in_ref[cols, :] = w_in[:, cols].T.astype(BF16)
-    copies[1].wait()
+    copies[2].wait()
     padded = jnp.concatenate([w_out[...], jnp.zeros((13, HID), F32)], axis=0)
-    out_ref[...] = padded.astype(BF16)
     for block in range(4):
         cols = slice(block * 128, block * 128 + 128)
         out_turned_ref[cols, :] = padded[:, cols].T.astype(BF16)
-    copies[2].wait()
-    lane = lane_ids(3)
-    ends = jnp.zeros((3, SC), F32)
-    target_ref[...] = jnp.zeros(target_ref.shape, F32)
-    for i in range(SR):
-        for kind in range(3):
-            line = targets[kind, :, i, :]
-            target_ref[kind, 0:3, i * SC : i * SC + SC] = line
-        ends = jnp.where(lane == i, spread_lane(line, SC - 1), ends)
-    ends_ref[...] = jnp.zeros((8, SC), F32)
-    ends_ref[0:3, :] = ends
     copies[3].wait()
-    mid_ref[...] = w_mid[...].astype(BF16)
     for i in range(4):
         for j in range(4):
             rows = slice(i * 128, i * 128 + 128)
@@ -258,28 +309,23 @@
             mid_turned_ref[cols, rows] = w_mid[rows, cols].T.astype(BF16)
 
 
-def prepare(offsets, w_in, w_mid, w_out, targets):
+def turned(w_in, w_mid, w_out, targets, pred):
     outs = (
-        jax.ShapeDtypeStruct((8, SC), F32),
-        jax.ShapeDtypeStruct((HID, 2 * CH), BF16),
         jax.ShapeDtypeStruct((2 * CH, HID), BF16),
         jax.ShapeDtypeStruct((HID, HID), BF16),
-        jax.ShapeDtypeStruct((HID, HID), BF16),
-        jax.ShapeDtypeStruct((16, HID), BF16),
         jax.ShapeDtypeStruct((HID, 16), BF16),
         jax.ShapeDtypeStruct((3, 8, SR * SC), F32),
-        jax.ShapeDtypeStruct((8, SC), F32),
     )
     return pl.pallas_call(
-        prepare_kernel,
+        turned_kernel,
         out_shape=outs,
-        in_specs=[smem(), hbm(), hbm(), hbm(), hbm()],
+        in_specs=[hbm()] * 4 + [vmem()],
         out_specs=(vmem(),) * len(outs),
         scratch_shapes=[pltpu.VMEM(a.shape, F32) for a in (w_in, w_mid, w_out, targets)]
         + [pltpu.SemaphoreType.DMA((4,))],
         compiler_params=pltpu.CompilerParams(vmem_limit_bytes=8 * MIB),
-        name="prepare",
-    )(offsets, *(in_hbm(a) for a in (w_in, w_mid, w_out, targets)))
+        name="turned",
+    )(*(in_hbm(a) for a in (w_in, w_mid, w_out, targets)), pred)
 
 
 def forward_kernel(
@@ -289,7 +335,7 @@
     row_ref,
     col_ref,
     corner_ref,
-    target_ref,
+    floor_ref,
     ends_ref,
     in_ref,
     mid_ref,
@@ -299,8 +345,8 @@
     pred_ref,
     row_one_ref,
     row_two_ref,
+    col_two_ref,
     col_one_ref,
-    col_two_ref,
 ):
     shift_y = shift_ref[0:1, :]
     shift_x = shift_ref[1:2, :]
@@ -357,7 +403,7 @@
             right = right + jnp.where(lane8 == row, spread_lane(tile, SC - 1), 0.0)
         if chain == 0:
             up = pred[:, 0:SC]
-    down = pred[:, WIDTH - SC :] + target_ref[1, :, SR * SC - SC :]
+    down = pred[:, WIDTH - SC :] + floor_ref[...]
     odd_row = axes_index(ROW) % 2 == 1
     odd_col = axes_index(COL) % 2 == 1
     row_one_ref[...] = jnp.where(odd_row, up, down)
@@ -423,8 +469,8 @@
     pred_ref,
     row_one_ref,
     row_two_ref,
+    col_two_ref,
     col_one_ref,
-    col_two_ref,
     target_ref,
     in_ref,
     in_turned_ref,
@@ -755,14 +801,16 @@
     corner_in = shifted(col_out, -1, -1)
     col_in = shifted(col_out, 0, -1)
     row_in = shifted(row_out, -1, 0)
-    shifts, low_in, in_turned, low_mid, mid_turned, low_out, out_turned, lines, ends = prepare(
+    shifts, low_in, low_mid, low_out, floor, ends = prepare(
         offsets, weight_in.T, weight_mid[0], weight_out, targets
     )
-    feat, pre, pred, row_one, row_two, col_one, col_two = forward(
-        shifts, fine_lines, coarse_lines, row_in, col_in, corner_in, lines, ends, low_in, low_mid, low_out
-    )
-    cols = meetings(col_one, col_two, COL)
-    halos = (*meetings(row_one, row_two, ROW), *cols)
+    feat, pre, pred, row_one, row_two, col_two, col_one = forward(
+        shifts, fine_lines, coarse_lines, row_in, col_in, corner_in, floor, ends, low_in, low_mid, low_out
+    )
+    late = turned(weight_in.T, weight_mid[0], weight_out, targets, pred)
+    in_turned, mid_turned, out_turned, lines = late
+    col_one, col_two = meetings(col_one, col_two, COL)
+    halos = (*meetings(row_one, row_two, ROW), col_two, col_one)
     keep, send, fine, coarse, row_out, col_out = backward(
         shifts, feat, pre, pred, *halos, lines, low_in, in_turned, mid_turned, out_turned
     )

time: 109 us -> 107 us (0.982)
  waiting for transfers between devices: 25.2 us -> 21.1 us
  starting transfers between devices: 44.6 us -> 46.7 us
    ppermute x2, waiting for transfers between devices: 4.78 us -> 0.01 us  [meetings(): block_two = lax.ppermute(block_two, axes, two)]
    ppermute x11, starting transfers between devices: 19.5 us -> 15.8 us  [swapped(): return lax.ppermute(block, axis, [(i, i ^ mask) for i in range(size)])]
    ppermute x2, starting transfers between devices: 4.17 us -> 6.75 us  [meetings(): return (lax.ppermute(block_one, axes, one), block_two)]
    ppermute x1, waiting for transfers between devices: 0.46 us -> 1.85 us  [shifted(): return lax.ppermute(block, ROW + COL, route)]
    ppermute x1, starting transfers between devices: 3.5 us -> 4.64 us  [reduce_grads(): part = tally(part, lax.ppermute(part, ('zl', 'zh'), across))]
    ppermute x2, starting transfers between devices: 5.07 us -> 6.2 us  [shifted(): lax.ppermute(block, COL, [(i, (i + right) % cols) for i in range(cols)])]
    pallas_call x1 -> x2, Pallas kernels: 2.22 us -> 3.12 us  [the longest x1 1.63 us: turned(): pl.pallas_call(turned_kernel, out_shape=outs, in_specs=[hbm()] * 4 + [vme...]
  transfers between devices with their start and end apart: 21 -> 21, of which waited for: 13 -> 11; matrix products, arithmetic and copies ran while one was open for 0% -> 0% of each run, Pallas kernels for 3% -> 4%
where the time goes in v5:
time: 107 us
  starting transfers between devices  46.7 us (44%)
  Pallas kernels  25.5 us (24%)
  waiting for transfers between devices  21.1 us (20%)
  blocking collectives  12.5 us (12%)
    ppermute x11, starting transfers between devices, swapped(): return lax.ppermute(block, axis, [(i, i ^ mask) for i in range(size)])  15.8 us
    all_to_all x1, blocking collectives, all_to_all(): return lax.all_to_all(blocks, ('x', 'y'), 0, 0, tiled=True)  12.5 us
    pallas_call x1, Pallas kernels, backward(): pl.pallas_call(backward_kernel, out_shape=outs, in_specs=[vmem()] * len(a...  11.6 us
    ppermute x11, waiting for transfers between devices, swapped(): return lax.ppermute(block, axis, [(i, i ^ mask) for i in range(size)])  10.9 us
    ppermute x2, starting transfers between devices, shifted(): lax.ppermute(block, ROW, [(i, (i + down) % rows) for i in range(rows)])  8.56 us
    ppermute x2, starting transfers between devices, meetings(): return (lax.ppermute(block_one, axes, one), block_two)  6.75 us
    ppermute x2, starting transfers between devices, shifted(): lax.ppermute(block, COL, [(i, (i + right) % cols) for i in range(cols)])  6.2 us
    ppermute x2, waiting for transfers between devices, shifted(): lax.ppermute(block, ROW, [(i, (i + down) % rows) for i in range(rows)])  5.58 us
  transfers between devices with their start and end apart: 21, of which 11 were waited for; matrix products, arithmetic and copies ran while one was open for 0% of the time, Pallas kernels for 4%

profile of v5, /device:TPU:1, one launch (start us, length us, event | category | flops | bytes accessed | tf_op | source)
XLA Modules:
  0.0 106.9 jit_solution(651556921419001351)
XLA Ops:
  0.6 2.5 %edges.1 = (f32[32,256]{1,0:T(8,128)S(1)}, f32[32,128]{1,0:T(8,128)S(1)}, f32[32,32,128]{2,1,0:T(8,128)S(1)}, f32[8,32,128]{2,1,0:T(8,128)S(1)}) custom-call(f32[32,32,128]{2,1,0:T(8,128)} %fine_hbm.1, f32[32,8,32]{2,1,0:T(8,128)} %coarse_hbm.1), custom_call_target="tpu_custom_call" | custom-call | tf_op jit(solution)/shard_map/edges/pallas_call | solution.py:182
  3.2 7.4 %collective-permute-start = (f32[32,256]{1,0:T(8,128)S(1)}, f32[32,256]{1,0:T(8,128)S(1)}, u32[]{:S(2)}, u32[]{:S(2)}) collective-permute-start(f32[32,256]{1,0:T(8,128)S(1)} %get-tuple-element.45), channel_id=1, source_target_pairs={{0,240},{16,0},{32,16},{48,32},{64,48},{80,64},{96,80},{112,96},{1... | collective-permute-start | bytes 98312 | tf_op jit(solution)/shard_map/ppermute | solution.py:56
  10.6 1.4 %collective-permute-start.2 = (f32[32,128]{1,0:T(8,128)S(1)}, f32[32,128]{1,0:T(8,128)S(1)}, u32[]{:S(2)}, u32[]{:S(2)}) collective-permute-start(f32[32,128]{1,0:T(8,128)S(1)} %get-tuple-element.46), channel_id=1, source_target_pairs={{0,255},{1,240},{2,241},{3,242},{4,243},{5,244},{6,245},{7,246},{8... | collective-permute-start | bytes 49160 | tf_op jit(solution)/shard_map/ppermute | solution.py:64
  12.0 3.2 %collective-permute-start.1 = (f32[32,128]{1,0:T(8,128)S(1)}, f32[32,128]{1,0:T(8,128)S(1)}, u32[]{:S(2)}, u32[]{:S(2)}) collective-permute-start(f32[32,128]{1,0:T(8,128)S(1)} %get-tuple-element.46), channel_id=1, source_target_pairs={{0,15},{1,0},{2,1},{3,2},{4,3},{5,4},{6,5},{7,6},{8,7},{9,8},{10,9... | collective-permute-start | bytes 49160 | tf_op jit(solution)/shard_map/ppermute | solution.py:58
  15.2 1.5 %prepare.1 = (f32[8,128]{1,0:T(8,128)S(1)}, bf16[512,64]{1,0:T(8,128)(2,1)S(1)}, bf16[512,512]{1,0:T(8,128)(2,1)S(1)}, bf16[16,512]{1,0:T(8,128)(2,1)S(1)}, f32[8,128]{1,0:T(8,128)S(1)}, /*index=5*/f32[8,128]{1,0:T(8,128)S(1)}) custom-call(s32[1,1,2]{2,1,0:T(1,128)} %offset_hbm.1, f32[64,512]{1,0:T(8,128)} %bitcast.24, f32[512,512]{1,0:T(8,128)} %bitcast.22, ...), custom_call_target="tpu_custom_call" | custom-call | tf_op jit(solution)/shard_map/prepare/pallas_call | solution.py:257
  16.7 1.9 %collective-permute-done.2.corner_ref = f32[32,128]{1,0:T(8,128)S(1)} collective-permute-done((f32[32,128]{1,0:T(8,128)S(1)}, f32[32,128]{1,0:T(8,128)S(1)}, u32[]{:S(2)}, u32[]{:S(2)}) %collective-permute-start.2) | collective-permute-done | bytes 16416 | tf_op jit(solution)/shard_map/ppermute | solution.py:64
  19.1 5.1 %forward.1 = (bf16[64,4096]{1,0:T(8,128)(2,1)S(1)}, f32[512,4096]{1,0:T(8,128)S(1)}, f32[8,4096]{1,0:T(8,128)S(1)}, f32[8,128]{1,0:T(8,128)S(1)}, f32[8,128]{1,0...) custom-call(f32[8,128]{1,0:T(8,128)S(1)} %get-tuple-element.42.shift_ref, ...), custom_call_target="tpu_custom_call" | custom-call | tf_op jit(solution)/shard_map/forward/pallas_call | solution.py:426
  24.1 1.4 %collective-permute-start.3 = (f32[8,128]{1,0:T(8,128)S(1)}, f32[8,128]{1,0:T(8,128)S(1)}, u32[]{:S(2)}, u32[]{:S(2)}) collective-permute-start(f32[8,128]{1,0:T(8,128)S(1)} %get-tuple-element.55), channel_id=1, source_target_pairs={{0,16},{16,0},{32,48},{48,32},{64,80},{80,64},{96,112},{112,96},{1... | collective-permute-start | bytes 12296 | tf_op jit(solution)/shard_map/ppermute | solution.py:72
  25.5 3.4 %collective-permute-start.5 = (f32[8,128]{1,0:T(8,128)S(1)}, f32[8,128]{1,0:T(8,128)S(1)}, u32[]{:S(2)}, u32[]{:S(2)}) collective-permute-start(f32[8,128]{1,0:T(8,128)S(1)} %get-tuple-element.57), channel_id=1, source_target_pairs={{0,15},{1,2},{2,1},{3,4},{4,3},{5,6},{6,5},{7,8},{8,7},{9,10},{10,... | collective-permute-start | bytes 12296 | tf_op jit(solution)/shard_map/ppermute | solution.py:71
  28.9 5.4 %collective-permute-start.6 = (f32[8,128]{1,0:T(8,128)S(1)}, f32[8,128]{1,0:T(8,128)S(1)}, u32[]{:S(2)}, u32[]{:S(2)}) collective-permute-start(f32[8,128]{1,0:T(8,128)S(1)} %get-tuple-element.58), channel_id=1, source_target_pairs={{0,1},{1,0},{2,3},{3,2},{4,5},{5,4},{6,7},{7,6},{8,9},{9,8},{10,11... | collective-permute-start | bytes 12296 | tf_op jit(solution)/shard_map/ppermute | solution.py:72
  34.3 1.6 %turned.1 = (bf16[64,512]{1,0:T(8,128)(2,1)S(1)}, bf16[512,512]{1,0:T(8,128)(2,1)S(1)}, bf16[512,16]{1,0:T(8,128)(2,1)S(1)}, f32[3,8,4096]{2,1,0:T(8,128)S(1)}) custom-call(f32[64,512]{1,0:T(8,128)} %bitcast.25, f32[512,512]{1,0:T(8,128)} %bitcast.23, f32[3,512]{1,0:T(4,128)} %out_hbm.3, f32[3,3,32,128]{3,2,1,0:T(8,128)} %target_hbm.3, ...), custom_call_target="tpu_custom_call" | custom-call | tf_op jit(solution)/shard_map/turned/pallas_call | solution.py:319
  36.1 11.6 %backward.1 = (f32[16,80,128]{2,1,0:T(8,128)S(1)}, f32[16,80,128]{2,1,0:T(8,128)S(1)}, f32[32,32,128]{2,1,0:T(8,128)S(1)}, f32[8,32,128]{2,1,0:T(8,128)S(1)}, f3...) custom-call(f32[8,128]{1,0:T(8,128)S(1)} %get-tuple-element.42.shift_ref, bf16[64,4096]{1,0:T(8,128)(2,1)S(1)} %get-tuple-element.52.feat_ref, ...), custom_call_target="tpu_custom_call" | custom-call | tf_op jit(solution)/shard_map/backward/pallas_call | solution.py:593
  47.8 2.1 %collective-permute-done.7 = f32[16,80,128]{2,1,0:T(8,128)S(1)} collective-permute-done((f32[16,80,128]{2,1,0:T(8,128)S(1)}, f32[16,80,128]{2,1,0:T(8,128)S(1)}, u32[]{:S(2)}, u32[]{:S(2)}) %collective-permute-start.7) | collective-permute-done | bytes 655392 | tf_op jit(solution)/shard_map/ppermute | solution.py:82
  50.0 2.3 %collective-permute-start.10 = (f32[4,80,128]{2,1,0:T(8,128)S(1)}, f32[4,80,128]{2,1,0:T(8,128)S(1)}, u32[]{:S(2)}, u32[]{:S(2)}) collective-permute-start(f32[4,80,128]{2,1,0:T(8,128)S(1)} %get-tuple-element.79), channel_id=1, source_target_pairs={{0,48},{16,32},{32,16},{48,0},{1,49},{17,33},{33,17},{49,1},{2,50}... | collective-permute-start | bytes 491528 | tf_op jit(solution)/shard_map/ppermute | solution.py:82
  53.4 3.0 %collective-permute-start.11 = (f32[32,128]{1,0:T(8,128)S(1)}, f32[32,128]{1,0:T(8,128)S(1)}, u32[]{:S(2)}, u32[]{:S(2)}) collective-permute-start(f32[32,128]{1,0:T(8,128)S(1)} %get-tuple-element.65), channel_id=1, source_target_pairs={{0,1},{1,2},{2,3},{3,4},{4,5},{5,6},{6,7},{7,8},{8,9},{9,10},{10,1... | collective-permute-start | bytes 49160 | tf_op jit(solution)/shard_map/ppermute | solution.py:58
  56.3 3.6 %collective-permute-done.10 = f32[4,80,128]{2,1,0:T(8,128)S(1)} collective-permute-done((f32[4,80,128]{2,1,0:T(8,128)S(1)}, f32[4,80,128]{2,1,0:T(8,128)S(1)}, u32[]{:S(2)}, u32[]{:S(2)}) %collective-permute-start.10) | collective-permute-done | bytes 163872 | tf_op jit(solution)/shard_map/ppermute | solution.py:82
  59.9 0.9 collective-permute-done.8
  60.9 1.6 %collective-permute-start.14 = (f32[80,128]{1,0:T(8,128)S(1)}, f32[80,128]{1,0:T(8,128)S(1)}, u32[]{:S(2)}, u32[]{:S(2)}) collective-permute-start(f32[80,128]{1,0:T(8,128)S(1)} %get-tuple-element.82), channel_id=1, source_target_pairs={{0,12},{4,8},{8,4},{12,0},{1,13},{5,9},{9,5},{13,1},{2,14},{6,10},... | collective-permute-start | bytes 122888 | tf_op jit(solution)/shard_map/ppermute | solution.py:82
  62.5 1.8 %collective-permute-start.12 = (f32[80,128]{1,0:T(8,128)S(1)}, f32[80,128]{1,0:T(8,128)S(1)}, u32[]{:S(2)}, u32[]{:S(2)}) collective-permute-start(f32[80,128]{1,0:T(8,128)S(1)} %get-tuple-element.84), channel_id=1, source_target_pairs={{0,4},{4,0},{8,12},{12,8},{1,5},{5,1},{9,13},{13,9},{2,6},{6,2},{1... | collective-permute-start | bytes 122888 | tf_op jit(solution)/shard_map/ppermute | solution.py:82
  64.3 1.1 %collective-permute-start.15 = (f32[32,256]{1,0:T(8,128)S(1)}, f32[32,256]{1,0:T(8,128)S(1)}, u32[]{:S(2)}, u32[]{:S(2)}) collective-permute-start(f32[32,256]{1,0:T(8,128)S(1)} %turn.1), channel_id=1, source_target_pairs={{0,16},{16,32},{32,48},{48,64},{64,80},{80,96},{96,112},{112,128},... | collective-permute-start | bytes 98312 | tf_op jit(solution)/shard_map/ppermute | solution.py:56
  65.4 5.6 %collective-permute-done.15.row_ref = f32[32,256]{1,0:T(8,128)S(1)} collective-permute-done((f32[32,256]{1,0:T(8,128)S(1)}, f32[32,256]{1,0:T(8,128)S(1)}, u32[]{:S(2)}, u32[]{:S(2)}) %collective-permute-start.15) | collective-permute-done | bytes 32800 | tf_op jit(solution)/shard_map/ppermute | solution.py:56
  71.0 0.6 join.1
  71.8 1.8 %collective-permute-start.18 = (f32[88,128]{1,0:T(8,128)S(1)}, f32[88,128]{1,0:T(8,128)S(1)}, u32[]{:S(2)}, u32[]{:S(2)}) collective-permute-start(f32[88,128]{1,0:T(8,128)S(1)} %pad_maximum_fusion), channel_id=1, source_target_pairs={{0,192},{64,128},{128,64},{192,0},{1,193},{65,129},{129,65},{193,1... | collective-permute-start | bytes 135176 | tf_op jit(solution)/shard_map/ppermute | solution.py:82
  73.6 0.9 collective-permute-start.16
  74.4 1.1 %collective-permute-done.17 = f32[88,128]{1,0:T(8,128)S(1)} collective-permute-done((f32[88,128]{1,0:T(8,128)S(1)}, f32[88,128]{1,0:T(8,128)S(1)}, u32[]{:S(2)}, u32[]{:S(2)}) %collective-permute-start.17) | collective-permute-done | bytes 45088 | tf_op jit(solution)/shard_map/ppermute | solution.py:82
  75.6 1.2 %collective-permute-done.18 = f32[88,128]{1,0:T(8,128)S(1)} collective-permute-done((f32[88,128]{1,0:T(8,128)S(1)}, f32[88,128]{1,0:T(8,128)S(1)}, u32[]{:S(2)}, u32[]{:S(2)}) %collective-permute-start.18) | collective-permute-done | bytes 45088 | tf_op jit(solution)/shard_map/ppermute | solution.py:82
  77.0 4.6 %collective-permute-start.19 = (f32[88,128]{1,0:T(8,128)S(1)}, f32[88,128]{1,0:T(8,128)S(1)}, u32[]{:S(2)}, u32[]{:S(2)}) collective-permute-start(f32[88,128]{1,0:T(8,128)S(1)} %add_add_fusion.one_ref), channel_id=1, source_target_pairs={{0,130},{2,128},{64,194},{66,192},{128,2},{130,0},{192,66},{194,64... | collective-permute-start | bytes 135176 | tf_op jit(solution)/shard_map/ppermute | solution.py:794
  81.6 2.3 %collective-permute-done.19.two_ref = f32[88,128]{1,0:T(8,128)S(1)} collective-permute-done((f32[88,128]{1,0:T(8,128)S(1)}, f32[88,128]{1,0:T(8,128)S(1)}, u32[]{:S(2)}, u32[]{:S(2)}) %collective-permute-start.19) | collective-permute-done | bytes 45088 | tf_op jit(solution)/shard_map/ppermute | solution.py:794
  84.0 12.5 %all_to_all.5.refs_0_ = f32[16,88,128]{2,1,0:T(8,128)S(1)} all-to-all(f32[16,88,128]{2,1,0:T(8,128)S(1)} %broadcast_in_dim.6), channel_id=1, replica_groups=mesh['zl'=4,'x'=4,'y'=4,'zh'=2,'c'=2] {'x','y'}, dimensions={0} | all-to-all | bytes 1441792 | tf_op jit(solution)/shard_map/all_to_all | solution.py:97
  96.5 6.3 %collective-permute-start.20 = (f32[16,88,128]{2,1,0:T(8,128)S(1)}, f32[16,88,128]{2,1,0:T(8,128)S(1)}, u32[]{:S(2)}, u32[]{:S(2)}) collective-permute-start(f32[16,88,128]{2,1,0:T(8,128)S(1)} %all_to_all.5.refs_0_), channel_id=1, source_target_pairs={{0,1},{1,0},{2,3},{3,2},{4,5},{5,4},{6,7},{7,6},{8,9},{9,8},{10,11... | collective-permute-start | bytes 2162696 | tf_op jit(solution)/shard_map/ppermute | solution.py:82
  102.8 1.8 %collective-permute-done.20.refs_1_ = f32[16,88,128]{2,1,0:T(8,128)S(1)} collective-permute-done((f32[16,88,128]{2,1,0:T(8,128)S(1)}, f32[16,88,128]{2,1,0:T(8,128)S(1)}, u32[]{:S(2)}, u32[]{:S(2)}) %collective-permute-start.20) | collective-permute-done | bytes 720928 | tf_op jit(solution)/shard_map/ppermute | solution.py:82
  104.6 2.3 %steps.1 = (f32[512,512]{1,0:T(8,128)}, f32[64,512]{1,0:T(8,128)}, f32[3,512]{1,0:T(4,128)}, f32[32,32,128]{2,1,0:T(8,128)}, f32[32,8,32]{2,1,0:T(8,128)}) custom-call(f32[16,88,128]{2,1,0:T(8,128)S(1)} %all_to_all.5.refs_0_, f32[16,88,128]{2,1,0:T(8,128)S(1)} %collective-permute-done.20.refs_1_, f32[32,32,128]{2,1,0:T(8,128)S(1)} %get-tuple-element.72.refs_2_, ...), custom_call_target="tpu_custom_call" | custom-call | tf_op jit(solution)/shard_map/steps/pallas_call | solution.py:750
  (48 shorter events, 2.5 us)
Async XLA Ops:
  3.2 15.9 %collective-permute-start = (f32[32,256]{1,0:T(8,128)S(1)}, f32[32,256]{1,0:T(8,128)S(1)}, u32[]{:S(2)}, u32[]{:S(2)}) collective-permute-start(f32[32,256]{1,0:T(8,128)S(1)} %get-tuple-element.45), channel_id=1, source_target_pairs={{0,240},{16,0},{32,16},{48,32},{64,48},{80,64},{96,80},{112,96},{1... | collective-permute-start | bytes 98312 | tf_op jit(solution)/shard_map/ppermute | solution.py:56
  10.6 8.0 %collective-permute-start.2 = (f32[32,128]{1,0:T(8,128)S(1)}, f32[32,128]{1,0:T(8,128)S(1)}, u32[]{:S(2)}, u32[]{:S(2)}) collective-permute-start(f32[32,128]{1,0:T(8,128)S(1)} %get-tuple-element.46), channel_id=1, source_target_pairs={{0,255},{1,240},{2,241},{3,242},{4,243},{5,244},{6,245},{7,246},{8... | collective-permute-start | bytes 49160 | tf_op jit(solution)/shard_map/ppermute | solution.py:64
  12.0 7.1 %collective-permute-start.1 = (f32[32,128]{1,0:T(8,128)S(1)}, f32[32,128]{1,0:T(8,128)S(1)}, u32[]{:S(2)}, u32[]{:S(2)}) collective-permute-start(f32[32,128]{1,0:T(8,128)S(1)} %get-tuple-element.46), channel_id=1, source_target_pairs={{0,15},{1,0},{2,1},{3,2},{4,3},{5,4},{6,5},{7,6},{8,7},{9,8},{10,9... | collective-permute-start | bytes 49160 | tf_op jit(solution)/shard_map/ppermute | solution.py:58
  24.1 11.8 %collective-permute-start.3 = (f32[8,128]{1,0:T(8,128)S(1)}, f32[8,128]{1,0:T(8,128)S(1)}, u32[]{:S(2)}, u32[]{:S(2)}) collective-permute-start(f32[8,128]{1,0:T(8,128)S(1)} %get-tuple-element.55), channel_id=1, source_target_pairs={{0,16},{16,0},{32,48},{48,32},{64,80},{80,64},{96,112},{112,96},{1... | collective-permute-start | bytes 12296 | tf_op jit(solution)/shard_map/ppermute | solution.py:72
  25.5 10.4 %collective-permute-start.4 = (f32[8,128]{1,0:T(8,128)S(1)}, f32[8,128]{1,0:T(8,128)S(1)}, u32[]{:S(2)}, u32[]{:S(2)}) collective-permute-start(f32[8,128]{1,0:T(8,128)S(1)} %get-tuple-element.56), channel_id=1, source_target_pairs={{0,240},{16,32},{32,16},{48,64},{64,48},{80,96},{96,80},{112,128},... | collective-permute-start | bytes 12296 | tf_op jit(solution)/shard_map/ppermute | solution.py:71
  25.5 10.4 %collective-permute-start.5 = (f32[8,128]{1,0:T(8,128)S(1)}, f32[8,128]{1,0:T(8,128)S(1)}, u32[]{:S(2)}, u32[]{:S(2)}) collective-permute-start(f32[8,128]{1,0:T(8,128)S(1)} %get-tuple-element.57), channel_id=1, source_target_pairs={{0,15},{1,2},{2,1},{3,4},{4,3},{5,6},{6,5},{7,8},{8,7},{9,10},{10,... | collective-permute-start | bytes 12296 | tf_op jit(solution)/shard_map/ppermute | solution.py:71
  28.9 7.1 %collective-permute-start.6 = (f32[8,128]{1,0:T(8,128)S(1)}, f32[8,128]{1,0:T(8,128)S(1)}, u32[]{:S(2)}, u32[]{:S(2)}) collective-permute-start(f32[8,128]{1,0:T(8,128)S(1)} %get-tuple-element.58), channel_id=1, source_target_pairs={{0,1},{1,0},{2,3},{3,2},{4,5},{5,4},{6,7},{7,6},{8,9},{9,8},{10,11... | collective-permute-start | bytes 12296 | tf_op jit(solution)/shard_map/ppermute | solution.py:72
  35.9 68.6 %copy-start = (f32[1,512,512]{2,1,0:T(8,128)S(1)}, f32[1,512,512]{2,1,0:T(8,128)}, u32[]{:S(2)}) copy-start(f32[1,512,512]{2,1,0:T(8,128)} %param.30) | copy-start | bytes 3145732
  36.0 68.6 %copy-start.1 = (f32[1,512,512]{2,1,0:T(8,128)S(1)}, f32[1,512,512]{2,1,0:T(8,128)}, u32[]{:S(2)}) copy-start(f32[1,512,512]{2,1,0:T(8,128)} %param.31) | copy-start | bytes 3145732
  36.0 68.6 %copy-start.2 = (f32[32,32,128]{2,1,0:T(8,128)S(1)}, f32[32,32,128]{2,1,0:T(8,128)}, u32[]{:S(2)}) copy-start(f32[32,32,128]{2,1,0:T(8,128)} %refs_10_.1) | copy-start | bytes 1572868
  36.0 68.6 %copy-start.3 = (f32[32,32,128]{2,1,0:T(8,128)S(1)}, f32[32,32,128]{2,1,0:T(8,128)}, u32[]{:S(2)}) copy-start(f32[32,32,128]{2,1,0:T(8,128)} %refs_11_.1) | copy-start | bytes 1572868
  36.0 68.6 %copy-start.4 = (f32[512,64]{0,1:T(8,128)S(1)}, f32[512,64]{0,1:T(8,128)}, u32[]{:S(2)}) copy-start(f32[512,64]{0,1:T(8,128)} %param.28) | copy-start | bytes 393220
  36.0 68.6 %copy-start.5 = (f32[512,64]{0,1:T(8,128)S(1)}, f32[512,64]{0,1:T(8,128)}, u32[]{:S(2)}) copy-start(f32[512,64]{0,1:T(8,128)} %param.29) | copy-start | bytes 393220
  36.0 68.6 %copy-start.6 = (f32[32,8,32]{2,1,0:T(8,128)S(1)}, f32[32,8,32]{2,1,0:T(8,128)}, u32[]{:S(2)}) copy-start(f32[32,8,32]{2,1,0:T(8,128)} %refs_12_.1) | copy-start | bytes 98308
  36.0 68.6 %copy-start.7 = (f32[32,8,32]{2,1,0:T(8,128)S(1)}, f32[32,8,32]{2,1,0:T(8,128)}, u32[]{:S(2)}) copy-start(f32[32,8,32]{2,1,0:T(8,128)} %refs_13_.1) | copy-start | bytes 98308
  36.0 68.6 %copy-start.8 = (f32[3,512]{1,0:T(4,128)S(1)}, f32[3,512]{1,0:T(4,128)}, u32[]{:S(2)}) copy-start(f32[3,512]{1,0:T(4,128)} %refs_8_.1) | copy-start | bytes 18436
  36.1 68.6 %copy-start.9 = (f32[3,512]{1,0:T(4,128)S(1)}, f32[3,512]{1,0:T(4,128)}, u32[]{:S(2)}) copy-start(f32[3,512]{1,0:T(4,128)} %refs_9_.1) | copy-start | bytes 18436
  47.7 2.2 %collective-permute-start.7 = (f32[16,80,128]{2,1,0:T(8,128)S(1)}, f32[16,80,128]{2,1,0:T(8,128)S(1)}, u32[]{:S(2)}, u32[]{:S(2)}) collective-permute-start(f32[16,80,128]{2,1,0:T(8,128)S(1)} %get-tuple-element.64), channel_id=1, source_target_pairs={{0,1},{1,0},{2,3},{3,2},{4,5},{5,4},{6,7},{7,6},{8,9},{9,8},{10,11... | collective-permute-start | bytes 1966088 | tf_op jit(solution)/shard_map/ppermute | solution.py:82
  50.0 9.9 %collective-permute-start.10 = (f32[4,80,128]{2,1,0:T(8,128)S(1)}, f32[4,80,128]{2,1,0:T(8,128)S(1)}, u32[]{:S(2)}, u32[]{:S(2)}) collective-permute-start(f32[4,80,128]{2,1,0:T(8,128)S(1)} %get-tuple-element.79), channel_id=1, source_target_pairs={{0,48},{16,32},{32,16},{48,0},{1,49},{17,33},{33,17},{49,1},{2,50}... | collective-permute-start | bytes 491528 | tf_op jit(solution)/shard_map/ppermute | solution.py:82
  52.3 7.6 %collective-permute-start.9 = (f32[4,80,128]{2,1,0:T(8,128)S(1)}, f32[4,80,128]{2,1,0:T(8,128)S(1)}, u32[]{:S(2)}, u32[]{:S(2)}) collective-permute-start(f32[4,80,128]{2,1,0:T(8,128)S(1)} %get-tuple-element.80), channel_id=1, source_target_pairs={{0,32},{16,48},{32,0},{48,16},{1,33},{17,49},{33,1},{49,17},{2,34}... | collective-permute-start | bytes 491528 | tf_op jit(solution)/shard_map/ppermute | solution.py:82
  52.8 8.0 %collective-permute-start.8 = (f32[4,80,128]{2,1,0:T(8,128)S(1)}, f32[4,80,128]{2,1,0:T(8,128)S(1)}, u32[]{:S(2)}, u32[]{:S(2)}) collective-permute-start(f32[4,80,128]{2,1,0:T(8,128)S(1)} %get-tuple-element.81), channel_id=1, source_target_pairs={{0,16},{16,0},{32,48},{48,32},{1,17},{17,1},{33,49},{49,33},{2,18}... | collective-permute-start | bytes 491528 | tf_op jit(solution)/shard_map/ppermute | solution.py:82
  53.4 7.5 %collective-permute-start.11 = (f32[32,128]{1,0:T(8,128)S(1)}, f32[32,128]{1,0:T(8,128)S(1)}, u32[]{:S(2)}, u32[]{:S(2)}) collective-permute-start(f32[32,128]{1,0:T(8,128)S(1)} %get-tuple-element.65), channel_id=1, source_target_pairs={{0,1},{1,2},{2,3},{3,4},{4,5},{5,6},{6,7},{7,8},{8,9},{9,10},{10,1... | collective-permute-start | bytes 49160 | tf_op jit(solution)/shard_map/ppermute | solution.py:58
  60.9 10.8 %collective-permute-start.14 = (f32[80,128]{1,0:T(8,128)S(1)}, f32[80,128]{1,0:T(8,128)S(1)}, u32[]{:S(2)}, u32[]{:S(2)}) collective-permute-start(f32[80,128]{1,0:T(8,128)S(1)} %get-tuple-element.82), channel_id=1, source_target_pairs={{0,12},{4,8},{8,4},{12,0},{1,13},{5,9},{9,5},{13,1},{2,14},{6,10},... | collective-permute-start | bytes 122888 | tf_op jit(solution)/shard_map/ppermute | solution.py:82
  62.5 9.2 %collective-permute-start.13 = (f32[80,128]{1,0:T(8,128)S(1)}, f32[80,128]{1,0:T(8,128)S(1)}, u32[]{:S(2)}, u32[]{:S(2)}) collective-permute-start(f32[80,128]{1,0:T(8,128)S(1)} %get-tuple-element.83), channel_id=1, source_target_pairs={{0,8},{4,12},{8,0},{12,4},{1,9},{5,13},{9,1},{13,5},{2,10},{6,14},... | collective-permute-start | bytes 122888 | tf_op jit(solution)/shard_map/ppermute | solution.py:82
  62.5 9.2 %collective-permute-start.12 = (f32[80,128]{1,0:T(8,128)S(1)}, f32[80,128]{1,0:T(8,128)S(1)}, u32[]{:S(2)}, u32[]{:S(2)}) collective-permute-start(f32[80,128]{1,0:T(8,128)S(1)} %get-tuple-element.84), channel_id=1, source_target_pairs={{0,4},{4,0},{8,12},{12,8},{1,5},{5,1},{9,13},{13,9},{2,6},{6,2},{1... | collective-permute-start | bytes 122888 | tf_op jit(solution)/shard_map/ppermute | solution.py:82
  64.3 6.7 %collective-permute-start.15 = (f32[32,256]{1,0:T(8,128)S(1)}, f32[32,256]{1,0:T(8,128)S(1)}, u32[]{:S(2)}, u32[]{:S(2)}) collective-permute-start(f32[32,256]{1,0:T(8,128)S(1)} %turn.1), channel_id=1, source_target_pairs={{0,16},{16,32},{32,48},{48,64},{64,80},{80,96},{96,112},{112,128},... | collective-permute-start | bytes 98312 | tf_op jit(solution)/shard_map/ppermute | solution.py:56
  71.7 3.9 %collective-permute-start.17 = (f32[88,128]{1,0:T(8,128)S(1)}, f32[88,128]{1,0:T(8,128)S(1)}, u32[]{:S(2)}, u32[]{:S(2)}) collective-permute-start(f32[88,128]{1,0:T(8,128)S(1)} %pad_maximum_fusion), channel_id=1, source_target_pairs={{0,128},{64,192},{128,0},{192,64},{1,129},{65,193},{129,1},{193,65... | collective-permute-start | bytes 135176 | tf_op jit(solution)/shard_map/ppermute | solution.py:82
  71.8 4.9 %collective-permute-start.18 = (f32[88,128]{1,0:T(8,128)S(1)}, f32[88,128]{1,0:T(8,128)S(1)}, u32[]{:S(2)}, u32[]{:S(2)}) collective-permute-start(f32[88,128]{1,0:T(8,128)S(1)} %pad_maximum_fusion), channel_id=1, source_target_pairs={{0,192},{64,128},{128,64},{192,0},{1,193},{65,129},{129,65},{193,1... | collective-permute-start | bytes 135176 | tf_op jit(solution)/shard_map/ppermute | solution.py:82
  73.6 3.4 %collective-permute-start.16 = (f32[88,128]{1,0:T(8,128)S(1)}, f32[88,128]{1,0:T(8,128)S(1)}, u32[]{:S(2)}, u32[]{:S(2)}) collective-permute-start(f32[88,128]{1,0:T(8,128)S(1)} %pad_maximum_fusion), channel_id=1, source_target_pairs={{0,64},{64,0},{128,192},{192,128},{1,65},{65,1},{129,193},{193,129... | collective-permute-start | bytes 135176 | tf_op jit(solution)/shard_map/ppermute | solution.py:82
  77.0 6.9 %collective-permute-start.19 = (f32[88,128]{1,0:T(8,128)S(1)}, f32[88,128]{1,0:T(8,128)S(1)}, u32[]{:S(2)}, u32[]{:S(2)}) collective-permute-start(f32[88,128]{1,0:T(8,128)S(1)} %add_add_fusion.one_ref), channel_id=1, source_target_pairs={{0,130},{2,128},{64,194},{66,192},{128,2},{130,0},{192,66},{194,64... | collective-permute-start | bytes 135176 | tf_op jit(solution)/shard_map/ppermute | solution.py:794
  96.5 8.1 %collective-permute-start.20 = (f32[16,88,128]{2,1,0:T(8,128)S(1)}, f32[16,88,128]{2,1,0:T(8,128)S(1)}, u32[]{:S(2)}, u32[]{:S(2)}) collective-permute-start(f32[16,88,128]{2,1,0:T(8,128)S(1)} %all_to_all.5.refs_0_), channel_id=1, source_target_pairs={{0,1},{1,0},{2,3},{3,2},{4,5},{5,4},{6,7},{7,6},{8,9},{9,8},{10,11... | collective-permute-start | bytes 2162696 | tf_op jit(solution)/shard_map/ppermute | solution.py:82

commit v6 on v5

--- a/solution.py
+++ b/solution.py
@@ -28,7 +28,7 @@
 CHAINS = 4
 WIDTH = SR * SC // CHAINS
 LINES = SR // CHAINS
-PARTS = 2
+PARTS = 1
 FINE_CORNER = 64
 COARSE_CORNER = 65
 F32 = jnp.float32

time: 107 us -> 108 us (level)
  no operation moved by 1% of the time
where the time goes in v6:
time: 108 us; the launch traced here: 107 us
  starting transfers between devices  46.7 us (43%)
  Pallas kernels  25.8 us (24%)
  waiting for transfers between devices  21.1 us (20%)
  blocking collectives  12.5 us (12%)
    ppermute x11, starting transfers between devices, swapped(): return lax.ppermute(block, axis, [(i, i ^ mask) for i in range(size)])  15.8 us
    all_to_all x1, blocking collectives, all_to_all(): return lax.all_to_all(blocks, ('x', 'y'), 0, 0, tiled=True)  12.5 us
    pallas_call x1, Pallas kernels, backward(): pl.pallas_call(backward_kernel, out_shape=outs, in_specs=[vmem()] * len(a...  11.6 us
    ppermute x11, waiting for transfers between devices, swapped(): return lax.ppermute(block, axis, [(i, i ^ mask) for i in range(size)])  10.9 us
    ppermute x2, starting transfers between devices, shifted(): lax.ppermute(block, ROW, [(i, (i + down) % rows) for i in range(rows)])  8.56 us
    ppermute x2, starting transfers between devices, meetings(): return (lax.ppermute(block_one, axes, one), block_two)  6.75 us
    ppermute x2, starting transfers between devices, shifted(): lax.ppermute(block, COL, [(i, (i + right) % cols) for i in range(cols)])  6.2 us
    ppermute x2, waiting for transfers between devices, shifted(): lax.ppermute(block, ROW, [(i, (i + down) % rows) for i in range(rows)])  5.58 us
  transfers between devices with their start and end apart: 21, of which 11 were waited for; matrix products, arithmetic and copies ran while one was open for 0% of the time, Pallas kernels for 4%

profile of v6, /device:TPU:1, one launch (start us, length us, event | category | flops | bytes accessed | tf_op | source)
XLA Modules:
  0.0 107.3 jit_solution(12532872358125132997)
XLA Ops:
  0.6 2.5 %edges.1 = (f32[32,256]{1,0:T(8,128)S(1)}, f32[32,128]{1,0:T(8,128)S(1)}, f32[32,32,128]{2,1,0:T(8,128)S(1)}, f32[8,32,128]{2,1,0:T(8,128)S(1)}) custom-call(f32[32,32,128]{2,1,0:T(8,128)} %fine_hbm.1, f32[32,8,32]{2,1,0:T(8,128)} %coarse_hbm.1), custom_call_target="tpu_custom_call" | custom-call | tf_op jit(solution)/shard_map/edges/pallas_call | solution.py:182
  3.2 7.4 %collective-permute-start = (f32[32,256]{1,0:T(8,128)S(1)}, f32[32,256]{1,0:T(8,128)S(1)}, u32[]{:S(2)}, u32[]{:S(2)}) collective-permute-start(f32[32,256]{1,0:T(8,128)S(1)} %get-tuple-element.45), channel_id=1, source_target_pairs={{0,240},{16,0},{32,16},{48,32},{64,48},{80,64},{96,80},{112,96},{1... | collective-permute-start | bytes 98312 | tf_op jit(solution)/shard_map/ppermute | solution.py:56
  10.6 1.4 %collective-permute-start.2 = (f32[32,128]{1,0:T(8,128)S(1)}, f32[32,128]{1,0:T(8,128)S(1)}, u32[]{:S(2)}, u32[]{:S(2)}) collective-permute-start(f32[32,128]{1,0:T(8,128)S(1)} %get-tuple-element.46), channel_id=1, source_target_pairs={{0,255},{1,240},{2,241},{3,242},{4,243},{5,244},{6,245},{7,246},{8... | collective-permute-start | bytes 49160 | tf_op jit(solution)/shard_map/ppermute | solution.py:64
  12.0 3.2 %collective-permute-start.1 = (f32[32,128]{1,0:T(8,128)S(1)}, f32[32,128]{1,0:T(8,128)S(1)}, u32[]{:S(2)}, u32[]{:S(2)}) collective-permute-start(f32[32,128]{1,0:T(8,128)S(1)} %get-tuple-element.46), channel_id=1, source_target_pairs={{0,15},{1,0},{2,1},{3,2},{4,3},{5,4},{6,5},{7,6},{8,7},{9,8},{10,9... | collective-permute-start | bytes 49160 | tf_op jit(solution)/shard_map/ppermute | solution.py:58
  15.2 1.5 %prepare.1 = (f32[8,128]{1,0:T(8,128)S(1)}, bf16[512,64]{1,0:T(8,128)(2,1)S(1)}, bf16[512,512]{1,0:T(8,128)(2,1)S(1)}, bf16[16,512]{1,0:T(8,128)(2,1)S(1)}, f32[8,128]{1,0:T(8,128)S(1)}, /*index=5*/f32[8,128]{1,0:T(8,128)S(1)}) custom-call(s32[1,1,2]{2,1,0:T(1,128)} %offset_hbm.1, f32[64,512]{1,0:T(8,128)} %bitcast.24, f32[512,512]{1,0:T(8,128)} %bitcast.22, ...), custom_call_target="tpu_custom_call" | custom-call | tf_op jit(solution)/shard_map/prepare/pallas_call | solution.py:257
  16.7 1.9 %collective-permute-done.2.corner_ref = f32[32,128]{1,0:T(8,128)S(1)} collective-permute-done((f32[32,128]{1,0:T(8,128)S(1)}, f32[32,128]{1,0:T(8,128)S(1)}, u32[]{:S(2)}, u32[]{:S(2)}) %collective-permute-start.2) | collective-permute-done | bytes 16416 | tf_op jit(solution)/shard_map/ppermute | solution.py:64
  19.1 5.1 %forward.1 = (bf16[64,4096]{1,0:T(8,128)(2,1)S(1)}, f32[512,4096]{1,0:T(8,128)S(1)}, f32[8,4096]{1,0:T(8,128)S(1)}, f32[8,128]{1,0:T(8,128)S(1)}, f32[8,128]{1,0...) custom-call(f32[8,128]{1,0:T(8,128)S(1)} %get-tuple-element.42.shift_ref, ...), custom_call_target="tpu_custom_call" | custom-call | tf_op jit(solution)/shard_map/forward/pallas_call | solution.py:426
  24.1 1.4 %collective-permute-start.3 = (f32[8,128]{1,0:T(8,128)S(1)}, f32[8,128]{1,0:T(8,128)S(1)}, u32[]{:S(2)}, u32[]{:S(2)}) collective-permute-start(f32[8,128]{1,0:T(8,128)S(1)} %get-tuple-element.55), channel_id=1, source_target_pairs={{0,16},{16,0},{32,48},{48,32},{64,80},{80,64},{96,112},{112,96},{1... | collective-permute-start | bytes 12296 | tf_op jit(solution)/shard_map/ppermute | solution.py:72
  25.5 3.4 %collective-permute-start.5 = (f32[8,128]{1,0:T(8,128)S(1)}, f32[8,128]{1,0:T(8,128)S(1)}, u32[]{:S(2)}, u32[]{:S(2)}) collective-permute-start(f32[8,128]{1,0:T(8,128)S(1)} %get-tuple-element.57), channel_id=1, source_target_pairs={{0,15},{1,2},{2,1},{3,4},{4,3},{5,6},{6,5},{7,8},{8,7},{9,10},{10,... | collective-permute-start | bytes 12296 | tf_op jit(solution)/shard_map/ppermute | solution.py:71
  28.9 5.4 %collective-permute-start.6 = (f32[8,128]{1,0:T(8,128)S(1)}, f32[8,128]{1,0:T(8,128)S(1)}, u32[]{:S(2)}, u32[]{:S(2)}) collective-permute-start(f32[8,128]{1,0:T(8,128)S(1)} %get-tuple-element.58), channel_id=1, source_target_pairs={{0,1},{1,0},{2,3},{3,2},{4,5},{5,4},{6,7},{7,6},{8,9},{9,8},{10,11... | collective-permute-start | bytes 12296 | tf_op jit(solution)/shard_map/ppermute | solution.py:72
  34.3 1.6 %turned.1 = (bf16[64,512]{1,0:T(8,128)(2,1)S(1)}, bf16[512,512]{1,0:T(8,128)(2,1)S(1)}, bf16[512,16]{1,0:T(8,128)(2,1)S(1)}, f32[3,8,4096]{2,1,0:T(8,128)S(1)}) custom-call(f32[64,512]{1,0:T(8,128)} %bitcast.25, f32[512,512]{1,0:T(8,128)} %bitcast.23, f32[3,512]{1,0:T(4,128)} %out_hbm.3, f32[3,3,32,128]{3,2,1,0:T(8,128)} %target_hbm.3, ...), custom_call_target="tpu_custom_call" | custom-call | tf_op jit(solution)/shard_map/turned/pallas_call | solution.py:319
  36.1 11.6 %backward.1 = (f32[16,80,128]{2,1,0:T(8,128)S(1)}, f32[16,80,128]{2,1,0:T(8,128)S(1)}, f32[32,32,128]{2,1,0:T(8,128)S(1)}, f32[8,32,128]{2,1,0:T(8,128)S(1)}, f3...) custom-call(f32[8,128]{1,0:T(8,128)S(1)} %get-tuple-element.42.shift_ref, bf16[64,4096]{1,0:T(8,128)(2,1)S(1)} %get-tuple-element.52.feat_ref, ...), custom_call_target="tpu_custom_call" | custom-call | tf_op jit(solution)/shard_map/backward/pallas_call | solution.py:593
  47.8 2.1 %collective-permute-done.7 = f32[16,80,128]{2,1,0:T(8,128)S(1)} collective-permute-done((f32[16,80,128]{2,1,0:T(8,128)S(1)}, f32[16,80,128]{2,1,0:T(8,128)S(1)}, u32[]{:S(2)}, u32[]{:S(2)}) %collective-permute-start.7) | collective-permute-done | bytes 655392 | tf_op jit(solution)/shard_map/ppermute | solution.py:82
  50.0 2.3 %collective-permute-start.10 = (f32[4,80,128]{2,1,0:T(8,128)S(1)}, f32[4,80,128]{2,1,0:T(8,128)S(1)}, u32[]{:S(2)}, u32[]{:S(2)}) collective-permute-start(f32[4,80,128]{2,1,0:T(8,128)S(1)} %get-tuple-element.79), channel_id=1, source_target_pairs={{0,48},{16,32},{32,16},{48,0},{1,49},{17,33},{33,17},{49,1},{2,50}... | collective-permute-start | bytes 491528 | tf_op jit(solution)/shard_map/ppermute | solution.py:82
  53.4 3.0 %collective-permute-start.11 = (f32[32,128]{1,0:T(8,128)S(1)}, f32[32,128]{1,0:T(8,128)S(1)}, u32[]{:S(2)}, u32[]{:S(2)}) collective-permute-start(f32[32,128]{1,0:T(8,128)S(1)} %get-tuple-element.65), channel_id=1, source_target_pairs={{0,1},{1,2},{2,3},{3,4},{4,5},{5,6},{6,7},{7,8},{8,9},{9,10},{10,1... | collective-permute-start | bytes 49160 | tf_op jit(solution)/shard_map/ppermute | solution.py:58
  56.3 3.6 %collective-permute-done.10 = f32[4,80,128]{2,1,0:T(8,128)S(1)} collective-permute-done((f32[4,80,128]{2,1,0:T(8,128)S(1)}, f32[4,80,128]{2,1,0:T(8,128)S(1)}, u32[]{:S(2)}, u32[]{:S(2)}) %collective-permute-start.10) | collective-permute-done | bytes 163872 | tf_op jit(solution)/shard_map/ppermute | solution.py:82
  59.9 0.9 collective-permute-done.8
  60.9 1.6 %collective-permute-start.14 = (f32[80,128]{1,0:T(8,128)S(1)}, f32[80,128]{1,0:T(8,128)S(1)}, u32[]{:S(2)}, u32[]{:S(2)}) collective-permute-start(f32[80,128]{1,0:T(8,128)S(1)} %get-tuple-element.82), channel_id=1, source_target_pairs={{0,12},{4,8},{8,4},{12,0},{1,13},{5,9},{9,5},{13,1},{2,14},{6,10},... | collective-permute-start | bytes 122888 | tf_op jit(solution)/shard_map/ppermute | solution.py:82
  62.5 1.8 %collective-permute-start.12 = (f32[80,128]{1,0:T(8,128)S(1)}, f32[80,128]{1,0:T(8,128)S(1)}, u32[]{:S(2)}, u32[]{:S(2)}) collective-permute-start(f32[80,128]{1,0:T(8,128)S(1)} %get-tuple-element.84), channel_id=1, source_target_pairs={{0,4},{4,0},{8,12},{12,8},{1,5},{5,1},{9,13},{13,9},{2,6},{6,2},{1... | collective-permute-start | bytes 122888 | tf_op jit(solution)/shard_map/ppermute | solution.py:82
  64.3 1.1 %collective-permute-start.15 = (f32[32,256]{1,0:T(8,128)S(1)}, f32[32,256]{1,0:T(8,128)S(1)}, u32[]{:S(2)}, u32[]{:S(2)}) collective-permute-start(f32[32,256]{1,0:T(8,128)S(1)} %turn.1), channel_id=1, source_target_pairs={{0,16},{16,32},{32,48},{48,64},{64,80},{80,96},{96,112},{112,128},... | collective-permute-start | bytes 98312 | tf_op jit(solution)/shard_map/ppermute | solution.py:56
  65.4 5.6 %collective-permute-done.15.row_ref = f32[32,256]{1,0:T(8,128)S(1)} collective-permute-done((f32[32,256]{1,0:T(8,128)S(1)}, f32[32,256]{1,0:T(8,128)S(1)}, u32[]{:S(2)}, u32[]{:S(2)}) %collective-permute-start.15) | collective-permute-done | bytes 32800 | tf_op jit(solution)/shard_map/ppermute | solution.py:56
  71.0 0.6 join.1
  71.8 1.8 %collective-permute-start.18 = (f32[88,128]{1,0:T(8,128)S(1)}, f32[88,128]{1,0:T(8,128)S(1)}, u32[]{:S(2)}, u32[]{:S(2)}) collective-permute-start(f32[88,128]{1,0:T(8,128)S(1)} %pad_maximum_fusion), channel_id=1, source_target_pairs={{0,192},{64,128},{128,64},{192,0},{1,193},{65,129},{129,65},{193,1... | collective-permute-start | bytes 135176 | tf_op jit(solution)/shard_map/ppermute | solution.py:82
  73.6 0.9 collective-permute-start.16
  74.4 1.1 %collective-permute-done.17 = f32[88,128]{1,0:T(8,128)S(1)} collective-permute-done((f32[88,128]{1,0:T(8,128)S(1)}, f32[88,128]{1,0:T(8,128)S(1)}, u32[]{:S(2)}, u32[]{:S(2)}) %collective-permute-start.17) | collective-permute-done | bytes 45088 | tf_op jit(solution)/shard_map/ppermute | solution.py:82
  75.6 1.2 %collective-permute-done.18 = f32[88,128]{1,0:T(8,128)S(1)} collective-permute-done((f32[88,128]{1,0:T(8,128)S(1)}, f32[88,128]{1,0:T(8,128)S(1)}, u32[]{:S(2)}, u32[]{:S(2)}) %collective-permute-start.18) | collective-permute-done | bytes 45088 | tf_op jit(solution)/shard_map/ppermute | solution.py:82
  77.0 4.6 %collective-permute-start.19 = (f32[88,128]{1,0:T(8,128)S(1)}, f32[88,128]{1,0:T(8,128)S(1)}, u32[]{:S(2)}, u32[]{:S(2)}) collective-permute-start(f32[88,128]{1,0:T(8,128)S(1)} %add_add_fusion.one_ref), channel_id=1, source_target_pairs={{0,130},{2,128},{64,194},{66,192},{128,2},{130,0},{192,66},{194,64... | collective-permute-start | bytes 135176 | tf_op jit(solution)/shard_map/ppermute | solution.py:794
  81.6 2.3 %collective-permute-done.19.two_ref = f32[88,128]{1,0:T(8,128)S(1)} collective-permute-done((f32[88,128]{1,0:T(8,128)S(1)}, f32[88,128]{1,0:T(8,128)S(1)}, u32[]{:S(2)}, u32[]{:S(2)}) %collective-permute-start.19) | collective-permute-done | bytes 45088 | tf_op jit(solution)/shard_map/ppermute | solution.py:794
  84.0 12.5 %all_to_all.5.refs_0_ = f32[16,88,128]{2,1,0:T(8,128)S(1)} all-to-all(f32[16,88,128]{2,1,0:T(8,128)S(1)} %broadcast_in_dim.6), channel_id=1, replica_groups=mesh['zl'=4,'x'=4,'y'=4,'zh'=2,'c'=2] {'x','y'}, dimensions={0} | all-to-all | bytes 1441792 | tf_op jit(solution)/shard_map/all_to_all | solution.py:97
  96.5 6.3 %collective-permute-start.20 = (f32[16,88,128]{2,1,0:T(8,128)S(1)}, f32[16,88,128]{2,1,0:T(8,128)S(1)}, u32[]{:S(2)}, u32[]{:S(2)}) collective-permute-start(f32[16,88,128]{2,1,0:T(8,128)S(1)} %all_to_all.5.refs_0_), channel_id=1, source_target_pairs={{0,1},{1,0},{2,3},{3,2},{4,5},{5,4},{6,7},{7,6},{8,9},{9,8},{10,11... | collective-permute-start | bytes 2162696 | tf_op jit(solution)/shard_map/ppermute | solution.py:82
  102.8 1.8 %collective-permute-done.20.refs_1_ = f32[16,88,128]{2,1,0:T(8,128)S(1)} collective-permute-done((f32[16,88,128]{2,1,0:T(8,128)S(1)}, f32[16,88,128]{2,1,0:T(8,128)S(1)}, u32[]{:S(2)}, u32[]{:S(2)}) %collective-permute-start.20) | collective-permute-done | bytes 720928 | tf_op jit(solution)/shard_map/ppermute | solution.py:82
  104.6 2.7 %steps.1 = (f32[512,512]{1,0:T(8,128)}, f32[64,512]{1,0:T(8,128)}, f32[3,512]{1,0:T(4,128)}, f32[32,32,128]{2,1,0:T(8,128)}, f32[32,8,32]{2,1,0:T(8,128)}) custom-call(f32[16,88,128]{2,1,0:T(8,128)S(1)} %all_to_all.5.refs_0_, f32[16,88,128]{2,1,0:T(8,128)S(1)} %collective-permute-done.20.refs_1_, f32[32,32,128]{2,1,0:T(8,128)S(1)} %get-tuple-element.72.refs_2_, ...), custom_call_target="tpu_custom_call" | custom-call | tf_op jit(solution)/shard_map/steps/pallas_call | solution.py:750
  (48 shorter events, 2.5 us)
Async XLA Ops:
  3.2 15.9 %collective-permute-start = (f32[32,256]{1,0:T(8,128)S(1)}, f32[32,256]{1,0:T(8,128)S(1)}, u32[]{:S(2)}, u32[]{:S(2)}) collective-permute-start(f32[32,256]{1,0:T(8,128)S(1)} %get-tuple-element.45), channel_id=1, source_target_pairs={{0,240},{16,0},{32,16},{48,32},{64,48},{80,64},{96,80},{112,96},{1... | collective-permute-start | bytes 98312 | tf_op jit(solution)/shard_map/ppermute | solution.py:56
  10.6 8.0 %collective-permute-start.2 = (f32[32,128]{1,0:T(8,128)S(1)}, f32[32,128]{1,0:T(8,128)S(1)}, u32[]{:S(2)}, u32[]{:S(2)}) collective-permute-start(f32[32,128]{1,0:T(8,128)S(1)} %get-tuple-element.46), channel_id=1, source_target_pairs={{0,255},{1,240},{2,241},{3,242},{4,243},{5,244},{6,245},{7,246},{8... | collective-permute-start | bytes 49160 | tf_op jit(solution)/shard_map/ppermute | solution.py:64
  12.0 7.1 %collective-permute-start.1 = (f32[32,128]{1,0:T(8,128)S(1)}, f32[32,128]{1,0:T(8,128)S(1)}, u32[]{:S(2)}, u32[]{:S(2)}) collective-permute-start(f32[32,128]{1,0:T(8,128)S(1)} %get-tuple-element.46), channel_id=1, source_target_pairs={{0,15},{1,0},{2,1},{3,2},{4,3},{5,4},{6,5},{7,6},{8,7},{9,8},{10,9... | collective-permute-start | bytes 49160 | tf_op jit(solution)/shard_map/ppermute | solution.py:58
  24.1 11.8 %collective-permute-start.3 = (f32[8,128]{1,0:T(8,128)S(1)}, f32[8,128]{1,0:T(8,128)S(1)}, u32[]{:S(2)}, u32[]{:S(2)}) collective-permute-start(f32[8,128]{1,0:T(8,128)S(1)} %get-tuple-element.55), channel_id=1, source_target_pairs={{0,16},{16,0},{32,48},{48,32},{64,80},{80,64},{96,112},{112,96},{1... | collective-permute-start | bytes 12296 | tf_op jit(solution)/shard_map/ppermute | solution.py:72
  25.5 10.4 %collective-permute-start.4 = (f32[8,128]{1,0:T(8,128)S(1)}, f32[8,128]{1,0:T(8,128)S(1)}, u32[]{:S(2)}, u32[]{:S(2)}) collective-permute-start(f32[8,128]{1,0:T(8,128)S(1)} %get-tuple-element.56), channel_id=1, source_target_pairs={{0,240},{16,32},{32,16},{48,64},{64,48},{80,96},{96,80},{112,128},... | collective-permute-start | bytes 12296 | tf_op jit(solution)/shard_map/ppermute | solution.py:71
  25.5 10.4 %collective-permute-start.5 = (f32[8,128]{1,0:T(8,128)S(1)}, f32[8,128]{1,0:T(8,128)S(1)}, u32[]{:S(2)}, u32[]{:S(2)}) collective-permute-start(f32[8,128]{1,0:T(8,128)S(1)} %get-tuple-element.57), channel_id=1, source_target_pairs={{0,15},{1,2},{2,1},{3,4},{4,3},{5,6},{6,5},{7,8},{8,7},{9,10},{10,... | collective-permute-start | bytes 12296 | tf_op jit(solution)/shard_map/ppermute | solution.py:71
  28.9 7.1 %collective-permute-start.6 = (f32[8,128]{1,0:T(8,128)S(1)}, f32[8,128]{1,0:T(8,128)S(1)}, u32[]{:S(2)}, u32[]{:S(2)}) collective-permute-start(f32[8,128]{1,0:T(8,128)S(1)} %get-tuple-element.58), channel_id=1, source_target_pairs={{0,1},{1,0},{2,3},{3,2},{4,5},{5,4},{6,7},{7,6},{8,9},{9,8},{10,11... | collective-permute-start | bytes 12296 | tf_op jit(solution)/shard_map/ppermute | solution.py:72
  35.9 68.6 %copy-start = (f32[1,512,512]{2,1,0:T(8,128)S(1)}, f32[1,512,512]{2,1,0:T(8,128)}, u32[]{:S(2)}) copy-start(f32[1,512,512]{2,1,0:T(8,128)} %param.30) | copy-start | bytes 3145732
  36.0 68.6 %copy-start.1 = (f32[1,512,512]{2,1,0:T(8,128)S(1)}, f32[1,512,512]{2,1,0:T(8,128)}, u32[]{:S(2)}) copy-start(f32[1,512,512]{2,1,0:T(8,128)} %param.31) | copy-start | bytes 3145732
  36.0 68.6 %copy-start.2 = (f32[32,32,128]{2,1,0:T(8,128)S(1)}, f32[32,32,128]{2,1,0:T(8,128)}, u32[]{:S(2)}) copy-start(f32[32,32,128]{2,1,0:T(8,128)} %refs_10_.1) | copy-start | bytes 1572868
  36.0 68.6 %copy-start.3 = (f32[32,32,128]{2,1,0:T(8,128)S(1)}, f32[32,32,128]{2,1,0:T(8,128)}, u32[]{:S(2)}) copy-start(f32[32,32,128]{2,1,0:T(8,128)} %refs_11_.1) | copy-start | bytes 1572868
  36.0 68.6 %copy-start.4 = (f32[512,64]{0,1:T(8,128)S(1)}, f32[512,64]{0,1:T(8,128)}, u32[]{:S(2)}) copy-start(f32[512,64]{0,1:T(8,128)} %param.28) | copy-start | bytes 393220
  36.0 68.6 %copy-start.5 = (f32[512,64]{0,1:T(8,128)S(1)}, f32[512,64]{0,1:T(8,128)}, u32[]{:S(2)}) copy-start(f32[512,64]{0,1:T(8,128)} %param.29) | copy-start | bytes 393220
  36.0 68.6 %copy-start.6 = (f32[32,8,32]{2,1,0:T(8,128)S(1)}, f32[32,8,32]{2,1,0:T(8,128)}, u32[]{:S(2)}) copy-start(f32[32,8,32]{2,1,0:T(8,128)} %refs_12_.1) | copy-start | bytes 98308
  36.0 68.6 %copy-start.7 = (f32[32,8,32]{2,1,0:T(8,128)S(1)}, f32[32,8,32]{2,1,0:T(8,128)}, u32[]{:S(2)}) copy-start(f32[32,8,32]{2,1,0:T(8,128)} %refs_13_.1) | copy-start | bytes 98308
  36.0 68.6 %copy-start.8 = (f32[3,512]{1,0:T(4,128)S(1)}, f32[3,512]{1,0:T(4,128)}, u32[]{:S(2)}) copy-start(f32[3,512]{1,0:T(4,128)} %refs_8_.1) | copy-start | bytes 18436
  36.1 68.6 %copy-start.9 = (f32[3,512]{1,0:T(4,128)S(1)}, f32[3,512]{1,0:T(4,128)}, u32[]{:S(2)}) copy-start(f32[3,512]{1,0:T(4,128)} %refs_9_.1) | copy-start | bytes 18436
  47.7 2.2 %collective-permute-start.7 = (f32[16,80,128]{2,1,0:T(8,128)S(1)}, f32[16,80,128]{2,1,0:T(8,128)S(1)}, u32[]{:S(2)}, u32[]{:S(2)}) collective-permute-start(f32[16,80,128]{2,1,0:T(8,128)S(1)} %get-tuple-element.64), channel_id=1, source_target_pairs={{0,1},{1,0},{2,3},{3,2},{4,5},{5,4},{6,7},{7,6},{8,9},{9,8},{10,11... | collective-permute-start | bytes 1966088 | tf_op jit(solution)/shard_map/ppermute | solution.py:82
  50.0 9.9 %collective-permute-start.10 = (f32[4,80,128]{2,1,0:T(8,128)S(1)}, f32[4,80,128]{2,1,0:T(8,128)S(1)}, u32[]{:S(2)}, u32[]{:S(2)}) collective-permute-start(f32[4,80,128]{2,1,0:T(8,128)S(1)} %get-tuple-element.79), channel_id=1, source_target_pairs={{0,48},{16,32},{32,16},{48,0},{1,49},{17,33},{33,17},{49,1},{2,50}... | collective-permute-start | bytes 491528 | tf_op jit(solution)/shard_map/ppermute | solution.py:82
  52.3 7.6 %collective-permute-start.9 = (f32[4,80,128]{2,1,0:T(8,128)S(1)}, f32[4,80,128]{2,1,0:T(8,128)S(1)}, u32[]{:S(2)}, u32[]{:S(2)}) collective-permute-start(f32[4,80,128]{2,1,0:T(8,128)S(1)} %get-tuple-element.80), channel_id=1, source_target_pairs={{0,32},{16,48},{32,0},{48,16},{1,33},{17,49},{33,1},{49,17},{2,34}... | collective-permute-start | bytes 491528 | tf_op jit(solution)/shard_map/ppermute | solution.py:82
  52.8 8.0 %collective-permute-start.8 = (f32[4,80,128]{2,1,0:T(8,128)S(1)}, f32[4,80,128]{2,1,0:T(8,128)S(1)}, u32[]{:S(2)}, u32[]{:S(2)}) collective-permute-start(f32[4,80,128]{2,1,0:T(8,128)S(1)} %get-tuple-element.81), channel_id=1, source_target_pairs={{0,16},{16,0},{32,48},{48,32},{1,17},{17,1},{33,49},{49,33},{2,18}... | collective-permute-start | bytes 491528 | tf_op jit(solution)/shard_map/ppermute | solution.py:82
  53.4 7.5 %collective-permute-start.11 = (f32[32,128]{1,0:T(8,128)S(1)}, f32[32,128]{1,0:T(8,128)S(1)}, u32[]{:S(2)}, u32[]{:S(2)}) collective-permute-start(f32[32,128]{1,0:T(8,128)S(1)} %get-tuple-element.65), channel_id=1, source_target_pairs={{0,1},{1,2},{2,3},{3,4},{4,5},{5,6},{6,7},{7,8},{8,9},{9,10},{10,1... | collective-permute-start | bytes 49160 | tf_op jit(solution)/shard_map/ppermute | solution.py:58
  60.9 10.8 %collective-permute-start.14 = (f32[80,128]{1,0:T(8,128)S(1)}, f32[80,128]{1,0:T(8,128)S(1)}, u32[]{:S(2)}, u32[]{:S(2)}) collective-permute-start(f32[80,128]{1,0:T(8,128)S(1)} %get-tuple-element.82), channel_id=1, source_target_pairs={{0,12},{4,8},{8,4},{12,0},{1,13},{5,9},{9,5},{13,1},{2,14},{6,10},... | collective-permute-start | bytes 122888 | tf_op jit(solution)/shard_map/ppermute | solution.py:82
  62.5 9.2 %collective-permute-start.13 = (f32[80,128]{1,0:T(8,128)S(1)}, f32[80,128]{1,0:T(8,128)S(1)}, u32[]{:S(2)}, u32[]{:S(2)}) collective-permute-start(f32[80,128]{1,0:T(8,128)S(1)} %get-tuple-element.83), channel_id=1, source_target_pairs={{0,8},{4,12},{8,0},{12,4},{1,9},{5,13},{9,1},{13,5},{2,10},{6,14},... | collective-permute-start | bytes 122888 | tf_op jit(solution)/shard_map/ppermute | solution.py:82
  62.5 9.2 %collective-permute-start.12 = (f32[80,128]{1,0:T(8,128)S(1)}, f32[80,128]{1,0:T(8,128)S(1)}, u32[]{:S(2)}, u32[]{:S(2)}) collective-permute-start(f32[80,128]{1,0:T(8,128)S(1)} %get-tuple-element.84), channel_id=1, source_target_pairs={{0,4},{4,0},{8,12},{12,8},{1,5},{5,1},{9,13},{13,9},{2,6},{6,2},{1... | collective-permute-start | bytes 122888 | tf_op jit(solution)/shard_map/ppermute | solution.py:82
  64.3 6.7 %collective-permute-start.15 = (f32[32,256]{1,0:T(8,128)S(1)}, f32[32,256]{1,0:T(8,128)S(1)}, u32[]{:S(2)}, u32[]{:S(2)}) collective-permute-start(f32[32,256]{1,0:T(8,128)S(1)} %turn.1), channel_id=1, source_target_pairs={{0,16},{16,32},{32,48},{48,64},{64,80},{80,96},{96,112},{112,128},... | collective-permute-start | bytes 98312 | tf_op jit(solution)/shard_map/ppermute | solution.py:56
  71.7 3.9 %collective-permute-start.17 = (f32[88,128]{1,0:T(8,128)S(1)}, f32[88,128]{1,0:T(8,128)S(1)}, u32[]{:S(2)}, u32[]{:S(2)}) collective-permute-start(f32[88,128]{1,0:T(8,128)S(1)} %pad_maximum_fusion), channel_id=1, source_target_pairs={{0,128},{64,192},{128,0},{192,64},{1,129},{65,193},{129,1},{193,65... | collective-permute-start | bytes 135176 | tf_op jit(solution)/shard_map/ppermute | solution.py:82
  71.8 4.9 %collective-permute-start.18 = (f32[88,128]{1,0:T(8,128)S(1)}, f32[88,128]{1,0:T(8,128)S(1)}, u32[]{:S(2)}, u32[]{:S(2)}) collective-permute-start(f32[88,128]{1,0:T(8,128)S(1)} %pad_maximum_fusion), channel_id=1, source_target_pairs={{0,192},{64,128},{128,64},{192,0},{1,193},{65,129},{129,65},{193,1... | collective-permute-start | bytes 135176 | tf_op jit(solution)/shard_map/ppermute | solution.py:82
  73.6 3.4 %collective-permute-start.16 = (f32[88,128]{1,0:T(8,128)S(1)}, f32[88,128]{1,0:T(8,128)S(1)}, u32[]{:S(2)}, u32[]{:S(2)}) collective-permute-start(f32[88,128]{1,0:T(8,128)S(1)} %pad_maximum_fusion), channel_id=1, source_target_pairs={{0,64},{64,0},{128,192},{192,128},{1,65},{65,1},{129,193},{193,129... | collective-permute-start | bytes 135176 | tf_op jit(solution)/shard_map/ppermute | solution.py:82
  77.0 6.9 %collective-permute-start.19 = (f32[88,128]{1,0:T(8,128)S(1)}, f32[88,128]{1,0:T(8,128)S(1)}, u32[]{:S(2)}, u32[]{:S(2)}) collective-permute-start(f32[88,128]{1,0:T(8,128)S(1)} %add_add_fusion.one_ref), channel_id=1, source_target_pairs={{0,130},{2,128},{64,194},{66,192},{128,2},{130,0},{192,66},{194,64... | collective-permute-start | bytes 135176 | tf_op jit(solution)/shard_map/ppermute | solution.py:794
  96.5 8.1 %collective-permute-start.20 = (f32[16,88,128]{2,1,0:T(8,128)S(1)}, f32[16,88,128]{2,1,0:T(8,128)S(1)}, u32[]{:S(2)}, u32[]{:S(2)}) collective-permute-start(f32[16,88,128]{2,1,0:T(8,128)S(1)} %all_to_all.5.refs_0_), channel_id=1, source_target_pairs={{0,1},{1,0},{2,3},{3,2},{4,5},{5,4},{6,7},{7,6},{8,9},{9,8},{10,11... | collective-permute-start | bytes 2162696 | tf_op jit(solution)/shard_map/ppermute | solution.py:82
